TPU v7x, 128 devices: a whole 4x4x4 slice. The times are simulated.
128 devices in a mesh: fsdp: 8 (over z, y_hi), cb: 16 (over y_lo, x, core).
Axes of the slice: x: 4, y: 4 (y_hi: 2, y_lo: 2; y = y_hi * 2 + y_lo), z: 4, core: 2. Of those that a mesh axis runs over, the one named last changes fastest.
Arguments:
- frames_in: bfloat16 [8, 256, 6144], P('fsdp', 'cb'), may hold values from -6 to 6
- valid_len: int32 [8], P('fsdp'), may hold values from 128 to 256
- tokens: int32 [8, 16, 256], P('fsdp', 'cb'), may hold values from 0 to 2047
- t_gain: float32 [6144], replicated, may hold values from 0.25 to 1.75
- w_qkv: bfloat16 [6144, 12288], P('fsdp', 'cb'), as said below
- w_out: bfloat16 [4096, 6144], P('cb', 'fsdp'), may hold values from -0.09375 to 0.09375
- h_gain: float32 [6144], replicated, may hold values from 0.25 to 1.75
- d_in: bfloat16 [16, 6144, 1024], P('cb'), may hold values from -0.078125 to 0.078125
- d_embed: bfloat16 [16, 2048, 1024], P('cb'), may hold values from -6 to 6
- d_gain: float32 [16, 1024], P('cb'), may hold values from 0.25 to 1.75
- d_qkv: bfloat16 [16, 1024, 3072], P('cb'), as said below
Outputs:
- depth_mix: bfloat16 [8, 16, 256, 1024], P('fsdp', 'cb')
Inputs may be any that keep to these rules, and one draw needn't show every extreme that they name: `w_qkv`: every entry of the temporal projections has magnitude at most 31 / sqrt(6144). `d_qkv`: every entry of the depth projections has magnitude at most 31 / sqrt(1024).
All inputs are finite; a program needn't handle non-finite values.
Results may differ from a plain program's by a relative error of at most 0.012.
Values may be sent and summed in bfloat16 or wider, within the bound.
No kernel may reach another device: no remote copies, remote signals or barrier semaphores. Data moves between devices by JAX's collectives and lax.ppermute only.
A program may use at most 128 MiB of HBM per device.

v0:
```python
import math

import jax
import jax.numpy as jnp
from jax import lax
from jax.experimental import pallas as pl
from jax.experimental.pallas import tpu as pltpu
from jax.sharding import PartitionSpec as P


HEAD = 128
DHEAD = 64
EPS = 1e-05
NEG = -1e30
BF = jnp.bfloat16
F32 = jnp.float32


VM = pl.BlockSpec(memory_space=pltpu.VMEM)
SM = pl.BlockSpec(memory_space=pltpu.SMEM)


def swap(value, axis, size, flip):
    return lax.ppermute(value, axis, [(i, i ^ flip) for i in range(size)])


def call(kernel, outs, scratch=(), smem=0, n_in=0, limit=8, last=False):
    kind = jax.ShapeDtypeStruct if last else pltpu.VMEM
    run = pl.pallas_call(
        kernel,
        out_shape=[kind(s, d) for s, d in outs],
        in_specs=[SM] * smem + [VM] * (n_in - smem),
        out_specs=[VM] * len(outs),
        scratch_shapes=list(scratch),
        compiler_params=pltpu.CompilerParams(vmem_limit_bytes=limit << 20),
    )

    def go(*args):
        near = [pltpu.with_memory_space_constraint(a, pltpu.VMEM) for a in args[smem:]]
        return run(*args[:smem], *near)

    return go


def norm_kernel(ids, x_ref, g_ref, o_ref):
    x = x_ref[...].astype(F32)
    scale = lax.rsqrt(jnp.mean(x * x, axis=-1, keepdims=True) + EPS)
    y = (x * scale * g_ref[...]).astype(BF)
    width = o_ref.shape[2]
    for b in range(o_ref.shape[0]):
        o_ref[ids[0] ^ b] = y[:, b * width:(b + 1) * width]


def qkv_kernel(g_ref, h_ref, w0_ref, w1_ref, *outs):
    width = w0_ref.shape[0]
    for d, o_ref in enumerate(outs):
        for kk, src in enumerate((g_ref, h_ref)):
            a = src[:, 2 * d].reshape(-1, width)
            b = src[:, 2 * d + 1].reshape(-1, width)
            acc = jnp.dot(a, w0_ref[...], preferred_element_type=F32)
            acc = acc + jnp.dot(b, w1_ref[...], preferred_element_type=F32)
            rows = acc.shape[0]
            o_ref[kk * rows:(kk + 1) * rows, :] = acc.astype(o_ref.dtype)


def place(row, section, step):
    group = row // step
    half = group // 8
    return (section ^ (2 * (group - 8 * half) + half)) * step + (row - group * step)


def attn_kernel(ids, own, r1, r2, r3, *rest):
    wo = rest[:8]
    outs = rest[8:10]
    packed = rest[10]
    mixed = rest[11]
    length = own.shape[0]
    packed[...] = (
        own[...] + r1[...].astype(F32) + r2[...].astype(F32) + r3[...].astype(F32)
    ).astype(BF)
    section = ids[1]
    valid = ids[2]
    rows = place(lax.broadcasted_iota(jnp.int32, (length, 1), 0), section, 16)
    cols = place(lax.broadcasted_iota(jnp.int32, (1, length), 1), section, 16)
    allowed = (cols <= rows) & (cols < valid)
    for h in range(own.shape[1] // (3 * HEAD)):
        base = h * 3 * HEAD
        q = packed[:, base:base + HEAD]
        k = packed[:, base + HEAD:base + 2 * HEAD]
        v = packed[:, base + 2 * HEAD:base + 3 * HEAD]
        s = lax.dot_general(q, k, (((1,), (1,)), ((), ())), preferred_element_type=F32)
        s = jnp.where(allowed, s * (1.0 / math.sqrt(HEAD)), NEG)
        top = jnp.max(s, axis=-1, keepdims=True)
        e = jnp.where(allowed, jnp.exp(s - top), 0.0)
        p = (e / jnp.sum(e, axis=-1, keepdims=True)).astype(BF)
        mixed[:, h * HEAD:(h + 1) * HEAD] = jnp.dot(
            p, v, preferred_element_type=F32
        ).astype(BF)
    half = length // 2
    width = wo[0].shape[1]
    for e in range(8):
        acc = jnp.dot(mixed[...], wo[e][...], preferred_element_type=F32).astype(BF)
        outs[0][:, e * width:(e + 1) * width] = acc[:half]
        outs[1][:, e * width:(e + 1) * width] = acc[half:]


def pair_kernel(a_ref, b_ref, *outs):
    for j, o_ref in enumerate(outs):
        rows = o_ref.shape[0]
        part = a_ref[j * rows:(j + 1) * rows, :].astype(F32) + b_ref[
            j * rows:(j + 1) * rows, :
        ].astype(F32)
        o_ref[...] = part.astype(o_ref.dtype)


def hidden_kernel(ids, frames, gain, *rest):
    pieces = rest[:8]
    o_ref = rest[8]
    acc = rest[9]
    width = frames.shape[1] // 8
    for e in range(8):
        cut = slice(e * width, (e + 1) * width)
        part = pieces[0][:, cut].astype(F32)
        for piece in pieces[1:]:
            part = part + piece[:, cut].astype(F32)
        acc[ids[0] ^ e] = part
    total = jnp.zeros((frames.shape[0], 1), F32)
    for b in range(8):
        cut = slice(b * width, (b + 1) * width)
        hid = frames[:, cut].astype(F32) + acc[b]
        acc[b] = hid
        total = total + jnp.sum(hid * hid, axis=-1, keepdims=True)
    scale = lax.rsqrt(total / frames.shape[1] + EPS)
    for b in range(8):
        cut = slice(b * width, (b + 1) * width)
        o_ref[:, cut] = (acc[b] * scale * gain[:, cut]).astype(BF)


def lift_kernel(g_ref, h_ref, din, emb, gain, wqkv, *outs):
    width = g_ref.shape[2]
    parts = []
    for src in (g_ref, h_ref):
        parts.append(src[...].reshape(-1, width))
    x = jnp.concatenate(parts, axis=0)
    lifted = jnp.dot(x, din[...], preferred_element_type=F32) + emb[...].astype(F32)
    scale = lax.rsqrt(jnp.mean(lifted * lifted, axis=-1, keepdims=True) + EPS)
    dn = (lifted * scale * gain[...]).astype(BF)
    step = 1024
    for s in range(wqkv.shape[1] // step):
        cut = slice(s * step, (s + 1) * step)
        y = jnp.dot(dn, wqkv[:, cut], preferred_element_type=F32).astype(BF)
        for e in range(8):
            outs[e][0, :, cut] = y[e * 16:(e + 1) * 16]
            outs[e][1, :, cut] = y[128 + e * 16:128 + (e + 1) * 16]


def fetch_kernel(*refs):
    sems = refs[-1]
    half = (len(refs) - 1) // 2
    copies = [
        pltpu.make_async_copy(refs[i], refs[half + i], sems.at[i]) for i in range(half)
    ]
    for copy in copies:
        copy.start()
    for copy in copies:
        copy.wait()


def fetch(*arrays):
    return pl.pallas_call(
        fetch_kernel,
        out_shape=[pltpu.VMEM(a.shape, a.dtype) for a in arrays],
        in_specs=[pl.BlockSpec(memory_space=pltpu.HBM)] * len(arrays),
        out_specs=[VM] * len(arrays),
        scratch_shapes=[pltpu.SemaphoreType.DMA((len(arrays),))],
        compiler_params=pltpu.CompilerParams(vmem_limit_bytes=1 << 20),
    )(*[pltpu.with_memory_space_constraint(a, pltpu.HBM) for a in arrays])


def depth_kernel(ids, *rest):
    pieces = rest[:8]
    other = rest[8]
    outs = rest[9:17]
    z = rest[17]
    for e in range(8):
        z[e * 16:(e + 1) * 16, :] = pieces[e][0]
        z[128 + e * 16:128 + (e + 1) * 16, :] = other[e]
    section = ids[1]
    rows = lax.broadcasted_iota(jnp.int32, (256, 1), 0)
    cols = lax.broadcasted_iota(jnp.int32, (1, 256), 1)
    rpos = place(rows, section, 16) // 16
    cpos = place(cols, section, 16) // 16
    keep = (cpos <= rpos) & (rows % 16 == cols % 16)
    bias = jnp.where(keep, 0.0, NEG)
    lane = lax.broadcasted_iota(jnp.int32, (256, 2 * DHEAD), 1)
    low = lane < DHEAD
    inner = z.shape[1] // 3
    for pair in range(inner // (2 * DHEAD)):
        base = pair * 2 * DHEAD
        q = z[:, base:base + 2 * DHEAD]
        k = z[:, inner + base:inner + base + 2 * DHEAD]
        v = z[:, 2 * inner + base:2 * inner + base + 2 * DHEAD]
        got = []
        for side in range(2):
            mask = low if side == 0 else jnp.logical_not(low)
            qs = jnp.where(mask, q, jnp.zeros_like(q))
            s = lax.dot_general(
                qs, k, (((1,), (1,)), ((), ())), preferred_element_type=F32
            )
            s = s * (1.0 / math.sqrt(DHEAD)) + bias
            top = jnp.max(s, axis=-1, keepdims=True)
            e = jnp.exp(s - top)
            total = jnp.sum(e, axis=-1, keepdims=True)
            o = jnp.dot(e.astype(BF), v, preferred_element_type=F32)
            got.append(o / total)
        res = jnp.where(low, got[0], got[1]).astype(BF)
        for e in range(8):
            outs[e][0, :, base:base + 2 * DHEAD] = res[e * 16:(e + 1) * 16]
            outs[e][1, :, base:base + 2 * DHEAD] = res[128 + e * 16:128 + (e + 1) * 16]


def final_kernel(ids, *rest):
    pieces = rest[:8]
    other = rest[8]
    o_ref = rest[9]
    for e in range(8):
        o_ref[ids[1] ^ (2 * e)] = pieces[e][0]
        o_ref[ids[1] ^ (2 * e + 1)] = other[e]


def gather(value):
    def cb(v, flip):
        return swap(v, "cb", 16, flip)

    y = cb(value, 8)
    x1 = cb(value, 2)
    x3 = cb(value, 6)
    x2 = cb(value, 4)
    y1 = cb(y, 2)
    y3 = cb(y, 6)
    y2 = cb(x2, 8)
    return [value, x1, x2, x3, y, y1, y2, y3]


def work(frames_in, valid_len, tokens, t_gain, w_qkv, w_out, h_gain, d_in, d_embed, d_gain, d_qkv):
    model = frames_in.shape[2]
    mine = frames_in[0]
    f = lax.axis_index("fsdp").astype(jnp.int32)
    c = lax.axis_index("cb").astype(jnp.int32)
    ids = jnp.stack([f, c, valid_len[0]])
    fs = lambda v, flip: swap(v, "fsdp", 8, flip)
    cb = lambda v, flip: swap(v, "cb", 16, flip)
    block = model // 8

    rel = call(norm_kernel, [((8, 16, block), BF)], smem=1, n_in=3)(
        ids, mine, t_gain[None]
    )[0]
    w_other = fs(w_qkv, 1)
    wo_other = fs(w_out, 1)
    local = [rel[0:2]] + [fs(rel[2 * d:2 * d + 2], 2 * d) for d in (1, 2, 3)]
    local = jnp.concatenate(local, axis=0)
    even = jnp.stack(gather(local))
    odd = cb(even, 1)
    cols = w_qkv.shape[1]
    parts = call(
        qkv_kernel, [((256, cols), F32)] + [((256, cols), BF)] * 3, n_in=4
    )(even, odd, w_qkv, w_other)
    wo_pair = jnp.stack([w_out, wo_other])
    wo_far = [fs(wo_pair, 2 * d) for d in (1, 2, 3)]
    wo = [w_out, wo_other]
    for pair in wo_far:
        wo += [pair[0], pair[1]]
    sums = [fs(parts[d], 2 * d) for d in (1, 2, 3)]
    keep, give = call(
        attn_kernel,
        [((128, model), BF)] * 2,
        scratch=[pltpu.VMEM((256, cols), BF), pltpu.VMEM((256, w_out.shape[0]), BF)],
        smem=1,
        n_in=13,
    )(ids, parts[0], *sums, *wo)
    taken = cb(give, 1)
    blocks = call(pair_kernel, [((16, model), F32)] + [((16, model), BF)] * 7, n_in=2)(
        keep, taken
    )
    pieces = [blocks[0]] + [cb(blocks[e], 2 * e) for e in range(1, 8)]
    hn = call(
        hidden_kernel,
        [((16, model), BF)],
        scratch=[pltpu.VMEM((8, 16, block), F32)],
        smem=1,
        n_in=11,
    )(ids, mine, h_gain[None], *pieces)[0]
    even = jnp.stack(gather(hn))
    odd = cb(even, 1)

    order = jnp.concatenate([2 * jnp.arange(8), 2 * jnp.arange(8) + 1]).astype(jnp.int32)
    ids_rel = tokens[0, 0].reshape(16, 16).at[c ^ order].get(mode="promise_in_bounds")
    emb = d_embed[0].at[ids_rel.reshape(256)].get(mode="promise_in_bounds")
    din, dqkv = fetch(d_in[0], d_qkv[0])
    inner = d_in.shape[2]
    sent = call(lift_kernel, [((2, 16, 3 * inner), BF)] * 8, n_in=6)(
        even, odd, din, emb, d_gain, dqkv
    )
    pieces = [sent[0]] + [cb(sent[e], 2 * e) for e in range(1, 8)]
    other = cb(jnp.stack([p[1] for p in pieces]), 1)
    outs = call(
        depth_kernel,
        [((2, 16, inner), BF)] * 8,
        scratch=[pltpu.VMEM((256, 3 * inner), BF)],
        smem=1,
        n_in=10,
    )(ids, *pieces, other)
    pieces = [outs[0]] + [cb(outs[e], 2 * e) for e in range(1, 8)]
    other = cb(jnp.stack([p[1] for p in pieces]), 1)
    out = call(final_kernel, [((16, 16, inner), BF)], smem=1, n_in=10, last=True)(
        ids, *pieces, other
    )[0]
    return out.reshape(1, 1, 256, inner)


def solution(mesh):
    placed = (
        P("fsdp", "cb", None),
        P("fsdp"),
        P("fsdp", "cb", None),
        P(),
        P("fsdp", "cb"),
        P("cb", "fsdp"),
        P(),
        P("cb", None, None),
        P("cb", None, None),
        P("cb", None),
        P("cb", None, None),
    )
    return jax.shard_map(
        work, mesh=mesh, in_specs=placed, out_specs=P("fsdp", "cb", None, None), check_vma=False
    )
```

profile of v0, /device:TPU:1, one launch (start us, length us, event | category | flops | bytes accessed | tf_op | source)
XLA Modules:
  0.0 224.6 jit_solution(12210798199098379044)
XLA Ops:
  3.2 4.7 %collective-permute-start.2 = (bf16[2,16,768]{2,1,0:T(8,128)(2,1)S(1)}, bf16[2,16,768]{2,1,0:T(8,128)(2,1)S(1)}, u32[]{:S(2)}, u32[]{:S(2)}) collective-permute-start(bf16[2,16,768]{2,1,0:T(8,128)(2,1)S(1)} %get-tuple-element.76), channel_id=1, source_target_pairs={{0,96},{16,112},{32,64},{48,80},{64,32},{80,48},{96,0},{112,16},{1... | collective-permute-start | bytes 147464 | tf_op jit(solution)/shard_map/ppermute | solution.py:24
  9.3 3.0 %collective-permute-done.1 = bf16[2,16,768]{2,1,0:T(8,128)(2,1)S(1)} collective-permute-done((bf16[2,16,768]{2,1,0:T(8,128)(2,1)S(1)}, bf16[2,16,768]{2,1,0:T(8,128)(2,1)S(1)}, u32[]{:S(2)}, u32[]{:S(2)}) %collective-permute-start.1) | collective-permute-done | bytes 49184 | tf_op jit(solution)/shard_map/ppermute | solution.py:24
  13.7 2.7 %collective-permute-start.4 = (bf16[8,16,768]{2,1,0:T(8,128)(2,1)S(1)}, bf16[8,16,768]{2,1,0:T(8,128)(2,1)S(1)}, u32[]{:S(2)}, u32[]{:S(2)}) collective-permute-start(bf16[8,16,768]{2,1,0:T(8,128)(2,1)S(1)} %pad_maximum_fusion.1), channel_id=1, source_target_pairs={{0,4},{1,5},{2,6},{3,7},{4,0},{5,1},{6,2},{7,3},{8,12},{9,13},{10,... | collective-permute-start | bytes 589832 | tf_op jit(solution)/shard_map/ppermute | solution.py:24
  20.7 2.9 %collective-permute-done.3 = bf16[8,16,768]{2,1,0:T(8,128)(2,1)S(1)} collective-permute-done((bf16[8,16,768]{2,1,0:T(8,128)(2,1)S(1)}, bf16[8,16,768]{2,1,0:T(8,128)(2,1)S(1)}, u32[]{:S(2)}, u32[]{:S(2)}) %collective-permute-start.3) | collective-permute-done | bytes 196640 | tf_op jit(solution)/shard_map/ppermute | solution.py:24
  25.3 2.5 %collective-permute-done.7 = bf16[8,16,768]{2,1,0:T(8,128)(2,1)S(1)} collective-permute-done((bf16[8,16,768]{2,1,0:T(8,128)(2,1)S(1)}, bf16[8,16,768]{2,1,0:T(8,128)(2,1)S(1)}, u32[]{:S(2)}, u32[]{:S(2)}) %collective-permute-start.7) | collective-permute-done | bytes 196640 | tf_op jit(solution)/shard_map/ppermute | solution.py:24
  31.7 2.6 %collective-permute-start.15 = (bf16[256,768]{1,0:T(8,128)(2,1)S(1)}, bf16[256,768]{1,0:T(8,128)(2,1)S(1)}, u32[]{:S(2)}, u32[]{:S(2)}) collective-permute-start(bf16[256,768]{1,0:T(8,128)(2,1)S(1)} %copy-done), channel_id=1, source_target_pairs={{0,16},{16,0},{32,48},{48,32},{64,80},{80,64},{96,112},{112,96},{1... | collective-permute-start | bytes 1179656 | tf_op jit(solution)/shard_map/ppermute | solution.py:24
  34.7 9.1 %collective-permute-done.15.rest_1_ = bf16[256,768]{1,0:T(8,128)(2,1)S(1)} collective-permute-done((bf16[256,768]{1,0:T(8,128)(2,1)S(1)}, bf16[256,768]{1,0:T(8,128)(2,1)S(1)}, u32[]{:S(2)}, u32[]{:S(2)}) %collective-permute-start.15) | collective-permute-done | bytes 393248 | tf_op jit(solution)/shard_map/ppermute | solution.py:24
  47.2 33.0 %collective-permute-done.18 = bf16[2,256,768]{2,1,0:T(8,128)(2,1)S(1)} collective-permute-done((bf16[2,256,768]{2,1,0:T(8,128)(2,1)S(1)}, bf16[2,256,768]{2,1,0:T(8,128)(2,1)S(1)}, u32[]{:S(2)}, u32[]{:S(2)}) %collective-permute-start.18) | collective-permute-done | bytes 786464 | tf_op jit(solution)/shard_map/ppermute | solution.py:24
  80.2 2.6 %shard_map.110 = (f32[256,768]{1,0:T(8,128)S(1)}, bf16[256,768]{1,0:T(8,128)(2,1)S(1)}, bf16[256,768]{1,0:T(8,128)(2,1)S(1)}, bf16[256,768]{1,0:T(8,128)(2,1)S(1)}) custom-call(bf16[8,8,16,768]{3,2,1,0:T(8,128)(2,1)S(1)} %bitcast_dynamic-update-slice_fusion.8.g_ref, bf16[8,8,16,768]{3,2,1,0:T(8,128)(2,1)S(1)} %collective-permute-done.10.h_ref, ...), custom_call_target="tpu_custom_call" | custom-call | tf_op jit(solution)/shard_map/pallas_call | solution.py:40
  86.9 4.9 %collective-permute-done.12.r1 = bf16[256,768]{1,0:T(8,128)(2,1)S(1)} collective-permute-done((bf16[256,768]{1,0:T(8,128)(2,1)S(1)}, bf16[256,768]{1,0:T(8,128)(2,1)S(1)}, u32[]{:S(2)}, u32[]{:S(2)}) %collective-permute-start.12) | collective-permute-done | bytes 393248 | tf_op jit(solution)/shard_map/ppermute | solution.py:24
  91.8 8.0 %collective-permute-done.13.r2 = bf16[256,768]{1,0:T(8,128)(2,1)S(1)} collective-permute-done((bf16[256,768]{1,0:T(8,128)(2,1)S(1)}, bf16[256,768]{1,0:T(8,128)(2,1)S(1)}, u32[]{:S(2)}, u32[]{:S(2)}) %collective-permute-start.13) | collective-permute-done | bytes 393248 | tf_op jit(solution)/shard_map/ppermute | solution.py:24
  99.8 2.5 %shard_map.111 = (bf16[128,6144]{1,0:T(8,128)(2,1)S(1)}, bf16[128,6144]{1,0:T(8,128)(2,1)S(1)}) custom-call(s32[3]{0:T(128)S(1)} %pad_add_fusion.ids, f32[256,768]{1,0:T(8,128)S(1)} %get-tuple-element.37.own, bf16[256,768]{1,0:T(8,128)(2,1)S(1)} %collective-permute-done.12.r1, bf16[256,768]{1,0:T(8,128)(2,1)S(1)} %collective-permute-done.13.r2, ...), custom_call_target="tpu_custom_call" | custom-call | tf_op jit(solution)/shard_map/pallas_call | solution.py:40
  102.3 5.9 %collective-permute-start.19 = (bf16[128,6144]{1,0:T(8,128)(2,1)S(1)}, bf16[128,6144]{1,0:T(8,128)(2,1)S(1)}, u32[]{:S(2)}, u32[]{:S(2)}) collective-permute-start(bf16[128,6144]{1,0:T(8,128)(2,1)S(1)} %get-tuple-element.42), channel_id=1, source_target_pairs={{0,1},{1,0},{2,3},{3,2},{4,5},{5,4},{6,7},{7,6},{8,9},{9,8},{10,11... | collective-permute-start | bytes 4718600 | tf_op jit(solution)/shard_map/ppermute | solution.py:24
  108.3 3.0 %collective-permute-done.19.b_ref = bf16[128,6144]{1,0:T(8,128)(2,1)S(1)} collective-permute-done((bf16[128,6144]{1,0:T(8,128)(2,1)S(1)}, bf16[128,6144]{1,0:T(8,128)(2,1)S(1)}, u32[]{:S(2)}, u32[]{:S(2)}) %collective-permute-start.19) | collective-permute-done | bytes 1572896 | tf_op jit(solution)/shard_map/ppermute | solution.py:24
  112.5 2.3 %collective-permute-start.21 = (bf16[16,6144]{1,0:T(8,128)(2,1)S(1)}, bf16[16,6144]{1,0:T(8,128)(2,1)S(1)}, u32[]{:S(2)}, u32[]{:S(2)}) collective-permute-start(bf16[16,6144]{1,0:T(8,128)(2,1)S(1)} %get-tuple-element.45), channel_id=1, source_target_pairs={{0,4},{1,5},{2,6},{3,7},{4,0},{5,1},{6,2},{7,3},{8,12},{9,13},{10,... | collective-permute-start | bytes 589832 | tf_op jit(solution)/shard_map/ppermute | solution.py:24
  119.9 3.8 %collective-permute-done.21.rest_2_ = bf16[16,6144]{1,0:T(8,128)(2,1)S(1)} collective-permute-done((bf16[16,6144]{1,0:T(8,128)(2,1)S(1)}, bf16[16,6144]{1,0:T(8,128)(2,1)S(1)}, u32[]{:S(2)}, u32[]{:S(2)}) %collective-permute-start.21) | collective-permute-done | bytes 196640 | tf_op jit(solution)/shard_map/ppermute | solution.py:24
  126.2 5.9 %collective-permute-done.25.rest_6_ = bf16[16,6144]{1,0:T(8,128)(2,1)S(1)} collective-permute-done((bf16[16,6144]{1,0:T(8,128)(2,1)S(1)}, bf16[16,6144]{1,0:T(8,128)(2,1)S(1)}, u32[]{:S(2)}, u32[]{:S(2)}) %collective-permute-start.25) | collective-permute-done | bytes 196640 | tf_op jit(solution)/shard_map/ppermute | solution.py:24
  132.1 4.0 %collective-permute-done.26.rest_7_ = bf16[16,6144]{1,0:T(8,128)(2,1)S(1)} collective-permute-done((bf16[16,6144]{1,0:T(8,128)(2,1)S(1)}, bf16[16,6144]{1,0:T(8,128)(2,1)S(1)}, u32[]{:S(2)}, u32[]{:S(2)}) %collective-permute-start.26) | collective-permute-done | bytes 196640 | tf_op jit(solution)/shard_map/ppermute | solution.py:24
  147.6 4.1 %collective-permute-done.31 = bf16[16,6144]{1,0:T(8,128)(2,1)S(1)} collective-permute-done((bf16[16,6144]{1,0:T(8,128)(2,1)S(1)}, bf16[16,6144]{1,0:T(8,128)(2,1)S(1)}, u32[]{:S(2)}, u32[]{:S(2)}) %collective-permute-start.31) | collective-permute-done | bytes 196640 | tf_op jit(solution)/shard_map/ppermute | solution.py:24
  152.2 3.5 %collective-permute-start.34 = (bf16[8,16,6144]{2,1,0:T(8,128)(2,1)S(1)}, bf16[8,16,6144]{2,1,0:T(8,128)(2,1)}, u32[]{:S(2)}, u32[]{:S(2)}) collective-permute-start(bf16[8,16,6144]{2,1,0:T(8,128)(2,1)S(1)} %bitcast_dynamic-update-slice_fusion.g_ref), channel_id=1, source_target_pairs={{0,1},{1,0},{2,3},{3,2},{4,5},{5,4},{6,7},{7,6},{8,9},{9,8},{10,11... | collective-permute-start | bytes 4718600 | tf_op jit(solution)/shard_map/ppermute | solution.py:24
  157.9 4.3 %gather_fusion.1 = bf16[256,1024]{1,0:T(8,128)(2,1)S(1)} fusion(bf16[2048,1024]{1,0:T(8,128)(2,1)} %bitcast.70, s32[1024]{0:T(1024)S(1)} %pad_clamp_fusion), kind=kCustom, calls=%fused_computation.1 | custom fusion | bytes 1049600 | tf_op jit(solution)/shard_map/gather | solution.py:298
  162.2 6.4 %shard_map.114 = (bf16[6144,1024]{1,0:T(8,128)(2,1)S(1)}, bf16[1024,3072]{1,0:T(8,128)(2,1)S(1)}) custom-call(bf16[6144,1024]{1,0:T(8,128)(2,1)} %bitcast.68, bf16[1024,3072]{1,0:T(8,128)(2,1)} %bitcast.69), custom_call_target="tpu_custom_call" | custom-call | tf_op jit(solution)/shard_map/pallas_call | solution.py:170
  168.6 6.8 %shard_map.115 = (bf16[2,16,3072]{2,1,0:T(8,128)(2,1)S(1)}, bf16[2,16,3072]{2,1,0:T(8,128)(2,1)S(1)}, bf16[2,16,3072]{2,1,0:T(8,128)(2,1)S(1)}, bf16[2,16,3072]{...) custom-call(bf16[8,16,6144]{2,1,0:T(8,128)(2,1)S(1)} %bitcast_dynami, ...), custom_call_target="tpu_custom_call" | custom-call | tf_op jit(solution)/shard_map/pallas_call | solution.py:40
  175.5 2.5 %collective-permute-start.36 = (bf16[2,16,3072]{2,1,0:T(8,128)(2,1)S(1)}, bf16[2,16,3072]{2,1,0:T(8,128)(2,1)S(1)}, u32[]{:S(2)}, u32[]{:S(2)}) collective-permute-start(bf16[2,16,3072]{2,1,0:T(8,128)(2,1)S(1)} %get-tuple-element.55), channel_id=1, source_target_pairs={{0,4},{1,5},{2,6},{3,7},{4,0},{5,1},{6,2},{7,3},{8,12},{9,13},{10,... | collective-permute-start | bytes 589832 | tf_op jit(solution)/shard_map/ppermute | solution.py:24
  183.7 3.5 %collective-permute-done.36.rest_2_ = bf16[2,16,3072]{2,1,0:T(8,128)(2,1)S(1)} collective-permute-done((bf16[2,16,3072]{2,1,0:T(8,128)(2,1)S(1)}, bf16[2,16,3072]{2,1,0:T(8,128)(2,1)S(1)}, u32[]{:S(2)}, u32[]{:S(2)}) %collective-permute-start.36) | collective-permute-done | bytes 196640 | tf_op jit(solution)/shard_map/ppermute | solution.py:24
  190.6 5.5 %collective-permute-done.40.rest_6_ = bf16[2,16,3072]{2,1,0:T(8,128)(2,1)S(1)} collective-permute-done((bf16[2,16,3072]{2,1,0:T(8,128)(2,1)S(1)}, bf16[2,16,3072]{2,1,0:T(8,128)(2,1)S(1)}, u32[]{:S(2)}, u32[]{:S(2)}) %collective-permute-start.40) | collective-permute-done | bytes 196640 | tf_op jit(solution)/shard_map/ppermute | solution.py:24
  196.1 3.7 %collective-permute-done.41.rest_7_ = bf16[2,16,3072]{2,1,0:T(8,128)(2,1)S(1)} collective-permute-done((bf16[2,16,3072]{2,1,0:T(8,128)(2,1)S(1)}, bf16[2,16,3072]{2,1,0:T(8,128)(2,1)S(1)}, u32[]{:S(2)}, u32[]{:S(2)}) %collective-permute-start.41) | collective-permute-done | bytes 196640 | tf_op jit(solution)/shard_map/ppermute | solution.py:24
  203.0 2.7 %shard_map.116 = (bf16[2,16,1024]{2,1,0:T(8,128)(2,1)S(1)}, bf16[2,16,1024]{2,1,0:T(8,128)(2,1)S(1)}, bf16[2,16,1024]{2,1,0:T(8,128)(2,1)S(1)}, bf16[2,16,1024]{...) custom-call(s32[3]{0:T(128)S(1)} %pad_add_fusion.ids, ...), custom_call_target="tpu_custom_call" | custom-call | tf_op jit(solution)/shard_map/pallas_call | solution.py:40
  205.7 2.4 %collective-permute-start.44 = (bf16[2,16,1024]{2,1,0:T(8,128)(2,1)S(1)}, bf16[2,16,1024]{2,1,0:T(8,128)(2,1)S(1)}, u32[]{:S(2)}, u32[]{:S(2)}) collective-permute-start(bf16[2,16,1024]{2,1,0:T(8,128)(2,1)S(1)} %get-tuple-element.63), channel_id=1, source_target_pairs={{0,4},{1,5},{2,6},{3,7},{4,0},{5,1},{6,2},{7,3},{8,12},{9,13},{10,... | collective-permute-start | bytes 196616 | tf_op jit(solution)/shard_map/ppermute | solution.py:24
  210.3 3.3 %collective-permute-start.48 = (bf16[2,16,1024]{2,1,0:T(8,128)(2,1)S(1)}, bf16[2,16,1024]{2,1,0:T(8,128)(2,1)S(1)}, u32[]{:S(2)}, u32[]{:S(2)}) collective-permute-start(bf16[2,16,1024]{2,1,0:T(8,128)(2,1)S(1)} %get-tuple-element.67), channel_id=1, source_target_pairs={{0,12},{1,13},{2,14},{3,15},{4,8},{5,9},{6,10},{7,11},{8,4},{9,5},... | collective-permute-start | bytes 196616 | tf_op jit(solution)/shard_map/ppermute | solution.py:24
  216.4 2.5 %collective-permute-done.49.rest_7_ = bf16[2,16,1024]{2,1,0:T(8,128)(2,1)S(1)} collective-permute-done((bf16[2,16,1024]{2,1,0:T(8,128)(2,1)S(1)}, bf16[2,16,1024]{2,1,0:T(8,128)(2,1)S(1)}, u32[]{:S(2)}, u32[]{:S(2)}) %collective-permute-start.49) | collective-permute-done | bytes 65568 | tf_op jit(solution)/shard_map/ppermute | solution.py:24
  218.9 3.2 %collective-permute-start.50 = (bf16[8,16,1024]{2,1,0:T(8,128)(2,1)S(1)}, bf16[8,16,1024]{2,1,0:T(8,128)(2,1)S(1)}, u32[]{:S(2)}, u32[]{:S(2)}) collective-permute-start(bf16[8,16,1024]{2,1,0:T(8,128)(2,1)S(1)} %constant_dynamic-update-slice_fusion), channel_id=1, source_target_pairs={{0,1},{1,0},{2,3},{3,2},{4,5},{5,4},{6,7},{7,6},{8,9},{9,8},{10,11... | collective-permute-start | bytes 786440 | tf_op jit(solution)/shard_map/ppermute | solution.py:24
  (145 shorter events, 65.8 us)
Async XLA Ops:
  16.7 8.5 %collective-permute-start.5 = (bf16[8,16,768]{2,1,0:T(8,128)(2,1)S(1)}, bf16[8,16,768]{2,1,0:T(8,128)(2,1)S(1)}, u32[]{:S(2)}, u32[]{:S(2)}) collective-permute-start(bf16[8,16,768]{2,1,0:T(8,128)(2,1)S(1)} %pad_maximum_fusion.1), channel_id=1, source_target_pairs={{0,6},{1,7},{2,4},{3,5},{4,2},{5,3},{6,0},{7,1},{8,14},{9,15},{10,... | collective-permute-start | bytes 589832 | tf_op jit(solution)/shard_map/ppermute | solution.py:24
  17.3 12.1 %collective-permute-start.9 = (bf16[8,16,768]{2,1,0:T(8,128)(2,1)S(1)}, bf16[8,16,768]{2,1,0:T(8,128)(2,1)S(1)}, u32[]{:S(2)}, u32[]{:S(2)}) collective-permute-start(bf16[8,16,768]{2,1,0:T(8,128)(2,1)S(1)} %collective-permute-done.6), channel_id=1, source_target_pairs={{0,6},{1,7},{2,4},{3,5},{4,2},{5,3},{6,0},{7,1},{8,14},{9,15},{10,... | collective-permute-start | bytes 589832 | tf_op jit(solution)/shard_map/ppermute | solution.py:24
  19.5 8.2 %collective-permute-start.7 = (bf16[8,16,768]{2,1,0:T(8,128)(2,1)S(1)}, bf16[8,16,768]{2,1,0:T(8,128)(2,1)S(1)}, u32[]{:S(2)}, u32[]{:S(2)}) collective-permute-start(bf16[8,16,768]{2,1,0:T(8,128)(2,1)S(1)} %collective-permute-done.6), channel_id=1, source_target_pairs={{0,2},{1,3},{2,0},{3,1},{4,6},{5,7},{6,4},{7,5},{8,10},{9,11},{10,... | collective-permute-start | bytes 589832 | tf_op jit(solution)/shard_map/ppermute | solution.py:24
  19.7 8.1 %collective-permute-start.8 = (bf16[8,16,768]{2,1,0:T(8,128)(2,1)S(1)}, bf16[8,16,768]{2,1,0:T(8,128)(2,1)S(1)}, u32[]{:S(2)}, u32[]{:S(2)}) collective-permute-start(bf16[8,16,768]{2,1,0:T(8,128)(2,1)S(1)} %collective-permute-done.4), channel_id=1, source_target_pairs={{0,8},{1,9},{2,10},{3,11},{4,12},{5,13},{6,14},{7,15},{8,0},{9,1},... | collective-permute-start | bytes 589832 | tf_op jit(solution)/shard_map/ppermute | solution.py:24
  29.5 50.8 %collective-permute-start.10 = (bf16[8,8,16,768]{3,2,1,0:T(8,128)(2,1)S(1)}, bf16[8,8,16,768]{3,2,1,0:T(8,128)(2,1)S(1)}, u32[]{:S(2)}, u32[]{:S(2)}) collective-permute-start(bf16[8,8,16,768]{3,2,1,0:T(8,128)(2,1)S(1)} %bitcast_dynamic-update-slice_fusion.8.g_ref), channel_id=1, source_target_pairs={{0,1},{1,0},{2,3},{3,2},{4,5},{5,4},{6,7},{7,6},{8,9},{9,8},{10,11... | collective-permute-start | bytes 4718600 | tf_op jit(solution)/shard_map/ppermute | solution.py:24
  31.7 12.1 %collective-permute-start.15 = (bf16[256,768]{1,0:T(8,128)(2,1)S(1)}, bf16[256,768]{1,0:T(8,128)(2,1)S(1)}, u32[]{:S(2)}, u32[]{:S(2)}) collective-permute-start(bf16[256,768]{1,0:T(8,128)(2,1)S(1)} %copy-done), channel_id=1, source_target_pairs={{0,16},{16,0},{32,48},{48,32},{64,80},{80,64},{96,112},{112,96},{1... | collective-permute-start | bytes 1179656 | tf_op jit(solution)/shard_map/ppermute | solution.py:24
  34.3 45.9 %collective-permute-start.11 = (bf16[768,768]{1,0:T(8,128)(2,1)S(1)}, bf16[768,768]{1,0:T(8,128)(2,1)S(1)}, u32[]{:S(2)}, u32[]{:S(2)}) collective-permute-start(bf16[768,768]{1,0:T(8,128)(2,1)S(1)} %copy-done.1), channel_id=1, source_target_pairs={{0,16},{16,0},{32,48},{48,32},{64,80},{80,64},{96,112},{112,96},{1... | collective-permute-start | bytes 3538952 | tf_op jit(solution)/shard_map/ppermute | solution.py:24
  43.8 36.3 %collective-permute-start.18 = (bf16[2,256,768]{2,1,0:T(8,128)(2,1)S(1)}, bf16[2,256,768]{2,1,0:T(8,128)(2,1)S(1)}, u32[]{:S(2)}, u32[]{:S(2)}) collective-permute-start(bf16[2,256,768]{2,1,0:T(8,128)(2,1)S(1)} %pad_maximum_fusion), channel_id=1, source_target_pairs={{0,96},{16,112},{32,64},{48,80},{64,32},{80,48},{96,0},{112,16},{1... | collective-permute-start | bytes 2359304 | tf_op jit(solution)/shard_map/ppermute | solution.py:24
  44.9 41.9 %collective-permute-start.17 = (bf16[2,256,768]{2,1,0:T(8,128)(2,1)S(1)}, bf16[2,256,768]{2,1,0:T(8,128)(2,1)S(1)}, u32[]{:S(2)}, u32[]{:S(2)}) collective-permute-start(bf16[2,256,768]{2,1,0:T(8,128)(2,1)S(1)} %pad_maximum_fusion), channel_id=1, source_target_pairs={{0,64},{16,80},{32,96},{48,112},{64,0},{80,16},{96,32},{112,48},{1... | collective-permute-start | bytes 2359304 | tf_op jit(solution)/shard_map/ppermute | solution.py:24
  45.9 41.0 %collective-permute-start.16 = (bf16[2,256,768]{2,1,0:T(8,128)(2,1)S(1)}, bf16[2,256,768]{2,1,0:T(8,128)(2,1)S(1)}, u32[]{:S(2)}, u32[]{:S(2)}) collective-permute-start(bf16[2,256,768]{2,1,0:T(8,128)(2,1)S(1)} %pad_maximum_fusion), channel_id=1, source_target_pairs={{0,32},{16,48},{32,0},{48,16},{64,96},{80,112},{96,64},{112,80},{1... | collective-permute-start | bytes 2359304 | tf_op jit(solution)/shard_map/ppermute | solution.py:24
  82.9 9.0 %collective-permute-start.12 = (bf16[256,768]{1,0:T(8,128)(2,1)S(1)}, bf16[256,768]{1,0:T(8,128)(2,1)S(1)}, u32[]{:S(2)}, u32[]{:S(2)}) collective-permute-start(bf16[256,768]{1,0:T(8,128)(2,1)S(1)} %get-tuple-element.38), channel_id=1, source_target_pairs={{0,32},{16,48},{32,0},{48,16},{64,96},{80,112},{96,64},{112,80},{1... | collective-permute-start | bytes 1179656 | tf_op jit(solution)/shard_map/ppermute | solution.py:24
  83.0 16.9 %collective-permute-start.13 = (bf16[256,768]{1,0:T(8,128)(2,1)S(1)}, bf16[256,768]{1,0:T(8,128)(2,1)S(1)}, u32[]{:S(2)}, u32[]{:S(2)}) collective-permute-start(bf16[256,768]{1,0:T(8,128)(2,1)S(1)} %get-tuple-element.39), channel_id=1, source_target_pairs={{0,64},{16,80},{32,96},{48,112},{64,0},{80,16},{96,32},{112,48},{1... | collective-permute-start | bytes 1179656 | tf_op jit(solution)/shard_map/ppermute | solution.py:24
  84.5 15.3 %collective-permute-start.14 = (bf16[256,768]{1,0:T(8,128)(2,1)S(1)}, bf16[256,768]{1,0:T(8,128)(2,1)S(1)}, u32[]{:S(2)}, u32[]{:S(2)}) collective-permute-start(bf16[256,768]{1,0:T(8,128)(2,1)S(1)} %get-tuple-element.40), channel_id=1, source_target_pairs={{0,96},{16,112},{32,64},{48,80},{64,32},{80,48},{96,0},{112,16},{1... | collective-permute-start | bytes 1179656 | tf_op jit(solution)/shard_map/ppermute | solution.py:24
  102.3 9.0 %collective-permute-start.19 = (bf16[128,6144]{1,0:T(8,128)(2,1)S(1)}, bf16[128,6144]{1,0:T(8,128)(2,1)S(1)}, u32[]{:S(2)}, u32[]{:S(2)}) collective-permute-start(bf16[128,6144]{1,0:T(8,128)(2,1)S(1)} %get-tuple-element.42), channel_id=1, source_target_pairs={{0,1},{1,0},{2,3},{3,2},{4,5},{5,4},{6,7},{7,6},{8,9},{9,8},{10,11... | collective-permute-start | bytes 4718600 | tf_op jit(solution)/shard_map/ppermute | solution.py:24
  112.5 11.2 %collective-permute-start.21 = (bf16[16,6144]{1,0:T(8,128)(2,1)S(1)}, bf16[16,6144]{1,0:T(8,128)(2,1)S(1)}, u32[]{:S(2)}, u32[]{:S(2)}) collective-permute-start(bf16[16,6144]{1,0:T(8,128)(2,1)S(1)} %get-tuple-element.45), channel_id=1, source_target_pairs={{0,4},{1,5},{2,6},{3,7},{4,0},{5,1},{6,2},{7,3},{8,12},{9,13},{10,... | collective-permute-start | bytes 589832 | tf_op jit(solution)/shard_map/ppermute | solution.py:24
  114.9 11.3 %collective-permute-start.22 = (bf16[16,6144]{1,0:T(8,128)(2,1)S(1)}, bf16[16,6144]{1,0:T(8,128)(2,1)S(1)}, u32[]{:S(2)}, u32[]{:S(2)}) collective-permute-start(bf16[16,6144]{1,0:T(8,128)(2,1)S(1)} %get-tuple-element.46), channel_id=1, source_target_pairs={{0,6},{1,7},{2,4},{3,5},{4,2},{5,3},{6,0},{7,1},{8,14},{9,15},{10,... | collective-permute-start | bytes 589832 | tf_op jit(solution)/shard_map/ppermute | solution.py:24
  115.6 10.5 %collective-permute-start.23 = (bf16[16,6144]{1,0:T(8,128)(2,1)S(1)}, bf16[16,6144]{1,0:T(8,128)(2,1)S(1)}, u32[]{:S(2)}, u32[]{:S(2)}) collective-permute-start(bf16[16,6144]{1,0:T(8,128)(2,1)S(1)} %get-tuple-element.47), channel_id=1, source_target_pairs={{0,8},{1,9},{2,10},{3,11},{4,12},{5,13},{6,14},{7,15},{8,0},{9,1},... | collective-permute-start | bytes 589832 | tf_op jit(solution)/shard_map/ppermute | solution.py:24
  115.8 10.4 %collective-permute-start.24 = (bf16[16,6144]{1,0:T(8,128)(2,1)S(1)}, bf16[16,6144]{1,0:T(8,128)(2,1)S(1)}, u32[]{:S(2)}, u32[]{:S(2)}) collective-permute-start(bf16[16,6144]{1,0:T(8,128)(2,1)S(1)} %get-tuple-element.48), channel_id=1, source_target_pairs={{0,10},{1,11},{2,8},{3,9},{4,14},{5,15},{6,12},{7,13},{8,2},{9,3},... | collective-permute-start | bytes 589832 | tf_op jit(solution)/shard_map/ppermute | solution.py:24
  117.8 14.3 %collective-permute-start.25 = (bf16[16,6144]{1,0:T(8,128)(2,1)S(1)}, bf16[16,6144]{1,0:T(8,128)(2,1)S(1)}, u32[]{:S(2)}, u32[]{:S(2)}) collective-permute-start(bf16[16,6144]{1,0:T(8,128)(2,1)S(1)} %get-tuple-element.49), channel_id=1, source_target_pairs={{0,12},{1,13},{2,14},{3,15},{4,8},{5,9},{6,10},{7,11},{8,4},{9,5},... | collective-permute-start | bytes 589832 | tf_op jit(solution)/shard_map/ppermute | solution.py:24
  123.7 12.3 %collective-permute-start.26 = (bf16[16,6144]{1,0:T(8,128)(2,1)S(1)}, bf16[16,6144]{1,0:T(8,128)(2,1)S(1)}, u32[]{:S(2)}, u32[]{:S(2)}) collective-permute-start(bf16[16,6144]{1,0:T(8,128)(2,1)S(1)} %get-tuple-element.50), channel_id=1, source_target_pairs={{0,14},{1,15},{2,12},{3,13},{4,10},{5,11},{6,8},{7,9},{8,6},{9,7},... | collective-permute-start | bytes 589832 | tf_op jit(solution)/shard_map/ppermute | solution.py:24
  137.1 10.5 %collective-permute-start.29 = (bf16[16,6144]{1,0:T(8,128)(2,1)S(1)}, bf16[16,6144]{1,0:T(8,128)(2,1)S(1)}, u32[]{:S(2)}, u32[]{:S(2)}) collective-permute-start(bf16[16,6144]{1,0:T(8,128)(2,1)S(1)} %shard_map.113), channel_id=1, source_target_pairs={{0,6},{1,7},{2,4},{3,5},{4,2},{5,3},{6,0},{7,1},{8,14},{9,15},{10,... | collective-permute-start | bytes 589832 | tf_op jit(solution)/shard_map/ppermute | solution.py:24
  139.2 8.3 %collective-permute-start.27 = (bf16[16,6144]{1,0:T(8,128)(2,1)S(1)}, bf16[16,6144]{1,0:T(8,128)(2,1)S(1)}, u32[]{:S(2)}, u32[]{:S(2)}) collective-permute-start(bf16[16,6144]{1,0:T(8,128)(2,1)S(1)} %shard_map.113), channel_id=1, source_target_pairs={{0,2},{1,3},{2,0},{3,1},{4,6},{5,7},{6,4},{7,5},{8,10},{9,11},{10,... | collective-permute-start | bytes 589832 | tf_op jit(solution)/shard_map/ppermute | solution.py:24
  142.6 9.7 %collective-permute-start.33 = (bf16[16,6144]{1,0:T(8,128)(2,1)S(1)}, bf16[16,6144]{1,0:T(8,128)(2,1)S(1)}, u32[]{:S(2)}, u32[]{:S(2)}) collective-permute-start(bf16[16,6144]{1,0:T(8,128)(2,1)S(1)} %collective-permute-done.30), channel_id=1, source_target_pairs={{0,6},{1,7},{2,4},{3,5},{4,2},{5,3},{6,0},{7,1},{8,14},{9,15},{10,... | collective-permute-start | bytes 589832 | tf_op jit(solution)/shard_map/ppermute | solution.py:24
  143.4 8.3 %collective-permute-start.31 = (bf16[16,6144]{1,0:T(8,128)(2,1)S(1)}, bf16[16,6144]{1,0:T(8,128)(2,1)S(1)}, u32[]{:S(2)}, u32[]{:S(2)}) collective-permute-start(bf16[16,6144]{1,0:T(8,128)(2,1)S(1)} %collective-permute-done.30), channel_id=1, source_target_pairs={{0,2},{1,3},{2,0},{3,1},{4,6},{5,7},{6,4},{7,5},{8,10},{9,11},{10,... | collective-permute-start | bytes 589832 | tf_op jit(solution)/shard_map/ppermute | solution.py:24
  152.2 16.4 %collective-permute-start.34 = (bf16[8,16,6144]{2,1,0:T(8,128)(2,1)S(1)}, bf16[8,16,6144]{2,1,0:T(8,128)(2,1)}, u32[]{:S(2)}, u32[]{:S(2)}) collective-permute-start(bf16[8,16,6144]{2,1,0:T(8,128)(2,1)S(1)} %bitcast_dynamic-update-slice_fusion.g_ref), channel_id=1, source_target_pairs={{0,1},{1,0},{2,3},{3,2},{4,5},{5,4},{6,7},{7,6},{8,9},{9,8},{10,11... | collective-permute-start | bytes 4718600 | tf_op jit(solution)/shard_map/ppermute | solution.py:24
  175.5 11.7 %collective-permute-start.36 = (bf16[2,16,3072]{2,1,0:T(8,128)(2,1)S(1)}, bf16[2,16,3072]{2,1,0:T(8,128)(2,1)S(1)}, u32[]{:S(2)}, u32[]{:S(2)}) collective-permute-start(bf16[2,16,3072]{2,1,0:T(8,128)(2,1)S(1)} %get-tuple-element.55), channel_id=1, source_target_pairs={{0,4},{1,5},{2,6},{3,7},{4,0},{5,1},{6,2},{7,3},{8,12},{9,13},{10,... | collective-permute-start | bytes 589832 | tf_op jit(solution)/shard_map/ppermute | solution.py:24
  178.0 11.3 %collective-permute-start.37 = (bf16[2,16,3072]{2,1,0:T(8,128)(2,1)S(1)}, bf16[2,16,3072]{2,1,0:T(8,128)(2,1)S(1)}, u32[]{:S(2)}, u32[]{:S(2)}) collective-permute-start(bf16[2,16,3072]{2,1,0:T(8,128)(2,1)S(1)} %get-tuple-element.56), channel_id=1, source_target_pairs={{0,6},{1,7},{2,4},{3,5},{4,2},{5,3},{6,0},{7,1},{8,14},{9,15},{10,... | collective-permute-start | bytes 589832 | tf_op jit(solution)/shard_map/ppermute | solution.py:24
  179.3 10.0 %collective-permute-start.38 = (bf16[2,16,3072]{2,1,0:T(8,128)(2,1)S(1)}, bf16[2,16,3072]{2,1,0:T(8,128)(2,1)S(1)}, u32[]{:S(2)}, u32[]{:S(2)}) collective-permute-start(bf16[2,16,3072]{2,1,0:T(8,128)(2,1)S(1)} %get-tuple-element.57), channel_id=1, source_target_pairs={{0,8},{1,9},{2,10},{3,11},{4,12},{5,13},{6,14},{7,15},{8,0},{9,1},... | collective-permute-start | bytes 589832 | tf_op jit(solution)/shard_map/ppermute | solution.py:24
  179.8 10.8 %collective-permute-start.39 = (bf16[2,16,3072]{2,1,0:T(8,128)(2,1)S(1)}, bf16[2,16,3072]{2,1,0:T(8,128)(2,1)S(1)}, u32[]{:S(2)}, u32[]{:S(2)}) collective-permute-start(bf16[2,16,3072]{2,1,0:T(8,128)(2,1)S(1)} %get-tuple-element.58), channel_id=1, source_target_pairs={{0,10},{1,11},{2,8},{3,9},{4,14},{5,15},{6,12},{7,13},{8,2},{9,3},... | collective-permute-start | bytes 589832 | tf_op jit(solution)/shard_map/ppermute | solution.py:24
  181.9 14.2 %collective-permute-start.40 = (bf16[2,16,3072]{2,1,0:T(8,128)(2,1)S(1)}, bf16[2,16,3072]{2,1,0:T(8,128)(2,1)S(1)}, u32[]{:S(2)}, u32[]{:S(2)}) collective-permute-start(bf16[2,16,3072]{2,1,0:T(8,128)(2,1)S(1)} %get-tuple-element.59), channel_id=1, source_target_pairs={{0,12},{1,13},{2,14},{3,15},{4,8},{5,9},{6,10},{7,11},{8,4},{9,5},... | collective-permute-start | bytes 589832 | tf_op jit(solution)/shard_map/ppermute | solution.py:24
  187.2 12.7 %collective-permute-start.41 = (bf16[2,16,3072]{2,1,0:T(8,128)(2,1)S(1)}, bf16[2,16,3072]{2,1,0:T(8,128)(2,1)S(1)}, u32[]{:S(2)}, u32[]{:S(2)}) collective-permute-start(bf16[2,16,3072]{2,1,0:T(8,128)(2,1)S(1)} %get-tuple-element.60), channel_id=1, source_target_pairs={{0,14},{1,15},{2,12},{3,13},{4,10},{5,11},{6,8},{7,9},{8,6},{9,7},... | collective-permute-start | bytes 589832 | tf_op jit(solution)/shard_map/ppermute | solution.py:24
  205.7 7.9 %collective-permute-start.44 = (bf16[2,16,1024]{2,1,0:T(8,128)(2,1)S(1)}, bf16[2,16,1024]{2,1,0:T(8,128)(2,1)S(1)}, u32[]{:S(2)}, u32[]{:S(2)}) collective-permute-start(bf16[2,16,1024]{2,1,0:T(8,128)(2,1)S(1)} %get-tuple-element.63), channel_id=1, source_target_pairs={{0,4},{1,5},{2,6},{3,7},{4,0},{5,1},{6,2},{7,3},{8,12},{9,13},{10,... | collective-permute-start | bytes 196616 | tf_op jit(solution)/shard_map/ppermute | solution.py:24
  (27 other events, 225.3 us)
where the time goes:
time: 225 us
  waiting for transfers between devices  120 us (53%)
  starting transfers between devices  70.7 us (31%)
  Pallas kernels  24.3 us (11%)
  local copies, waits for them, and re-layouts  7.78 us (3%)
    ppermute x51, waiting for transfers between devices, swap(): return lax.ppermute(value, axis, [(i, i ^ flip) for i in range(size)])  120 us
    ppermute x51, starting transfers between devices, swap(): return lax.ppermute(value, axis, [(i, i ^ flip) for i in range(size)])  70.7 us
    pallas_call x8, Pallas kernels, go(): return run(*args[:smem], *near)  17.9 us
    pallas_call x1, Pallas kernels, fetch(): pl.pallas_call(fetch_kernel, out_shape=[pltpu.VMEM(a.shape, a.dtype) for...  6.39 us
  transfers between devices with their start and end apart: 51, of which 32 were waited for; matrix products, arithmetic and copies ran while one was open for 3% of the time, Pallas kernels for 4%

commit v1 on v0

--- a/solution.py
+++ b/solution.py
@@ -51,14 +51,16 @@
         o_ref[ids[0] ^ b] = y[:, b * width:(b + 1) * width]
 
 
-def qkv_kernel(g_ref, h_ref, w0_ref, w1_ref, *outs):
+def qkv_kernel(g_ref, h_ref, w0_ref, w1_ref, w2_ref, *outs):
     width = w0_ref.shape[0]
+    half = width // 2
     for d, o_ref in enumerate(outs):
         for kk, src in enumerate((g_ref, h_ref)):
             a = src[:, 2 * d].reshape(-1, width)
             b = src[:, 2 * d + 1].reshape(-1, width)
             acc = jnp.dot(a, w0_ref[...], preferred_element_type=F32)
-            acc = acc + jnp.dot(b, w1_ref[...], preferred_element_type=F32)
+            acc = acc + jnp.dot(b[:, :half], w1_ref[...], preferred_element_type=F32)
+            acc = acc + jnp.dot(b[:, half:], w2_ref[...], preferred_element_type=F32)
             rows = acc.shape[0]
             o_ref[kk * rows:(kk + 1) * rows, :] = acc.astype(o_ref.dtype)
 
@@ -114,9 +116,9 @@
 
 
 def hidden_kernel(ids, frames, gain, *rest):
-    pieces = rest[:8]
-    o_ref = rest[8]
-    acc = rest[9]
+    pieces = rest[:5]
+    o_ref = rest[5]
+    acc = rest[6]
     width = frames.shape[1] // 8
     for e in range(8):
         cut = slice(e * width, (e + 1) * width)
@@ -228,7 +230,18 @@
         o_ref[ids[1] ^ (2 * e + 1)] = other[e]
 
 
-def gather(value):
+def add_kernel(*refs):
+    part = refs[0][...].astype(F32)
+    for ref in refs[1:-1]:
+        part = part + ref[...].astype(F32)
+    refs[-1][...] = part.astype(BF)
+
+
+def add(*values):
+    return call(add_kernel, [(values[0].shape, BF)], n_in=len(values), limit=2)(*values)[0]
+
+
+def gather(value, across=False):
     def cb(v, flip):
         return swap(v, "cb", 16, flip)
 
@@ -238,7 +251,7 @@
     x2 = cb(value, 4)
     y1 = cb(y, 2)
     y3 = cb(y, 6)
-    y2 = cb(x2, 8)
+    y2 = cb(y, 4) if across else cb(x2, 8)
     return [value, x1, x2, x3, y, y1, y2, y3]
 
 
@@ -255,21 +268,20 @@
     rel = call(norm_kernel, [((8, 16, block), BF)], smem=1, n_in=3)(
         ids, mine, t_gain[None]
     )[0]
-    w_other = fs(w_qkv, 1)
-    wo_other = fs(w_out, 1)
+    rows = w_qkv.shape[0] // 2
+    w_other0 = fs(w_qkv[:rows], 1)
+    w_other1 = fs(w_qkv[rows:], 1)
     local = [rel[0:2]] + [fs(rel[2 * d:2 * d + 2], 2 * d) for d in (1, 2, 3)]
     local = jnp.concatenate(local, axis=0)
-    even = jnp.stack(gather(local))
+    wo_even = [w_out] + [fs(w_out, 2 * d) for d in (1, 2, 3)]
+    wo_odd = [fs(w, 1) for w in wo_even]
+    wo = [w for pair in zip(wo_even, wo_odd) for w in pair]
+    even = jnp.stack(gather(local, True))
     odd = cb(even, 1)
     cols = w_qkv.shape[1]
     parts = call(
-        qkv_kernel, [((256, cols), F32)] + [((256, cols), BF)] * 3, n_in=4
-    )(even, odd, w_qkv, w_other)
-    wo_pair = jnp.stack([w_out, wo_other])
-    wo_far = [fs(wo_pair, 2 * d) for d in (1, 2, 3)]
-    wo = [w_out, wo_other]
-    for pair in wo_far:
-        wo += [pair[0], pair[1]]
+        qkv_kernel, [((256, cols), F32)] + [((256, cols), BF)] * 3, n_in=5
+    )(even, odd, w_qkv, w_other0, w_other1)
     sums = [fs(parts[d], 2 * d) for d in (1, 2, 3)]
     keep, give = call(
         attn_kernel,
@@ -282,13 +294,18 @@
     blocks = call(pair_kernel, [((16, model), F32)] + [((16, model), BF)] * 7, n_in=2)(
         keep, taken
     )
-    pieces = [blocks[0]] + [cb(blocks[e], 2 * e) for e in range(1, 8)]
+    far1, far3 = cb(blocks[5], 2), cb(blocks[7], 6)
+    far2 = cb(blocks[6], 8)
+    near1, near3 = cb(blocks[1], 2), cb(blocks[3], 6)
+    side = add(blocks[4], far1, far3)
+    deep = add(blocks[2], far2)
+    pieces = [blocks[0], near1, near3, cb(side, 8), cb(deep, 4)]
     hn = call(
         hidden_kernel,
         [((16, model), BF)],
         scratch=[pltpu.VMEM((8, 16, block), F32)],
         smem=1,
-        n_in=11,
+        n_in=8,
     )(ids, mine, h_gain[None], *pieces)[0]
     even = jnp.stack(gather(hn))
     odd = cb(even, 1)

time: 225 us -> 215 us (0.956)
  waiting for transfers between devices: 120 us -> 100 us
  starting transfers between devices: 70.7 us -> 79.9 us
    ppermute x51 -> x55, waiting for transfers between devices: 120 us -> 100 us  [swap(): return lax.ppermute(value, axis, [(i, i ^ flip) for i in range(size)])]
    ppermute x51 -> x55, starting transfers between devices: 70.7 us -> 79.9 us  [swap(): return lax.ppermute(value, axis, [(i, i ^ flip) for i in range(size)])]
    pallas_call x8 -> x10, Pallas kernels: 17.9 us -> 18.3 us  [go(): return run(*args[:smem], *near)]
  transfers between devices with their start and end apart: 51 -> 55, of which waited for: 32 -> 35; matrix products, arithmetic and copies ran while one was open for 3% -> 3% of each run, Pallas kernels for 4% -> 4%
where the time goes in v1:
time: 215 us
  waiting for transfers between devices  100 us (47%)
  starting transfers between devices  79.9 us (37%)
  Pallas kernels  24.7 us (11%)
  local copies, waits for them, and re-layouts  7.68 us (4%)
    ppermute x55, waiting for transfers between devices, swap(): return lax.ppermute(value, axis, [(i, i ^ flip) for i in range(size)])  100 us
    ppermute x55, starting transfers between devices, swap(): return lax.ppermute(value, axis, [(i, i ^ flip) for i in range(size)])  79.9 us
    pallas_call x10, Pallas kernels, go(): return run(*args[:smem], *near)  18.3 us
    pallas_call x1, Pallas kernels, fetch(): pl.pallas_call(fetch_kernel, out_shape=[pltpu.VMEM(a.shape, a.dtype) for...  6.39 us
  transfers between devices with their start and end apart: 55, of which 35 were waited for; matrix products, arithmetic and copies ran while one was open for 3% of the time, Pallas kernels for 4%

profile of v1, /device:TPU:1, one launch (start us, length us, event | category | flops | bytes accessed | tf_op | source)
XLA Modules:
  0.0 214.6 jit_solution(12626936910750075257)
XLA Ops:
  3.2 4.7 %collective-permute-start.2 = (bf16[2,16,768]{2,1,0:T(8,128)(2,1)S(1)}, bf16[2,16,768]{2,1,0:T(8,128)(2,1)S(1)}, u32[]{:S(2)}, u32[]{:S(2)}) collective-permute-start(bf16[2,16,768]{2,1,0:T(8,128)(2,1)S(1)} %get-tuple-element.72), channel_id=1, source_target_pairs={{0,96},{16,112},{32,64},{48,80},{64,32},{80,48},{96,0},{112,16},{1... | collective-permute-start | bytes 147464 | tf_op jit(solution)/shard_map/ppermute | solution.py:24
  9.3 3.0 %collective-permute-done.1 = bf16[2,16,768]{2,1,0:T(8,128)(2,1)S(1)} collective-permute-done((bf16[2,16,768]{2,1,0:T(8,128)(2,1)S(1)}, bf16[2,16,768]{2,1,0:T(8,128)(2,1)S(1)}, u32[]{:S(2)}, u32[]{:S(2)}) %collective-permute-start.1) | collective-permute-done | bytes 49184 | tf_op jit(solution)/shard_map/ppermute | solution.py:24
  20.7 3.6 %collective-permute-done.4 = bf16[8,16,768]{2,1,0:T(8,128)(2,1)S(1)} collective-permute-done((bf16[8,16,768]{2,1,0:T(8,128)(2,1)S(1)}, bf16[8,16,768]{2,1,0:T(8,128)(2,1)S(1)}, u32[]{:S(2)}, u32[]{:S(2)}) %collective-permute-start.4) | collective-permute-done | bytes 196640 | tf_op jit(solution)/shard_map/ppermute | solution.py:24
  24.4 7.7 %collective-permute-done.7 = bf16[8,16,768]{2,1,0:T(8,128)(2,1)S(1)} collective-permute-done((bf16[8,16,768]{2,1,0:T(8,128)(2,1)S(1)}, bf16[8,16,768]{2,1,0:T(8,128)(2,1)S(1)}, u32[]{:S(2)}, u32[]{:S(2)}) %collective-permute-start.7) | collective-permute-done | bytes 196640 | tf_op jit(solution)/shard_map/ppermute | solution.py:24
  32.6 3.6 %collective-permute-start.10 = (bf16[8,8,16,768]{3,2,1,0:T(8,128)(2,1)S(1)}, bf16[8,8,16,768]{3,2,1,0:T(8,128)(2,1)S(1)}, u32[]{:S(2)}, u32[]{:S(2)}) collective-permute-start(bf16[8,8,16,768]{3,2,1,0:T(8,128)(2,1)S(1)} %bitcast_dynamic-update-slice_fusion.8.g_ref), channel_id=1, source_target_pairs={{0,1},{1,0},{2,3},{3,2},{4,5},{5,4},{6,7},{7,6},{8,9},{9,8},{10,11... | collective-permute-start | bytes 4718600 | tf_op jit(solution)/shard_map/ppermute | solution.py:24
  39.5 2.7 %collective-permute-start.12 = (bf16[384,768]{1,0:T(8,128)(2,1)S(1)}, bf16[384,768]{1,0:T(8,128)(2,1)S(1)}, u32[]{:S(2)}, u32[]{:S(2)}) collective-permute-start(bf16[384,768]{1,0:T(8,128)(2,1)S(1)} %get-tuple-element.69), channel_id=1, source_target_pairs={{0,16},{16,0},{32,48},{48,32},{64,80},{80,64},{96,112},{112,96},{1... | collective-permute-start | bytes 1769480 | tf_op jit(solution)/shard_map/ppermute | solution.py:24
  42.2 6.1 %collective-permute-done.19.rest_4_ = bf16[256,768]{1,0:T(8,128)(2,1)S(1)} collective-permute-done((bf16[256,768]{1,0:T(8,128)(2,1)S(1)}, bf16[256,768]{1,0:T(8,128)(2,1)S(1)}, u32[]{:S(2)}, u32[]{:S(2)}) %collective-permute-start.19) | collective-permute-done | bytes 393248 | tf_op jit(solution)/shard_map/ppermute | solution.py:24
  48.3 2.6 %collective-permute-start.11 = (bf16[384,768]{1,0:T(8,128)(2,1)S(1)}, bf16[384,768]{1,0:T(8,128)(2,1)S(1)}, u32[]{:S(2)}, u32[]{:S(2)}) collective-permute-start(bf16[384,768]{1,0:T(8,128)(2,1)S(1)} %get-tuple-element.70), channel_id=1, source_target_pairs={{0,16},{16,0},{32,48},{48,32},{64,80},{80,64},{96,112},{112,96},{1... | collective-permute-start | bytes 1769480 | tf_op jit(solution)/shard_map/ppermute | solution.py:24
  50.9 4.6 %collective-permute-done.17.rest_2_ = bf16[256,768]{1,0:T(8,128)(2,1)S(1)} collective-permute-done((bf16[256,768]{1,0:T(8,128)(2,1)S(1)}, bf16[256,768]{1,0:T(8,128)(2,1)S(1)}, u32[]{:S(2)}, u32[]{:S(2)}) %collective-permute-start.17) | collective-permute-done | bytes 393248 | tf_op jit(solution)/shard_map/ppermute | solution.py:24
  55.5 2.6 %collective-permute-start.16 = (bf16[256,768]{1,0:T(8,128)(2,1)S(1)}, bf16[256,768]{1,0:T(8,128)(2,1)S(1)}, u32[]{:S(2)}, u32[]{:S(2)}) collective-permute-start(bf16[256,768]{1,0:T(8,128)(2,1)S(1)} %copy-done.3), channel_id=1, source_target_pairs={{0,16},{16,0},{32,48},{48,32},{64,80},{80,64},{96,112},{112,96},{1... | collective-permute-start | bytes 1179656 | tf_op jit(solution)/shard_map/ppermute | solution.py:24
  61.1 6.5 %collective-permute-done.11.w1_ref = bf16[384,768]{1,0:T(8,128)(2,1)S(1)} collective-permute-done((bf16[384,768]{1,0:T(8,128)(2,1)S(1)}, bf16[384,768]{1,0:T(8,128)(2,1)S(1)}, u32[]{:S(2)}, u32[]{:S(2)}) %collective-permute-start.11) | collective-permute-done | bytes 589856 | tf_op jit(solution)/shard_map/ppermute | solution.py:24
  67.7 2.6 %collective-permute-start.22 = (bf16[256,768]{1,0:T(8,128)(2,1)S(1)}, bf16[256,768]{1,0:T(8,128)(2,1)S(1)}, u32[]{:S(2)}, u32[]{:S(2)}) collective-permute-start(bf16[256,768]{1,0:T(8,128)(2,1)S(1)} %collective-permute-done.21.rest_6_), channel_id=1, source_target_pairs={{0,16},{16,0},{32,48},{48,32},{64,80},{80,64},{96,112},{112,96},{1... | collective-permute-start | bytes 1179656 | tf_op jit(solution)/shard_map/ppermute | solution.py:24
  70.3 3.0 %shard_map.110 = (f32[256,768]{1,0:T(8,128)S(1)}, bf16[256,768]{1,0:T(8,128)(2,1)S(1)}, bf16[256,768]{1,0:T(8,128)(2,1)S(1)}, bf16[256,768]{1,0:T(8,128)(2,1)S(1)}) custom-call(bf16[8,8,16,768]{3,2,1,0:T(8,128)(2,1)S(1)} %bitcast_dynamic-update-slice_fusion.8.g_ref, bf16[8,8,16,768]{3,2,1,0:T(8,128)(2,1)S(1)} %collective-permute-done.10.h_ref, ...), custom_call_target="tpu_custom_call" | custom-call | tf_op jit(solution)/shard_map/pallas_call | solution.py:40
  78.1 6.5 %collective-permute-done.20.rest_5_ = bf16[256,768]{1,0:T(8,128)(2,1)S(1)} collective-permute-done((bf16[256,768]{1,0:T(8,128)(2,1)S(1)}, bf16[256,768]{1,0:T(8,128)(2,1)S(1)}, u32[]{:S(2)}, u32[]{:S(2)}) %collective-permute-start.20) | collective-permute-done | bytes 393248 | tf_op jit(solution)/shard_map/ppermute | solution.py:24
  86.1 6.9 %collective-permute-done.18.rest_3_ = bf16[256,768]{1,0:T(8,128)(2,1)S(1)} collective-permute-done((bf16[256,768]{1,0:T(8,128)(2,1)S(1)}, bf16[256,768]{1,0:T(8,128)(2,1)S(1)}, u32[]{:S(2)}, u32[]{:S(2)}) %collective-permute-start.18) | collective-permute-done | bytes 393248 | tf_op jit(solution)/shard_map/ppermute | solution.py:24
  93.0 8.4 %collective-permute-done.22.rest_7_ = bf16[256,768]{1,0:T(8,128)(2,1)S(1)} collective-permute-done((bf16[256,768]{1,0:T(8,128)(2,1)S(1)}, bf16[256,768]{1,0:T(8,128)(2,1)S(1)}, u32[]{:S(2)}, u32[]{:S(2)}) %collective-permute-start.22) | collective-permute-done | bytes 393248 | tf_op jit(solution)/shard_map/ppermute | solution.py:24
  101.6 2.5 %shard_map.111 = (bf16[128,6144]{1,0:T(8,128)(2,1)S(1)}, bf16[128,6144]{1,0:T(8,128)(2,1)S(1)}) custom-call(s32[3]{0:T(128)S(1)} %pad_add_fusion.ids, f32[256,768]{1,0:T(8,128)S(1)} %get-tuple-element.37.own, bf16[256,768]{1,0:T(8,128)(2,1)S(1)} %collective-permute-done.13.r1, bf16[256,768]{1,0:T(8,128)(2,1)S(1)} %collective-permute-done.14.r2, ...), custom_call_target="tpu_custom_call" | custom-call | tf_op jit(solution)/shard_map/pallas_call | solution.py:40
  106.0 3.0 %collective-permute-done.23.b_ref = bf16[128,6144]{1,0:T(8,128)(2,1)S(1)} collective-permute-done((bf16[128,6144]{1,0:T(8,128)(2,1)S(1)}, bf16[128,6144]{1,0:T(8,128)(2,1)S(1)}, u32[]{:S(2)}, u32[]{:S(2)}) %collective-permute-start.23) | collective-permute-done | bytes 1572896 | tf_op jit(solution)/shard_map/ppermute | solution.py:24
  121.6 2.3 %collective-permute-done.30.rest_4_ = bf16[16,6144]{1,0:T(8,128)(2,1)S(1)} collective-permute-done((bf16[16,6144]{1,0:T(8,128)(2,1)S(1)}, bf16[16,6144]{1,0:T(8,128)(2,1)S(1)}, u32[]{:S(2)}, u32[]{:S(2)}) %collective-permute-start.30) | collective-permute-done | bytes 196640 | tf_op jit(solution)/shard_map/ppermute | solution.py:24
  130.7 2.7 %collective-permute-done.32 = bf16[16,6144]{1,0:T(8,128)(2,1)S(1)} collective-permute-done((bf16[16,6144]{1,0:T(8,128)(2,1)S(1)}, bf16[16,6144]{1,0:T(8,128)(2,1)S(1)}, u32[]{:S(2)}, u32[]{:S(2)}) %collective-permute-start.32) | collective-permute-done | bytes 196640 | tf_op jit(solution)/shard_map/ppermute | solution.py:24
  134.2 3.4 %collective-permute-done.35 = bf16[16,6144]{1,0:T(8,128)(2,1)S(1)} collective-permute-done((bf16[16,6144]{1,0:T(8,128)(2,1)S(1)}, bf16[16,6144]{1,0:T(8,128)(2,1)S(1)}, u32[]{:S(2)}, u32[]{:S(2)}) %collective-permute-start.35) | collective-permute-done | bytes 196640 | tf_op jit(solution)/shard_map/ppermute | solution.py:24
  139.2 7.1 %collective-permute-start.38 = (bf16[8,16,6144]{2,1,0:T(8,128)(2,1)S(1)}, bf16[8,16,6144]{2,1,0:T(8,128)(2,1)}, u32[]{:S(2)}, u32[]{:S(2)}) collective-permute-start(bf16[8,16,6144]{2,1,0:T(8,128)(2,1)S(1)} %bitcast_dynamic-update-slice_fusion.g_ref), channel_id=1, source_target_pairs={{0,1},{1,0},{2,3},{3,2},{4,5},{5,4},{6,7},{7,6},{8,9},{9,8},{10,11... | collective-permute-start | bytes 4718600 | tf_op jit(solution)/shard_map/ppermute | solution.py:24
  148.3 4.3 %gather_fusion.1 = bf16[256,1024]{1,0:T(8,128)(2,1)S(1)} fusion(bf16[2048,1024]{1,0:T(8,128)(2,1)} %bitcast.54, s32[1024]{0:T(1024)S(1)} %pad_clamp_fusion), kind=kCustom, calls=%fused_computation.1 | custom fusion | bytes 1049600 | tf_op jit(solution)/shard_map/gather | solution.py:315
  152.7 6.4 %shard_map.116 = (bf16[6144,1024]{1,0:T(8,128)(2,1)S(1)}, bf16[1024,3072]{1,0:T(8,128)(2,1)S(1)}) custom-call(bf16[6144,1024]{1,0:T(8,128)(2,1)} %bitcast.52, bf16[1024,3072]{1,0:T(8,128)(2,1)} %bitcast.53), custom_call_target="tpu_custom_call" | custom-call | tf_op jit(solution)/shard_map/pallas_call | solution.py:172
  159.1 6.8 %shard_map.117 = (bf16[2,16,3072]{2,1,0:T(8,128)(2,1)S(1)}, bf16[2,16,3072]{2,1,0:T(8,128)(2,1)S(1)}, bf16[2,16,3072]{2,1,0:T(8,128)(2,1)S(1)}, bf16[2,16,3072]{...) custom-call(bf16[8,16,6144]{2,1,0:T(8,128)(2,1)S(1)} %bitcast_dynami, ...), custom_call_target="tpu_custom_call" | custom-call | tf_op jit(solution)/shard_map/pallas_call | solution.py:40
  173.4 3.6 %collective-permute-done.40.rest_2_ = bf16[2,16,3072]{2,1,0:T(8,128)(2,1)S(1)} collective-permute-done((bf16[2,16,3072]{2,1,0:T(8,128)(2,1)S(1)}, bf16[2,16,3072]{2,1,0:T(8,128)(2,1)S(1)}, u32[]{:S(2)}, u32[]{:S(2)}) %collective-permute-start.40) | collective-permute-done | bytes 196640 | tf_op jit(solution)/shard_map/ppermute | solution.py:24
  180.9 4.8 %collective-permute-done.44.rest_6_ = bf16[2,16,3072]{2,1,0:T(8,128)(2,1)S(1)} collective-permute-done((bf16[2,16,3072]{2,1,0:T(8,128)(2,1)S(1)}, bf16[2,16,3072]{2,1,0:T(8,128)(2,1)S(1)}, u32[]{:S(2)}, u32[]{:S(2)}) %collective-permute-start.44) | collective-permute-done | bytes 196640 | tf_op jit(solution)/shard_map/ppermute | solution.py:24
  185.7 3.9 %collective-permute-done.45.rest_7_ = bf16[2,16,3072]{2,1,0:T(8,128)(2,1)S(1)} collective-permute-done((bf16[2,16,3072]{2,1,0:T(8,128)(2,1)S(1)}, bf16[2,16,3072]{2,1,0:T(8,128)(2,1)S(1)}, u32[]{:S(2)}, u32[]{:S(2)}) %collective-permute-start.45) | collective-permute-done | bytes 196640 | tf_op jit(solution)/shard_map/ppermute | solution.py:24
  192.5 2.7 %shard_map.118 = (bf16[2,16,1024]{2,1,0:T(8,128)(2,1)S(1)}, bf16[2,16,1024]{2,1,0:T(8,128)(2,1)S(1)}, bf16[2,16,1024]{2,1,0:T(8,128)(2,1)S(1)}, bf16[2,16,1024]{...) custom-call(s32[3]{0:T(128)S(1)} %pad_add_fusion.ids, ...), custom_call_target="tpu_custom_call" | custom-call | tf_op jit(solution)/shard_map/pallas_call | solution.py:40
  195.2 3.1 %collective-permute-start.48 = (bf16[2,16,1024]{2,1,0:T(8,128)(2,1)S(1)}, bf16[2,16,1024]{2,1,0:T(8,128)(2,1)S(1)}, u32[]{:S(2)}, u32[]{:S(2)}) collective-permute-start(bf16[2,16,1024]{2,1,0:T(8,128)(2,1)S(1)} %get-tuple-element.63), channel_id=1, source_target_pairs={{0,4},{1,5},{2,6},{3,7},{4,0},{5,1},{6,2},{7,3},{8,12},{9,13},{10,... | collective-permute-start | bytes 196616 | tf_op jit(solution)/shard_map/ppermute | solution.py:24
  200.1 3.6 %collective-permute-start.52 = (bf16[2,16,1024]{2,1,0:T(8,128)(2,1)S(1)}, bf16[2,16,1024]{2,1,0:T(8,128)(2,1)S(1)}, u32[]{:S(2)}, u32[]{:S(2)}) collective-permute-start(bf16[2,16,1024]{2,1,0:T(8,128)(2,1)S(1)} %get-tuple-element.67), channel_id=1, source_target_pairs={{0,12},{1,13},{2,14},{3,15},{4,8},{5,9},{6,10},{7,11},{8,4},{9,5},... | collective-permute-start | bytes 196616 | tf_op jit(solution)/shard_map/ppermute | solution.py:24
  208.9 3.2 %collective-permute-start.54 = (bf16[8,16,1024]{2,1,0:T(8,128)(2,1)S(1)}, bf16[8,16,1024]{2,1,0:T(8,128)(2,1)S(1)}, u32[]{:S(2)}, u32[]{:S(2)}) collective-permute-start(bf16[8,16,1024]{2,1,0:T(8,128)(2,1)S(1)} %constant_dynamic-update-slice_fusion), channel_id=1, source_target_pairs={{0,1},{1,0},{2,3},{3,2},{4,5},{5,4},{6,7},{7,6},{8,9},{9,8},{10,11... | collective-permute-start | bytes 786440 | tf_op jit(solution)/shard_map/ppermute | solution.py:24
  (152 shorter events, 75.2 us)
Async XLA Ops:
  14.9 9.5 %collective-permute-start.5 = (bf16[8,16,768]{2,1,0:T(8,128)(2,1)S(1)}, bf16[8,16,768]{2,1,0:T(8,128)(2,1)S(1)}, u32[]{:S(2)}, u32[]{:S(2)}) collective-permute-start(bf16[8,16,768]{2,1,0:T(8,128)(2,1)S(1)} %pad_maximum_fusion), channel_id=1, source_target_pairs={{0,6},{1,7},{2,4},{3,5},{4,2},{5,3},{6,0},{7,1},{8,14},{9,15},{10,... | collective-permute-start | bytes 589832 | tf_op jit(solution)/shard_map/ppermute | solution.py:24
  16.7 7.6 %collective-permute-start.4 = (bf16[8,16,768]{2,1,0:T(8,128)(2,1)S(1)}, bf16[8,16,768]{2,1,0:T(8,128)(2,1)S(1)}, u32[]{:S(2)}, u32[]{:S(2)}) collective-permute-start(bf16[8,16,768]{2,1,0:T(8,128)(2,1)S(1)} %pad_maximum_fusion), channel_id=1, source_target_pairs={{0,4},{1,5},{2,6},{3,7},{4,0},{5,1},{6,2},{7,3},{8,12},{9,13},{10,... | collective-permute-start | bytes 589832 | tf_op jit(solution)/shard_map/ppermute | solution.py:24
  17.4 15.2 %collective-permute-start.9 = (bf16[8,16,768]{2,1,0:T(8,128)(2,1)S(1)}, bf16[8,16,768]{2,1,0:T(8,128)(2,1)S(1)}, u32[]{:S(2)}, u32[]{:S(2)}) collective-permute-start(bf16[8,16,768]{2,1,0:T(8,128)(2,1)S(1)} %collective-permute-done.6), channel_id=1, source_target_pairs={{0,6},{1,7},{2,4},{3,5},{4,2},{5,3},{6,0},{7,1},{8,14},{9,15},{10,... | collective-permute-start | bytes 589832 | tf_op jit(solution)/shard_map/ppermute | solution.py:24
  19.5 12.6 %collective-permute-start.8 = (bf16[8,16,768]{2,1,0:T(8,128)(2,1)S(1)}, bf16[8,16,768]{2,1,0:T(8,128)(2,1)S(1)}, u32[]{:S(2)}, u32[]{:S(2)}) collective-permute-start(bf16[8,16,768]{2,1,0:T(8,128)(2,1)S(1)} %collective-permute-done.6), channel_id=1, source_target_pairs={{0,4},{1,5},{2,6},{3,7},{4,0},{5,1},{6,2},{7,3},{8,12},{9,13},{10,... | collective-permute-start | bytes 589832 | tf_op jit(solution)/shard_map/ppermute | solution.py:24
  20.1 12.0 %collective-permute-start.7 = (bf16[8,16,768]{2,1,0:T(8,128)(2,1)S(1)}, bf16[8,16,768]{2,1,0:T(8,128)(2,1)S(1)}, u32[]{:S(2)}, u32[]{:S(2)}) collective-permute-start(bf16[8,16,768]{2,1,0:T(8,128)(2,1)S(1)} %collective-permute-done.6), channel_id=1, source_target_pairs={{0,2},{1,3},{2,0},{3,1},{4,6},{5,7},{6,4},{7,5},{8,10},{9,11},{10,... | collective-permute-start | bytes 589832 | tf_op jit(solution)/shard_map/ppermute | solution.py:24
  32.6 37.7 %collective-permute-start.10 = (bf16[8,8,16,768]{3,2,1,0:T(8,128)(2,1)S(1)}, bf16[8,8,16,768]{3,2,1,0:T(8,128)(2,1)S(1)}, u32[]{:S(2)}, u32[]{:S(2)}) collective-permute-start(bf16[8,8,16,768]{3,2,1,0:T(8,128)(2,1)S(1)} %bitcast_dynamic-update-slice_fusion.8.g_ref), channel_id=1, source_target_pairs={{0,1},{1,0},{2,3},{3,2},{4,5},{5,4},{6,7},{7,6},{8,9},{9,8},{10,11... | collective-permute-start | bytes 4718600 | tf_op jit(solution)/shard_map/ppermute | solution.py:24
  36.2 12.1 %collective-permute-start.19 = (bf16[256,768]{1,0:T(8,128)(2,1)S(1)}, bf16[256,768]{1,0:T(8,128)(2,1)S(1)}, u32[]{:S(2)}, u32[]{:S(2)}) collective-permute-start(bf16[256,768]{1,0:T(8,128)(2,1)S(1)} %copy-done.3), channel_id=1, source_target_pairs={{0,64},{16,80},{32,96},{48,112},{64,0},{80,16},{96,32},{112,48},{1... | collective-permute-start | bytes 1179656 | tf_op jit(solution)/shard_map/ppermute | solution.py:24
  38.1 17.4 %collective-permute-start.17 = (bf16[256,768]{1,0:T(8,128)(2,1)S(1)}, bf16[256,768]{1,0:T(8,128)(2,1)S(1)}, u32[]{:S(2)}, u32[]{:S(2)}) collective-permute-start(bf16[256,768]{1,0:T(8,128)(2,1)S(1)} %copy-done.3), channel_id=1, source_target_pairs={{0,32},{16,48},{32,0},{48,16},{64,96},{80,112},{96,64},{112,80},{1... | collective-permute-start | bytes 1179656 | tf_op jit(solution)/shard_map/ppermute | solution.py:24
  38.1 20.0 %collective-permute-start.21 = (bf16[256,768]{1,0:T(8,128)(2,1)S(1)}, bf16[256,768]{1,0:T(8,128)(2,1)S(1)}, u32[]{:S(2)}, u32[]{:S(2)}) collective-permute-start(bf16[256,768]{1,0:T(8,128)(2,1)S(1)} %copy-done.3), channel_id=1, source_target_pairs={{0,96},{16,112},{32,64},{48,80},{64,32},{80,48},{96,0},{112,16},{1... | collective-permute-start | bytes 1179656 | tf_op jit(solution)/shard_map/ppermute | solution.py:24
  39.5 20.3 %collective-permute-start.12 = (bf16[384,768]{1,0:T(8,128)(2,1)S(1)}, bf16[384,768]{1,0:T(8,128)(2,1)S(1)}, u32[]{:S(2)}, u32[]{:S(2)}) collective-permute-start(bf16[384,768]{1,0:T(8,128)(2,1)S(1)} %get-tuple-element.69), channel_id=1, source_target_pairs={{0,16},{16,0},{32,48},{48,32},{64,80},{80,64},{96,112},{112,96},{1... | collective-permute-start | bytes 1769480 | tf_op jit(solution)/shard_map/ppermute | solution.py:24
  48.3 19.4 %collective-permute-start.11 = (bf16[384,768]{1,0:T(8,128)(2,1)S(1)}, bf16[384,768]{1,0:T(8,128)(2,1)S(1)}, u32[]{:S(2)}, u32[]{:S(2)}) collective-permute-start(bf16[384,768]{1,0:T(8,128)(2,1)S(1)} %get-tuple-element.70), channel_id=1, source_target_pairs={{0,16},{16,0},{32,48},{48,32},{64,80},{80,64},{96,112},{112,96},{1... | collective-permute-start | bytes 1769480 | tf_op jit(solution)/shard_map/ppermute | solution.py:24
  55.5 20.6 %collective-permute-start.16 = (bf16[256,768]{1,0:T(8,128)(2,1)S(1)}, bf16[256,768]{1,0:T(8,128)(2,1)S(1)}, u32[]{:S(2)}, u32[]{:S(2)}) collective-permute-start(bf16[256,768]{1,0:T(8,128)(2,1)S(1)} %copy-done.3), channel_id=1, source_target_pairs={{0,16},{16,0},{32,48},{48,32},{64,80},{80,64},{96,112},{112,96},{1... | collective-permute-start | bytes 1179656 | tf_op jit(solution)/shard_map/ppermute | solution.py:24
  58.2 26.4 %collective-permute-start.20 = (bf16[256,768]{1,0:T(8,128)(2,1)S(1)}, bf16[256,768]{1,0:T(8,128)(2,1)S(1)}, u32[]{:S(2)}, u32[]{:S(2)}) collective-permute-start(bf16[256,768]{1,0:T(8,128)(2,1)S(1)} %collective-permute-done.19.rest_4_), channel_id=1, source_target_pairs={{0,16},{16,0},{32,48},{48,32},{64,80},{80,64},{96,112},{112,96},{1... | collective-permute-start | bytes 1179656 | tf_op jit(solution)/shard_map/ppermute | solution.py:24
  59.8 33.2 %collective-permute-start.18 = (bf16[256,768]{1,0:T(8,128)(2,1)S(1)}, bf16[256,768]{1,0:T(8,128)(2,1)S(1)}, u32[]{:S(2)}, u32[]{:S(2)}) collective-permute-start(bf16[256,768]{1,0:T(8,128)(2,1)S(1)} %collective-permute-done.17.rest_2_), channel_id=1, source_target_pairs={{0,16},{16,0},{32,48},{48,32},{64,80},{80,64},{96,112},{112,96},{1... | collective-permute-start | bytes 1179656 | tf_op jit(solution)/shard_map/ppermute | solution.py:24
  67.7 33.7 %collective-permute-start.22 = (bf16[256,768]{1,0:T(8,128)(2,1)S(1)}, bf16[256,768]{1,0:T(8,128)(2,1)S(1)}, u32[]{:S(2)}, u32[]{:S(2)}) collective-permute-start(bf16[256,768]{1,0:T(8,128)(2,1)S(1)} %collective-permute-done.21.rest_6_), channel_id=1, source_target_pairs={{0,16},{16,0},{32,48},{48,32},{64,80},{80,64},{96,112},{112,96},{1... | collective-permute-start | bytes 1179656 | tf_op jit(solution)/shard_map/ppermute | solution.py:24
  73.3 28.1 %collective-permute-start.13 = (bf16[256,768]{1,0:T(8,128)(2,1)S(1)}, bf16[256,768]{1,0:T(8,128)(2,1)S(1)}, u32[]{:S(2)}, u32[]{:S(2)}) collective-permute-start(bf16[256,768]{1,0:T(8,128)(2,1)S(1)} %get-tuple-element.38), channel_id=1, source_target_pairs={{0,32},{16,48},{32,0},{48,16},{64,96},{80,112},{96,64},{112,80},{1... | collective-permute-start | bytes 1179656 | tf_op jit(solution)/shard_map/ppermute | solution.py:24
  76.1 25.3 %collective-permute-start.14 = (bf16[256,768]{1,0:T(8,128)(2,1)S(1)}, bf16[256,768]{1,0:T(8,128)(2,1)S(1)}, u32[]{:S(2)}, u32[]{:S(2)}) collective-permute-start(bf16[256,768]{1,0:T(8,128)(2,1)S(1)} %get-tuple-element.39), channel_id=1, source_target_pairs={{0,64},{16,80},{32,96},{48,112},{64,0},{80,16},{96,32},{112,48},{1... | collective-permute-start | bytes 1179656 | tf_op jit(solution)/shard_map/ppermute | solution.py:24
  84.5 17.1 %collective-permute-start.15 = (bf16[256,768]{1,0:T(8,128)(2,1)S(1)}, bf16[256,768]{1,0:T(8,128)(2,1)S(1)}, u32[]{:S(2)}, u32[]{:S(2)}) collective-permute-start(bf16[256,768]{1,0:T(8,128)(2,1)S(1)} %get-tuple-element.40), channel_id=1, source_target_pairs={{0,96},{16,112},{32,64},{48,80},{64,32},{80,48},{96,0},{112,16},{1... | collective-permute-start | bytes 1179656 | tf_op jit(solution)/shard_map/ppermute | solution.py:24
  109.5 7.1 %collective-permute-start.27 = (bf16[16,6144]{1,0:T(8,128)(2,1)S(1)}, bf16[16,6144]{1,0:T(8,128)(2,1)S(1)}, u32[]{:S(2)}, u32[]{:S(2)}) collective-permute-start(bf16[16,6144]{1,0:T(8,128)(2,1)S(1)} %get-tuple-element.48), channel_id=1, source_target_pairs={{0,6},{1,7},{2,4},{3,5},{4,2},{5,3},{6,0},{7,1},{8,14},{9,15},{10,... | collective-permute-start | bytes 589832 | tf_op jit(solution)/shard_map/ppermute | solution.py:24
  111.5 8.2 %collective-permute-start.24 = (bf16[16,6144]{1,0:T(8,128)(2,1)S(1)}, bf16[16,6144]{1,0:T(8,128)(2,1)S(1)}, u32[]{:S(2)}, u32[]{:S(2)}) collective-permute-start(bf16[16,6144]{1,0:T(8,128)(2,1)S(1)} %get-tuple-element.44), channel_id=1, source_target_pairs={{0,2},{1,3},{2,0},{3,1},{4,6},{5,7},{6,4},{7,5},{8,10},{9,11},{10,... | collective-permute-start | bytes 589832 | tf_op jit(solution)/shard_map/ppermute | solution.py:24
  112.3 8.5 %collective-permute-start.25 = (bf16[16,6144]{1,0:T(8,128)(2,1)S(1)}, bf16[16,6144]{1,0:T(8,128)(2,1)S(1)}, u32[]{:S(2)}, u32[]{:S(2)}) collective-permute-start(bf16[16,6144]{1,0:T(8,128)(2,1)S(1)} %get-tuple-element.45), channel_id=1, source_target_pairs={{0,6},{1,7},{2,4},{3,5},{4,2},{5,3},{6,0},{7,1},{8,14},{9,15},{10,... | collective-permute-start | bytes 589832 | tf_op jit(solution)/shard_map/ppermute | solution.py:24
  125.3 8.8 %collective-permute-start.33 = (bf16[16,6144]{1,0:T(8,128)(2,1)S(1)}, bf16[16,6144]{1,0:T(8,128)(2,1)S(1)}, u32[]{:S(2)}, u32[]{:S(2)}) collective-permute-start(bf16[16,6144]{1,0:T(8,128)(2,1)S(1)} %shard_map.115), channel_id=1, source_target_pairs={{0,6},{1,7},{2,4},{3,5},{4,2},{5,3},{6,0},{7,1},{8,14},{9,15},{10,... | collective-permute-start | bytes 589832 | tf_op jit(solution)/shard_map/ppermute | solution.py:24
  129.4 9.8 %collective-permute-start.37 = (bf16[16,6144]{1,0:T(8,128)(2,1)S(1)}, bf16[16,6144]{1,0:T(8,128)(2,1)S(1)}, u32[]{:S(2)}, u32[]{:S(2)}) collective-permute-start(bf16[16,6144]{1,0:T(8,128)(2,1)S(1)} %collective-permute-done.34), channel_id=1, source_target_pairs={{0,6},{1,7},{2,4},{3,5},{4,2},{5,3},{6,0},{7,1},{8,14},{9,15},{10,... | collective-permute-start | bytes 589832 | tf_op jit(solution)/shard_map/ppermute | solution.py:24
  130.7 6.9 %collective-permute-start.35 = (bf16[16,6144]{1,0:T(8,128)(2,1)S(1)}, bf16[16,6144]{1,0:T(8,128)(2,1)S(1)}, u32[]{:S(2)}, u32[]{:S(2)}) collective-permute-start(bf16[16,6144]{1,0:T(8,128)(2,1)S(1)} %collective-permute-done.34), channel_id=1, source_target_pairs={{0,2},{1,3},{2,0},{3,1},{4,6},{5,7},{6,4},{7,5},{8,10},{9,11},{10,... | collective-permute-start | bytes 589832 | tf_op jit(solution)/shard_map/ppermute | solution.py:24
  139.2 19.8 %collective-permute-start.38 = (bf16[8,16,6144]{2,1,0:T(8,128)(2,1)S(1)}, bf16[8,16,6144]{2,1,0:T(8,128)(2,1)}, u32[]{:S(2)}, u32[]{:S(2)}) collective-permute-start(bf16[8,16,6144]{2,1,0:T(8,128)(2,1)S(1)} %bitcast_dynamic-update-slice_fusion.g_ref), channel_id=1, source_target_pairs={{0,1},{1,0},{2,3},{3,2},{4,5},{5,4},{6,7},{7,6},{8,9},{9,8},{10,11... | collective-permute-start | bytes 4718600 | tf_op jit(solution)/shard_map/ppermute | solution.py:24
  165.9 11.1 %collective-permute-start.40 = (bf16[2,16,3072]{2,1,0:T(8,128)(2,1)S(1)}, bf16[2,16,3072]{2,1,0:T(8,128)(2,1)S(1)}, u32[]{:S(2)}, u32[]{:S(2)}) collective-permute-start(bf16[2,16,3072]{2,1,0:T(8,128)(2,1)S(1)} %get-tuple-element.55), channel_id=1, source_target_pairs={{0,4},{1,5},{2,6},{3,7},{4,0},{5,1},{6,2},{7,3},{8,12},{9,13},{10,... | collective-permute-start | bytes 589832 | tf_op jit(solution)/shard_map/ppermute | solution.py:24
  167.8 11.3 %collective-permute-start.41 = (bf16[2,16,3072]{2,1,0:T(8,128)(2,1)S(1)}, bf16[2,16,3072]{2,1,0:T(8,128)(2,1)S(1)}, u32[]{:S(2)}, u32[]{:S(2)}) collective-permute-start(bf16[2,16,3072]{2,1,0:T(8,128)(2,1)S(1)} %get-tuple-element.56), channel_id=1, source_target_pairs={{0,6},{1,7},{2,4},{3,5},{4,2},{5,3},{6,0},{7,1},{8,14},{9,15},{10,... | collective-permute-start | bytes 589832 | tf_op jit(solution)/shard_map/ppermute | solution.py:24
  169.8 9.3 %collective-permute-start.42 = (bf16[2,16,3072]{2,1,0:T(8,128)(2,1)S(1)}, bf16[2,16,3072]{2,1,0:T(8,128)(2,1)S(1)}, u32[]{:S(2)}, u32[]{:S(2)}) collective-permute-start(bf16[2,16,3072]{2,1,0:T(8,128)(2,1)S(1)} %get-tuple-element.57), channel_id=1, source_target_pairs={{0,8},{1,9},{2,10},{3,11},{4,12},{5,13},{6,14},{7,15},{8,0},{9,1},... | collective-permute-start | bytes 589832 | tf_op jit(solution)/shard_map/ppermute | solution.py:24
  170.1 10.8 %collective-permute-start.43 = (bf16[2,16,3072]{2,1,0:T(8,128)(2,1)S(1)}, bf16[2,16,3072]{2,1,0:T(8,128)(2,1)S(1)}, u32[]{:S(2)}, u32[]{:S(2)}) collective-permute-start(bf16[2,16,3072]{2,1,0:T(8,128)(2,1)S(1)} %get-tuple-element.58), channel_id=1, source_target_pairs={{0,10},{1,11},{2,8},{3,9},{4,14},{5,15},{6,12},{7,13},{8,2},{9,3},... | collective-permute-start | bytes 589832 | tf_op jit(solution)/shard_map/ppermute | solution.py:24
  172.3 13.4 %collective-permute-start.44 = (bf16[2,16,3072]{2,1,0:T(8,128)(2,1)S(1)}, bf16[2,16,3072]{2,1,0:T(8,128)(2,1)S(1)}, u32[]{:S(2)}, u32[]{:S(2)}) collective-permute-start(bf16[2,16,3072]{2,1,0:T(8,128)(2,1)S(1)} %get-tuple-element.59), channel_id=1, source_target_pairs={{0,12},{1,13},{2,14},{3,15},{4,8},{5,9},{6,10},{7,11},{8,4},{9,5},... | collective-permute-start | bytes 589832 | tf_op jit(solution)/shard_map/ppermute | solution.py:24
  177.0 12.7 %collective-permute-start.45 = (bf16[2,16,3072]{2,1,0:T(8,128)(2,1)S(1)}, bf16[2,16,3072]{2,1,0:T(8,128)(2,1)S(1)}, u32[]{:S(2)}, u32[]{:S(2)}) collective-permute-start(bf16[2,16,3072]{2,1,0:T(8,128)(2,1)S(1)} %get-tuple-element.60), channel_id=1, source_target_pairs={{0,14},{1,15},{2,12},{3,13},{4,10},{5,11},{6,8},{7,9},{8,6},{9,7},... | collective-permute-start | bytes 589832 | tf_op jit(solution)/shard_map/ppermute | solution.py:24
  195.2 8.4 %collective-permute-start.48 = (bf16[2,16,1024]{2,1,0:T(8,128)(2,1)S(1)}, bf16[2,16,1024]{2,1,0:T(8,128)(2,1)S(1)}, u32[]{:S(2)}, u32[]{:S(2)}) collective-permute-start(bf16[2,16,1024]{2,1,0:T(8,128)(2,1)S(1)} %get-tuple-element.63), channel_id=1, source_target_pairs={{0,4},{1,5},{2,6},{3,7},{4,0},{5,1},{6,2},{7,3},{8,12},{9,13},{10,... | collective-permute-start | bytes 196616 | tf_op jit(solution)/shard_map/ppermute | solution.py:24
  (31 other events, 236.3 us)

commit v2 on v1

--- a/solution.py
+++ b/solution.py
@@ -1,3 +1,4 @@
+import functools
 import math
 
 import jax
@@ -51,18 +52,14 @@
         o_ref[ids[0] ^ b] = y[:, b * width:(b + 1) * width]
 
 
-def qkv_kernel(g_ref, h_ref, w0_ref, w1_ref, w2_ref, *outs):
+def qkv_kernel(src, w0_ref, w1_ref, *outs):
     width = w0_ref.shape[0]
-    half = width // 2
     for d, o_ref in enumerate(outs):
-        for kk, src in enumerate((g_ref, h_ref)):
-            a = src[:, 2 * d].reshape(-1, width)
-            b = src[:, 2 * d + 1].reshape(-1, width)
-            acc = jnp.dot(a, w0_ref[...], preferred_element_type=F32)
-            acc = acc + jnp.dot(b[:, :half], w1_ref[...], preferred_element_type=F32)
-            acc = acc + jnp.dot(b[:, half:], w2_ref[...], preferred_element_type=F32)
-            rows = acc.shape[0]
-            o_ref[kk * rows:(kk + 1) * rows, :] = acc.astype(o_ref.dtype)
+        a = src[:, 2 * d].reshape(-1, width)
+        b = src[:, 2 * d + 1].reshape(-1, width)
+        acc = jnp.dot(a, w0_ref[...], preferred_element_type=F32)
+        acc = acc + jnp.dot(b, w1_ref[...], preferred_element_type=F32)
+        o_ref[...] = acc.astype(o_ref.dtype)
 
 
 def place(row, section, step):
@@ -71,21 +68,22 @@
     return (section ^ (2 * (group - 8 * half) + half)) * step + (row - group * step)
 
 
-def attn_kernel(ids, own, r1, r2, r3, *rest):
+def attn_kernel(ids, a0, a1, a2, b0, b1, b2, *rest):
     wo = rest[:8]
     outs = rest[8:10]
     packed = rest[10]
     mixed = rest[11]
-    length = own.shape[0]
-    packed[...] = (
-        own[...] + r1[...].astype(F32) + r2[...].astype(F32) + r3[...].astype(F32)
-    ).astype(BF)
+    length, width = packed.shape
+    half = length // 2
+    for at, trio in ((0, (a0, a1, a2)), (half, (b0, b1, b2))):
+        part = trio[0][...] + trio[1][...].astype(F32) + trio[2][...].astype(F32)
+        packed[at:at + half, :] = part.astype(BF)
     section = ids[1]
     valid = ids[2]
     rows = place(lax.broadcasted_iota(jnp.int32, (length, 1), 0), section, 16)
     cols = place(lax.broadcasted_iota(jnp.int32, (1, length), 1), section, 16)
     allowed = (cols <= rows) & (cols < valid)
-    for h in range(own.shape[1] // (3 * HEAD)):
+    for h in range(width // (3 * HEAD)):
         base = h * 3 * HEAD
         q = packed[:, base:base + HEAD]
         k = packed[:, base + HEAD:base + 2 * HEAD]
@@ -98,7 +96,6 @@
         mixed[:, h * HEAD:(h + 1) * HEAD] = jnp.dot(
             p, v, preferred_element_type=F32
         ).astype(BF)
-    half = length // 2
     width = wo[0].shape[1]
     for e in range(8):
         acc = jnp.dot(mixed[...], wo[e][...], preferred_element_type=F32).astype(BF)
@@ -138,13 +135,10 @@
         o_ref[:, cut] = (acc[b] * scale * gain[:, cut]).astype(BF)
 
 
-def lift_kernel(g_ref, h_ref, din, emb, gain, wqkv, *outs):
-    width = g_ref.shape[2]
-    parts = []
-    for src in (g_ref, h_ref):
-        parts.append(src[...].reshape(-1, width))
-    x = jnp.concatenate(parts, axis=0)
-    lifted = jnp.dot(x, din[...], preferred_element_type=F32) + emb[...].astype(F32)
+def lift_kernel(row, src, din, emb, gain, wqkv, *outs):
+    x = src[...].reshape(-1, src.shape[2])
+    near = emb[row:row + x.shape[0], :].astype(F32)
+    lifted = jnp.dot(x, din[...], preferred_element_type=F32) + near
     scale = lax.rsqrt(jnp.mean(lifted * lifted, axis=-1, keepdims=True) + EPS)
     dn = (lifted * scale * gain[...]).astype(BF)
     step = 1024
@@ -152,41 +146,47 @@
         cut = slice(s * step, (s + 1) * step)
         y = jnp.dot(dn, wqkv[:, cut], preferred_element_type=F32).astype(BF)
         for e in range(8):
-            outs[e][0, :, cut] = y[e * 16:(e + 1) * 16]
-            outs[e][1, :, cut] = y[128 + e * 16:128 + (e + 1) * 16]
-
-
-def fetch_kernel(*refs):
-    sems = refs[-1]
-    half = (len(refs) - 1) // 2
+            if len(outs) == 8:
+                outs[e][:, cut] = y[e * 16:(e + 1) * 16]
+            else:
+                outs[0][e, :, cut] = y[e * 16:(e + 1) * 16]
+
+
+def fetch_kernel(picks, din, dqkv, table, din_o, dqkv_o, rows_o, near, sems):
+    moves = ((table, near), (din, din_o), (dqkv, dqkv_o))
     copies = [
-        pltpu.make_async_copy(refs[i], refs[half + i], sems.at[i]) for i in range(half)
+        pltpu.make_async_copy(src, dst, sems.at[i]) for i, (src, dst) in enumerate(moves)
     ]
     for copy in copies:
         copy.start()
-    for copy in copies:
-        copy.wait()
-
-
-def fetch(*arrays):
+    copies[0].wait()
+    count = near.shape[0]
+    lane = lax.broadcasted_iota(jnp.int32, (picks.shape[0], count), 1)
+    hot = jnp.where(lane == picks[...], 1.0, 0.0).astype(BF)
+    rows_o[...] = jnp.dot(hot, near[...], preferred_element_type=F32).astype(BF)
+    copies[1].wait()
+    copies[2].wait()
+
+
+def fetch(picks, din, dqkv, table):
+    far = pl.BlockSpec(memory_space=pltpu.HBM)
+    shapes = [din.shape, dqkv.shape, (picks.shape[0], table.shape[1])]
+    big = [pltpu.with_memory_space_constraint(a, pltpu.HBM) for a in (din, dqkv, table)]
     return pl.pallas_call(
         fetch_kernel,
-        out_shape=[pltpu.VMEM(a.shape, a.dtype) for a in arrays],
-        in_specs=[pl.BlockSpec(memory_space=pltpu.HBM)] * len(arrays),
-        out_specs=[VM] * len(arrays),
-        scratch_shapes=[pltpu.SemaphoreType.DMA((len(arrays),))],
-        compiler_params=pltpu.CompilerParams(vmem_limit_bytes=1 << 20),
-    )(*[pltpu.with_memory_space_constraint(a, pltpu.HBM) for a in arrays])
+        out_shape=[pltpu.VMEM(s, BF) for s in shapes],
+        in_specs=[VM, far, far, far],
+        out_specs=[VM] * 3,
+        scratch_shapes=[pltpu.VMEM(table.shape, BF), pltpu.SemaphoreType.DMA((3,))],
+        compiler_params=pltpu.CompilerParams(vmem_limit_bytes=14 << 20),
+    )(pltpu.with_memory_space_constraint(picks, pltpu.VMEM), *big)
 
 
 def depth_kernel(ids, *rest):
-    pieces = rest[:8]
-    other = rest[8]
-    outs = rest[9:17]
-    z = rest[17]
-    for e in range(8):
-        z[e * 16:(e + 1) * 16, :] = pieces[e][0]
-        z[128 + e * 16:128 + (e + 1) * 16, :] = other[e]
+    outs = rest[16:24]
+    z = rest[24]
+    for m in range(16):
+        z[m * 16:(m + 1) * 16, :] = rest[m][...]
     section = ids[1]
     rows = lax.broadcasted_iota(jnp.int32, (256, 1), 0)
     cols = lax.broadcasted_iota(jnp.int32, (1, 256), 1)
@@ -268,28 +268,37 @@
     rel = call(norm_kernel, [((8, 16, block), BF)], smem=1, n_in=3)(
         ids, mine, t_gain[None]
     )[0]
-    rows = w_qkv.shape[0] // 2
-    w_other0 = fs(w_qkv[:rows], 1)
-    w_other1 = fs(w_qkv[rows:], 1)
+    near = fs(w_out, 1)
+    w_other = fs(w_qkv, 1)
     local = [rel[0:2]] + [fs(rel[2 * d:2 * d + 2], 2 * d) for d in (1, 2, 3)]
     local = jnp.concatenate(local, axis=0)
     wo_even = [w_out] + [fs(w_out, 2 * d) for d in (1, 2, 3)]
-    wo_odd = [fs(w, 1) for w in wo_even]
+    wo_odd = [near] + [fs(w, 1) for w in wo_even[1:]]
     wo = [w for pair in zip(wo_even, wo_odd) for w in pair]
     even = jnp.stack(gather(local, True))
     odd = cb(even, 1)
     cols = w_qkv.shape[1]
-    parts = call(
-        qkv_kernel, [((256, cols), F32)] + [((256, cols), BF)] * 3, n_in=5
-    )(even, odd, w_qkv, w_other0, w_other1)
-    sums = [fs(parts[d], 2 * d) for d in (1, 2, 3)]
+
+    def project(src, kinds):
+        return call(qkv_kernel, [((128, cols), k) for k in kinds], n_in=3)(
+            src, w_qkv, w_other
+        )
+
+    a0, a1, a2, a3 = project(even, (F32, BF, BF, F32))
+    relay_a = fs(a2, 2)
+    plain_a = fs(a1, 2)
+    b0, b1, b2, b3 = project(odd, (F32, F32, BF, BF))
+    relay_b = fs(b2, 6)
+    plain_b = fs(b3, 6)
+    sum_a = fs(add(a3, relay_a), 6)
+    sum_b = fs(add(b1, relay_b), 2)
     keep, give = call(
         attn_kernel,
         [((128, model), BF)] * 2,
         scratch=[pltpu.VMEM((256, cols), BF), pltpu.VMEM((256, w_out.shape[0]), BF)],
         smem=1,
-        n_in=13,
-    )(ids, parts[0], *sums, *wo)
+        n_in=15,
+    )(ids, a0, plain_a, sum_a, b0, plain_b, sum_b, *wo)
     taken = cb(give, 1)
     blocks = call(pair_kernel, [((16, model), F32)] + [((16, model), BF)] * 7, n_in=2)(
         keep, taken
@@ -311,22 +320,30 @@
     odd = cb(even, 1)
 
     order = jnp.concatenate([2 * jnp.arange(8), 2 * jnp.arange(8) + 1]).astype(jnp.int32)
-    ids_rel = tokens[0, 0].reshape(16, 16).at[c ^ order].get(mode="promise_in_bounds")
-    emb = d_embed[0].at[ids_rel.reshape(256)].get(mode="promise_in_bounds")
-    din, dqkv = fetch(d_in[0], d_qkv[0])
+    mine_at = (jnp.arange(16, dtype=jnp.int32)[None, :] == (c ^ order)[:, None])[:, :, None]
+    picks = jnp.sum(jnp.where(mine_at, tokens[0, 0].reshape(1, 16, 16), 0), axis=1)
+    din, dqkv, emb = fetch(picks.reshape(256, 1), d_in[0], d_qkv[0], d_embed[0])
     inner = d_in.shape[2]
-    sent = call(lift_kernel, [((2, 16, 3 * inner), BF)] * 8, n_in=6)(
-        even, odd, din, emb, d_gain, dqkv
-    )
-    pieces = [sent[0]] + [cb(sent[e], 2 * e) for e in range(1, 8)]
-    other = cb(jnp.stack([p[1] for p in pieces]), 1)
+
+    def lift(src, row, outs):
+        return call(functools.partial(lift_kernel, row), outs, n_in=5, limit=12)(
+            src, din, emb, d_gain, dqkv
+        )
+
+    low = lift(even, 0, [((16, 3 * inner), BF)] * 8)
+    high = lift(odd, 128, [((8, 16, 3 * inner), BF)])[0]
+    high = cb(high, 1)
+    got = {e: cb(low[e], 2 * e) for e in (1, 2, 3)}
+    got.update({e: cb(low[e], 2 * e) for e in (4, 5, 6, 7)})
+    deep = [high[0]] + [cb(high[e], 2 * e) for e in range(1, 8)]
+    pieces = [low[0]] + [got[e] for e in range(1, 8)] + deep
     outs = call(
         depth_kernel,
         [((2, 16, inner), BF)] * 8,
         scratch=[pltpu.VMEM((256, 3 * inner), BF)],
         smem=1,
-        n_in=10,
-    )(ids, *pieces, other)
+        n_in=17,
+    )(ids, *pieces)
     pieces = [outs[0]] + [cb(outs[e], 2 * e) for e in range(1, 8)]
     other = cb(jnp.stack([p[1] for p in pieces]), 1)
     out = call(final_kernel, [((16, 16, inner), BF)], smem=1, n_in=10, last=True)(

time: 215 us -> 211 us (0.981)
  starting transfers between devices: 79.9 us -> 87.4 us
  waiting for transfers between devices: 100 us -> 93.4 us
  local copies, waits for them, and re-layouts: 7.68 us -> 2.78 us
    ppermute x55 -> x64, starting transfers between devices: 79.9 us -> 87.4 us  [swap(): return lax.ppermute(value, axis, [(i, i ^ flip) for i in range(size)])]
    ppermute x55 -> x64, waiting for transfers between devices: 100 us -> 93.4 us  [swap(): return lax.ppermute(value, axis, [(i, i ^ flip) for i in range(size)])]
    gather x2 -> x0, local copies, waits for them, and re-layouts: 4.85 us -> none  [the longest x1 4.29 us: work(): emb = d_embed[0].at[ids_rel.reshape(256)].get(mode='promise_in_bounds')]
    pallas_call x10 -> x14, Pallas kernels: 18.3 us -> 17.3 us  [go(): return run(*args[:smem], *near)]
  transfers between devices with their start and end apart: 55 -> 64, of which waited for: 35 -> 28; matrix products, arithmetic and copies ran while one was open for 3% -> 1% of each run, Pallas kernels for 4% -> 6%
where the time goes in v2:
time: 211 us
  waiting for transfers between devices  93.4 us (44%)
  starting transfers between devices  87.4 us (41%)
  Pallas kernels  25 us (12%)
  local copies, waits for them, and re-layouts  2.78 us (1%)
    ppermute x64, waiting for transfers between devices, swap(): return lax.ppermute(value, axis, [(i, i ^ flip) for i in range(size)])  93.4 us
    ppermute x64, starting transfers between devices, swap(): return lax.ppermute(value, axis, [(i, i ^ flip) for i in range(size)])  87.4 us
    pallas_call x14, Pallas kernels, go(): return run(*args[:smem], *near)  17.3 us
    pallas_call x1, Pallas kernels, fetch(): pl.pallas_call(fetch_kernel, out_shape=[pltpu.VMEM(s, BF) for s in shapes...  7.67 us
  transfers between devices with their start and end apart: 64, of which 28 were waited for; matrix products, arithmetic and copies ran while one was open for 1% of the time, Pallas kernels for 6%

profile of v2, /device:TPU:1, one launch (start us, length us, event | category | flops | bytes accessed | tf_op | source)
XLA Modules:
  0.0 210.8 jit_solution(9118988764373426457)
XLA Ops:
  3.2 4.7 %collective-permute-start.2 = (bf16[2,16,768]{2,1,0:T(8,128)(2,1)S(1)}, bf16[2,16,768]{2,1,0:T(8,128)(2,1)S(1)}, u32[]{:S(2)}, u32[]{:S(2)}) collective-permute-start(bf16[2,16,768]{2,1,0:T(8,128)(2,1)S(1)} %get-tuple-element.88), channel_id=1, source_target_pairs={{0,96},{16,112},{32,64},{48,80},{64,32},{80,48},{96,0},{112,16},{1... | collective-permute-start | bytes 147464 | tf_op jit(solution)/shard_map/ppermute | solution.py:25
  9.3 3.0 %collective-permute-done.1 = bf16[2,16,768]{2,1,0:T(8,128)(2,1)S(1)} collective-permute-done((bf16[2,16,768]{2,1,0:T(8,128)(2,1)S(1)}, bf16[2,16,768]{2,1,0:T(8,128)(2,1)S(1)}, u32[]{:S(2)}, u32[]{:S(2)}) %collective-permute-start.1) | collective-permute-done | bytes 49184 | tf_op jit(solution)/shard_map/ppermute | solution.py:25
  20.7 3.6 %collective-permute-done.4 = bf16[8,16,768]{2,1,0:T(8,128)(2,1)S(1)} collective-permute-done((bf16[8,16,768]{2,1,0:T(8,128)(2,1)S(1)}, bf16[8,16,768]{2,1,0:T(8,128)(2,1)S(1)}, u32[]{:S(2)}, u32[]{:S(2)}) %collective-permute-start.4) | collective-permute-done | bytes 196640 | tf_op jit(solution)/shard_map/ppermute | solution.py:25
  24.4 7.7 %collective-permute-done.7 = bf16[8,16,768]{2,1,0:T(8,128)(2,1)S(1)} collective-permute-done((bf16[8,16,768]{2,1,0:T(8,128)(2,1)S(1)}, bf16[8,16,768]{2,1,0:T(8,128)(2,1)S(1)}, u32[]{:S(2)}, u32[]{:S(2)}) %collective-permute-start.7) | collective-permute-done | bytes 196640 | tf_op jit(solution)/shard_map/ppermute | solution.py:25
  32.6 3.6 %collective-permute-start.14 = (bf16[8,8,16,768]{3,2,1,0:T(8,128)(2,1)S(1)}, bf16[8,8,16,768]{3,2,1,0:T(8,128)(2,1)S(1)}, u32[]{:S(2)}, u32[]{:S(2)}) collective-permute-start(bf16[8,8,16,768]{3,2,1,0:T(8,128)(2,1)S(1)} %bitcast_dynamic-update-slice_fusion.8.src), channel_id=1, source_target_pairs={{0,1},{1,0},{2,3},{3,2},{4,5},{5,4},{6,7},{7,6},{8,9},{9,8},{10,11... | collective-permute-start | bytes 4718600 | tf_op jit(solution)/shard_map/ppermute | solution.py:25
  36.2 2.6 %collective-permute-start.10 = (bf16[768,768]{1,0:T(8,128)(2,1)S(1)}, bf16[768,768]{1,0:T(8,128)(2,1)S(1)}, u32[]{:S(2)}, u32[]{:S(2)}) collective-permute-start(bf16[768,768]{1,0:T(8,128)(2,1)S(1)} %copy-done), channel_id=1, source_target_pairs={{0,16},{16,0},{32,48},{48,32},{64,80},{80,64},{96,112},{112,96},{1... | collective-permute-start | bytes 3538952 | tf_op jit(solution)/shard_map/ppermute | solution.py:25
  42.1 23.0 %collective-permute-done.10.w1_ref = bf16[768,768]{1,0:T(8,128)(2,1)S(1)} collective-permute-done((bf16[768,768]{1,0:T(8,128)(2,1)S(1)}, bf16[768,768]{1,0:T(8,128)(2,1)S(1)}, u32[]{:S(2)}, u32[]{:S(2)}) %collective-permute-start.10) | collective-permute-done | bytes 1179680 | tf_op jit(solution)/shard_map/ppermute | solution.py:25
  65.1 2.6 %collective-permute-start.18 = (bf16[256,768]{1,0:T(8,128)(2,1)S(1)}, bf16[256,768]{1,0:T(8,128)(2,1)S(1)}, u32[]{:S(2)}, u32[]{:S(2)}) collective-permute-start(bf16[256,768]{1,0:T(8,128)(2,1)S(1)} %copy-done.3), channel_id=1, source_target_pairs={{0,16},{16,0},{32,48},{48,32},{64,80},{80,64},{96,112},{112,96},{1... | collective-permute-start | bytes 1179656 | tf_op jit(solution)/shard_map/ppermute | solution.py:25
  69.7 2.6 %collective-permute-start.20 = (bf16[256,768]{1,0:T(8,128)(2,1)S(1)}, bf16[256,768]{1,0:T(8,128)(2,1)S(1)}, u32[]{:S(2)}, u32[]{:S(2)}) collective-permute-start(bf16[256,768]{1,0:T(8,128)(2,1)S(1)} %collective-permute-done.19.rest_2_), channel_id=1, source_target_pairs={{0,16},{16,0},{32,48},{48,32},{64,80},{80,64},{96,112},{112,96},{1... | collective-permute-start | bytes 1179656 | tf_op jit(solution)/shard_map/ppermute | solution.py:25
  76.3 3.5 %collective-permute-done.16.refs_1_ = bf16[128,768]{1,0:T(8,128)(2,1)S(1)} collective-permute-done((bf16[128,768]{1,0:T(8,128)(2,1)S(1)}, bf16[128,768]{1,0:T(8,128)(2,1)S(1)}, u32[]{:S(2)}, u32[]{:S(2)}) %collective-permute-start.16) | collective-permute-done | bytes 196640 | tf_op jit(solution)/shard_map/ppermute | solution.py:25
  82.1 2.7 %collective-permute-done.22.rest_5_ = bf16[256,768]{1,0:T(8,128)(2,1)S(1)} collective-permute-done((bf16[256,768]{1,0:T(8,128)(2,1)S(1)}, bf16[256,768]{1,0:T(8,128)(2,1)S(1)}, u32[]{:S(2)}, u32[]{:S(2)}) %collective-permute-start.22) | collective-permute-done | bytes 393248 | tf_op jit(solution)/shard_map/ppermute | solution.py:25
  86.0 7.2 %collective-permute-done.20.rest_3_ = bf16[256,768]{1,0:T(8,128)(2,1)S(1)} collective-permute-done((bf16[256,768]{1,0:T(8,128)(2,1)S(1)}, bf16[256,768]{1,0:T(8,128)(2,1)S(1)}, u32[]{:S(2)}, u32[]{:S(2)}) %collective-permute-start.20) | collective-permute-done | bytes 393248 | tf_op jit(solution)/shard_map/ppermute | solution.py:25
  93.2 8.4 %collective-permute-done.24.rest_7_ = bf16[256,768]{1,0:T(8,128)(2,1)S(1)} collective-permute-done((bf16[256,768]{1,0:T(8,128)(2,1)S(1)}, bf16[256,768]{1,0:T(8,128)(2,1)S(1)}, u32[]{:S(2)}, u32[]{:S(2)}) %collective-permute-start.24) | collective-permute-done | bytes 393248 | tf_op jit(solution)/shard_map/ppermute | solution.py:25
  101.6 2.5 %shard_map.114 = (bf16[128,6144]{1,0:T(8,128)(2,1)S(1)}, bf16[128,6144]{1,0:T(8,128)(2,1)S(1)}) custom-call(s32[3]{0:T(128)S(1)} %pad_add_fusion.ids, f32[128,768]{1,0:T(8,128)S(1)} %get-tuple-element.42.a0, bf16[128,768]{1,0:T(8,128)(2,1)S(1)} %collective-permute-done.11.a1, bf16[128,768]{1,0:T(8,128)(2,1)S(1)} %collective-permute-done.13.a2, ...), custom_call_target="tpu_custom_call" | custom-call | tf_op jit(solution)/shard_map/pallas_call | solution.py:41
  106.2 3.0 %collective-permute-done.25.b_ref = bf16[128,6144]{1,0:T(8,128)(2,1)S(1)} collective-permute-done((bf16[128,6144]{1,0:T(8,128)(2,1)S(1)}, bf16[128,6144]{1,0:T(8,128)(2,1)S(1)}, u32[]{:S(2)}, u32[]{:S(2)}) %collective-permute-start.25) | collective-permute-done | bytes 1572896 | tf_op jit(solution)/shard_map/ppermute | solution.py:25
  121.8 2.3 %collective-permute-done.32.rest_4_ = bf16[16,6144]{1,0:T(8,128)(2,1)S(1)} collective-permute-done((bf16[16,6144]{1,0:T(8,128)(2,1)S(1)}, bf16[16,6144]{1,0:T(8,128)(2,1)S(1)}, u32[]{:S(2)}, u32[]{:S(2)}) %collective-permute-start.32) | collective-permute-done | bytes 196640 | tf_op jit(solution)/shard_map/ppermute | solution.py:25
  130.9 2.7 %collective-permute-done.34 = bf16[16,6144]{1,0:T(8,128)(2,1)S(1)} collective-permute-done((bf16[16,6144]{1,0:T(8,128)(2,1)S(1)}, bf16[16,6144]{1,0:T(8,128)(2,1)S(1)}, u32[]{:S(2)}, u32[]{:S(2)}) %collective-permute-start.34) | collective-permute-done | bytes 196640 | tf_op jit(solution)/shard_map/ppermute | solution.py:25
  134.4 3.4 %collective-permute-done.37 = bf16[16,6144]{1,0:T(8,128)(2,1)S(1)} collective-permute-done((bf16[16,6144]{1,0:T(8,128)(2,1)S(1)}, bf16[16,6144]{1,0:T(8,128)(2,1)S(1)}, u32[]{:S(2)}, u32[]{:S(2)}) %collective-permute-start.37) | collective-permute-done | bytes 196640 | tf_op jit(solution)/shard_map/ppermute | solution.py:25
  139.4 7.1 %collective-permute-start.47 = (bf16[8,16,6144]{2,1,0:T(8,128)(2,1)S(1)}, bf16[8,16,6144]{2,1,0:T(8,128)(2,1)S(1)}, u32[]{:S(2)}, u32[]{:S(2)}) collective-permute-start(bf16[8,16,6144]{2,1,0:T(8,128)(2,1)S(1)} %bitcast_dynamic-update-slice_fusion.src), channel_id=1, source_target_pairs={{0,1},{1,0},{2,3},{3,2},{4,5},{5,4},{6,7},{7,6},{8,9},{9,8},{10,11... | collective-permute-start | bytes 4718600 | tf_op jit(solution)/shard_map/ppermute | solution.py:25
  148.3 7.7 %shard_map.119 = (bf16[6144,1024]{1,0:T(8,128)(2,1)S(1)}, bf16[1024,3072]{1,0:T(8,128)(2,1)S(1)}, bf16[256,1024]{1,0:T(8,128)(2,1)S(1)}) custom-call(s32[256,1]{1,0:T(8,128)S(1)} %reshape.42.picks, bf16[6144,1024]{1,0:T(8,128)(2,1)} %bitcast.61, bf16[1024,3072]{1,0:T(8,128)(2,1)} %bitcast.62, bf16[2048,1024]{1,0:T(8,128)(2,1)} %bitcast.63), custom_call_target="tpu_custom_call" | custom-call | tf_op jit(solution)/shard_map/pallas_call | solution.py:175
  156.0 3.0 %shard_map.121 = bf16[8,16,3072]{2,1,0:T(8,128)(2,1)S(1)} custom-call(bf16[8,16,6144]{2,1,0:T(8,128)(2,1)S(1)} %collective-permute-done.47.src, bf16[6144,1024]{1,0:T(8,128)(2,1)S(1)} %get-tuple-element.60.din, bf16[256,1024]{1,0:T(8,128)(2,1)S(1)} %get-tuple-element.61.emb, f32[1,1024]{1,0:T(1,128)S(1)} %copy-done.6, ...), custom_call_target="tpu_custom_call" | custom-call | tf_op jit(solution)/shard_map/pallas_call | solution.py:41
  159.1 3.0 %shard_map.120 = (bf16[16,3072]{1,0:T(8,128)(2,1)S(1)}, bf16[16,3072]{1,0:T(8,128)(2,1)S(1)}, bf16[16,3072]{1,0:T(8,128)(2,1)S(1)}, bf16[16,3072]{1,0:T(8,128)(2...) custom-call(bf16[8,16,6144]{2,1,0:T(8,128)(2,1)S(1)} %bitcast_dynami, ...), custom_call_target="tpu_custom_call" | custom-call | tf_op jit(solution)/shard_map/pallas_call | solution.py:41
  166.6 3.1 %collective-permute-start.45 = (bf16[16,3072]{1,0:T(8,128)(2,1)S(1)}, bf16[16,3072]{1,0:T(8,128)(2,1)S(1)}, u32[]{:S(2)}, u32[]{:S(2)}) collective-permute-start(bf16[16,3072]{1,0:T(8,128)(2,1)S(1)} %get-tuple-element.69), channel_id=1, source_target_pairs={{0,12},{1,13},{2,14},{3,15},{4,8},{5,9},{6,10},{7,11},{8,4},{9,5},... | collective-permute-start | bytes 294920 | tf_op jit(solution)/shard_map/ppermute | solution.py:25
  169.7 2.6 %collective-permute-start.46 = (bf16[16,3072]{1,0:T(8,128)(2,1)S(1)}, bf16[16,3072]{1,0:T(8,128)(2,1)S(1)}, u32[]{:S(2)}, u32[]{:S(2)}) collective-permute-start(bf16[16,3072]{1,0:T(8,128)(2,1)S(1)} %get-tuple-element.70), channel_id=1, source_target_pairs={{0,14},{1,15},{2,12},{3,13},{4,10},{5,11},{6,8},{7,9},{8,6},{9,7},... | collective-permute-start | bytes 294920 | tf_op jit(solution)/shard_map/ppermute | solution.py:25
  173.3 3.2 %collective-permute-start.53 = (bf16[16,3072]{1,0:T(8,128)(2,1)S(1)}, bf16[16,3072]{1,0:T(8,128)(2,1)S(1)}, u32[]{:S(2)}, u32[]{:S(2)}) collective-permute-start(bf16[16,3072]{1,0:T(8,128)(2,1)S(1)} %get-tuple-element.81), channel_id=1, source_target_pairs={{0,10},{1,11},{2,8},{3,9},{4,14},{5,15},{6,12},{7,13},{8,2},{9,3},... | collective-permute-start | bytes 294920 | tf_op jit(solution)/shard_map/ppermute | solution.py:25
  178.6 2.5 %collective-permute-done.55.rest_15_ = bf16[16,3072]{1,0:T(8,128)(2,1)S(1)} collective-permute-done((bf16[16,3072]{1,0:T(8,128)(2,1)S(1)}, bf16[16,3072]{1,0:T(8,128)(2,1)S(1)}, u32[]{:S(2)}, u32[]{:S(2)}) %collective-permute-start.55) | collective-permute-done | bytes 98336 | tf_op jit(solution)/shard_map/ppermute | solution.py:25
  181.1 5.3 %collective-permute-done.52.rest_12_ = bf16[16,3072]{1,0:T(8,128)(2,1)S(1)} collective-permute-done((bf16[16,3072]{1,0:T(8,128)(2,1)S(1)}, bf16[16,3072]{1,0:T(8,128)(2,1)S(1)}, u32[]{:S(2)}, u32[]{:S(2)}) %collective-permute-start.52) | collective-permute-done | bytes 98336 | tf_op jit(solution)/shard_map/ppermute | solution.py:25
  186.5 2.6 %shard_map.122 = (bf16[2,16,1024]{2,1,0:T(8,128)(2,1)S(1)}, bf16[2,16,1024]{2,1,0:T(8,128)(2,1)S(1)}, bf16[2,16,1024]{2,1,0:T(8,128)(2,1)S(1)}, bf16[2,16,1024]{...) custom-call(s32[3]{0:T(128)S(1)} %pad_add_fusion.ids, ...), custom_call_target="tpu_custom_call" | custom-call | tf_op jit(solution)/shard_map/pallas_call | solution.py:41
  189.3 2.4 %collective-permute-start.57 = (bf16[2,16,1024]{2,1,0:T(8,128)(2,1)S(1)}, bf16[2,16,1024]{2,1,0:T(8,128)(2,1)S(1)}, u32[]{:S(2)}, u32[]{:S(2)}) collective-permute-start(bf16[2,16,1024]{2,1,0:T(8,128)(2,1)S(1)} %get-tuple-element.73), channel_id=1, source_target_pairs={{0,4},{1,5},{2,6},{3,7},{4,0},{5,1},{6,2},{7,3},{8,12},{9,13},{10,... | collective-permute-start | bytes 196616 | tf_op jit(solution)/shard_map/ppermute | solution.py:25
  193.2 3.9 %collective-permute-start.61 = (bf16[2,16,1024]{2,1,0:T(8,128)(2,1)S(1)}, bf16[2,16,1024]{2,1,0:T(8,128)(2,1)S(1)}, u32[]{:S(2)}, u32[]{:S(2)}) collective-permute-start(bf16[2,16,1024]{2,1,0:T(8,128)(2,1)S(1)} %get-tuple-element.77), channel_id=1, source_target_pairs={{0,12},{1,13},{2,14},{3,15},{4,8},{5,9},{6,10},{7,11},{8,4},{9,5},... | collective-permute-start | bytes 196616 | tf_op jit(solution)/shard_map/ppermute | solution.py:25
  199.6 3.4 %collective-permute-done.62.rest_7_ = bf16[2,16,1024]{2,1,0:T(8,128)(2,1)S(1)} collective-permute-done((bf16[2,16,1024]{2,1,0:T(8,128)(2,1)S(1)}, bf16[2,16,1024]{2,1,0:T(8,128)(2,1)S(1)}, u32[]{:S(2)}, u32[]{:S(2)}) %collective-permute-start.62) | collective-permute-done | bytes 65568 | tf_op jit(solution)/shard_map/ppermute | solution.py:25
  202.9 5.3 %collective-permute-start.63 = (bf16[8,16,1024]{2,1,0:T(8,128)(2,1)S(1)}, bf16[8,16,1024]{2,1,0:T(8,128)(2,1)S(1)}, u32[]{:S(2)}, u32[]{:S(2)}) collective-permute-start(bf16[8,16,1024]{2,1,0:T(8,128)(2,1)S(1)} %constant_dynamic-update-slice_fusion), channel_id=1, source_target_pairs={{0,1},{1,0},{2,3},{3,2},{4,5},{5,4},{6,7},{7,6},{8,9},{9,8},{10,11... | collective-permute-start | bytes 786440 | tf_op jit(solution)/shard_map/ppermute | solution.py:25
  (163 shorter events, 65.6 us)
Async XLA Ops:
  14.9 9.5 %collective-permute-start.5 = (bf16[8,16,768]{2,1,0:T(8,128)(2,1)S(1)}, bf16[8,16,768]{2,1,0:T(8,128)(2,1)S(1)}, u32[]{:S(2)}, u32[]{:S(2)}) collective-permute-start(bf16[8,16,768]{2,1,0:T(8,128)(2,1)S(1)} %pad_maximum_fusion), channel_id=1, source_target_pairs={{0,6},{1,7},{2,4},{3,5},{4,2},{5,3},{6,0},{7,1},{8,14},{9,15},{10,... | collective-permute-start | bytes 589832 | tf_op jit(solution)/shard_map/ppermute | solution.py:25
  16.7 7.6 %collective-permute-start.4 = (bf16[8,16,768]{2,1,0:T(8,128)(2,1)S(1)}, bf16[8,16,768]{2,1,0:T(8,128)(2,1)S(1)}, u32[]{:S(2)}, u32[]{:S(2)}) collective-permute-start(bf16[8,16,768]{2,1,0:T(8,128)(2,1)S(1)} %pad_maximum_fusion), channel_id=1, source_target_pairs={{0,4},{1,5},{2,6},{3,7},{4,0},{5,1},{6,2},{7,3},{8,12},{9,13},{10,... | collective-permute-start | bytes 589832 | tf_op jit(solution)/shard_map/ppermute | solution.py:25
  17.4 15.2 %collective-permute-start.9 = (bf16[8,16,768]{2,1,0:T(8,128)(2,1)S(1)}, bf16[8,16,768]{2,1,0:T(8,128)(2,1)S(1)}, u32[]{:S(2)}, u32[]{:S(2)}) collective-permute-start(bf16[8,16,768]{2,1,0:T(8,128)(2,1)S(1)} %collective-permute-done.6), channel_id=1, source_target_pairs={{0,6},{1,7},{2,4},{3,5},{4,2},{5,3},{6,0},{7,1},{8,14},{9,15},{10,... | collective-permute-start | bytes 589832 | tf_op jit(solution)/shard_map/ppermute | solution.py:25
  19.5 12.6 %collective-permute-start.8 = (bf16[8,16,768]{2,1,0:T(8,128)(2,1)S(1)}, bf16[8,16,768]{2,1,0:T(8,128)(2,1)S(1)}, u32[]{:S(2)}, u32[]{:S(2)}) collective-permute-start(bf16[8,16,768]{2,1,0:T(8,128)(2,1)S(1)} %collective-permute-done.6), channel_id=1, source_target_pairs={{0,4},{1,5},{2,6},{3,7},{4,0},{5,1},{6,2},{7,3},{8,12},{9,13},{10,... | collective-permute-start | bytes 589832 | tf_op jit(solution)/shard_map/ppermute | solution.py:25
  20.1 12.0 %collective-permute-start.7 = (bf16[8,16,768]{2,1,0:T(8,128)(2,1)S(1)}, bf16[8,16,768]{2,1,0:T(8,128)(2,1)S(1)}, u32[]{:S(2)}, u32[]{:S(2)}) collective-permute-start(bf16[8,16,768]{2,1,0:T(8,128)(2,1)S(1)} %collective-permute-done.6), channel_id=1, source_target_pairs={{0,2},{1,3},{2,0},{3,1},{4,6},{5,7},{6,4},{7,5},{8,10},{9,11},{10,... | collective-permute-start | bytes 589832 | tf_op jit(solution)/shard_map/ppermute | solution.py:25
  32.6 37.1 %collective-permute-start.14 = (bf16[8,8,16,768]{3,2,1,0:T(8,128)(2,1)S(1)}, bf16[8,8,16,768]{3,2,1,0:T(8,128)(2,1)S(1)}, u32[]{:S(2)}, u32[]{:S(2)}) collective-permute-start(bf16[8,8,16,768]{3,2,1,0:T(8,128)(2,1)S(1)} %bitcast_dynamic-update-slice_fusion.8.src), channel_id=1, source_target_pairs={{0,1},{1,0},{2,3},{3,2},{4,5},{5,4},{6,7},{7,6},{8,9},{9,8},{10,11... | collective-permute-start | bytes 4718600 | tf_op jit(solution)/shard_map/ppermute | solution.py:25
  36.2 28.9 %collective-permute-start.10 = (bf16[768,768]{1,0:T(8,128)(2,1)S(1)}, bf16[768,768]{1,0:T(8,128)(2,1)S(1)}, u32[]{:S(2)}, u32[]{:S(2)}) collective-permute-start(bf16[768,768]{1,0:T(8,128)(2,1)S(1)} %copy-done), channel_id=1, source_target_pairs={{0,16},{16,0},{32,48},{48,32},{64,80},{80,64},{96,112},{112,96},{1... | collective-permute-start | bytes 3538952 | tf_op jit(solution)/shard_map/ppermute | solution.py:25
  38.8 30.3 %collective-permute-start.21 = (bf16[256,768]{1,0:T(8,128)(2,1)S(1)}, bf16[256,768]{1,0:T(8,128)(2,1)S(1)}, u32[]{:S(2)}, u32[]{:S(2)}) collective-permute-start(bf16[256,768]{1,0:T(8,128)(2,1)S(1)} %copy-done.3), channel_id=1, source_target_pairs={{0,64},{16,80},{32,96},{48,112},{64,0},{80,16},{96,32},{112,48},{1... | collective-permute-start | bytes 1179656 | tf_op jit(solution)/shard_map/ppermute | solution.py:25
  40.8 28.5 %collective-permute-start.19 = (bf16[256,768]{1,0:T(8,128)(2,1)S(1)}, bf16[256,768]{1,0:T(8,128)(2,1)S(1)}, u32[]{:S(2)}, u32[]{:S(2)}) collective-permute-start(bf16[256,768]{1,0:T(8,128)(2,1)S(1)} %copy-done.3), channel_id=1, source_target_pairs={{0,32},{16,48},{32,0},{48,16},{64,96},{80,112},{96,64},{112,80},{1... | collective-permute-start | bytes 1179656 | tf_op jit(solution)/shard_map/ppermute | solution.py:25
  40.8 32.9 %collective-permute-start.23 = (bf16[256,768]{1,0:T(8,128)(2,1)S(1)}, bf16[256,768]{1,0:T(8,128)(2,1)S(1)}, u32[]{:S(2)}, u32[]{:S(2)}) collective-permute-start(bf16[256,768]{1,0:T(8,128)(2,1)S(1)} %copy-done.3), channel_id=1, source_target_pairs={{0,96},{16,112},{32,64},{48,80},{64,32},{80,48},{96,0},{112,16},{1... | collective-permute-start | bytes 1179656 | tf_op jit(solution)/shard_map/ppermute | solution.py:25
  65.1 14.9 %collective-permute-start.18 = (bf16[256,768]{1,0:T(8,128)(2,1)S(1)}, bf16[256,768]{1,0:T(8,128)(2,1)S(1)}, u32[]{:S(2)}, u32[]{:S(2)}) collective-permute-start(bf16[256,768]{1,0:T(8,128)(2,1)S(1)} %copy-done.3), channel_id=1, source_target_pairs={{0,16},{16,0},{32,48},{48,32},{64,80},{80,64},{96,112},{112,96},{1... | collective-permute-start | bytes 1179656 | tf_op jit(solution)/shard_map/ppermute | solution.py:25
  69.2 15.5 %collective-permute-start.22 = (bf16[256,768]{1,0:T(8,128)(2,1)S(1)}, bf16[256,768]{1,0:T(8,128)(2,1)S(1)}, u32[]{:S(2)}, u32[]{:S(2)}) collective-permute-start(bf16[256,768]{1,0:T(8,128)(2,1)S(1)} %collective-permute-done.21.rest_4_), channel_id=1, source_target_pairs={{0,16},{16,0},{32,48},{48,32},{64,80},{80,64},{96,112},{112,96},{1... | collective-permute-start | bytes 1179656 | tf_op jit(solution)/shard_map/ppermute | solution.py:25
  69.7 23.5 %collective-permute-start.20 = (bf16[256,768]{1,0:T(8,128)(2,1)S(1)}, bf16[256,768]{1,0:T(8,128)(2,1)S(1)}, u32[]{:S(2)}, u32[]{:S(2)}) collective-permute-start(bf16[256,768]{1,0:T(8,128)(2,1)S(1)} %collective-permute-done.19.rest_2_), channel_id=1, source_target_pairs={{0,16},{16,0},{32,48},{48,32},{64,80},{80,64},{96,112},{112,96},{1... | collective-permute-start | bytes 1179656 | tf_op jit(solution)/shard_map/ppermute | solution.py:25
  75.9 25.7 %collective-permute-start.24 = (bf16[256,768]{1,0:T(8,128)(2,1)S(1)}, bf16[256,768]{1,0:T(8,128)(2,1)S(1)}, u32[]{:S(2)}, u32[]{:S(2)}) collective-permute-start(bf16[256,768]{1,0:T(8,128)(2,1)S(1)} %collective-permute-done.23.rest_6_), channel_id=1, source_target_pairs={{0,16},{16,0},{32,48},{48,32},{64,80},{80,64},{96,112},{112,96},{1... | collective-permute-start | bytes 1179656 | tf_op jit(solution)/shard_map/ppermute | solution.py:25
  79.8 21.8 %collective-permute-start.11 = (bf16[128,768]{1,0:T(8,128)(2,1)S(1)}, bf16[128,768]{1,0:T(8,128)(2,1)S(1)}, u32[]{:S(2)}, u32[]{:S(2)}) collective-permute-start(bf16[128,768]{1,0:T(8,128)(2,1)S(1)} %get-tuple-element.43), channel_id=1, source_target_pairs={{0,32},{16,48},{32,0},{48,16},{64,96},{80,112},{96,64},{112,80},{1... | collective-permute-start | bytes 589832 | tf_op jit(solution)/shard_map/ppermute | solution.py:25
  80.0 21.6 %collective-permute-start.13 = (bf16[128,768]{1,0:T(8,128)(2,1)S(1)}, bf16[128,768]{1,0:T(8,128)(2,1)S(1)}, u32[]{:S(2)}, u32[]{:S(2)}) collective-permute-start(bf16[128,768]{1,0:T(8,128)(2,1)S(1)} %shard_map.111), channel_id=1, source_target_pairs={{0,96},{16,112},{32,64},{48,80},{64,32},{80,48},{96,0},{112,16},{1... | collective-permute-start | bytes 589832 | tf_op jit(solution)/shard_map/ppermute | solution.py:25
  84.7 16.9 %collective-permute-start.15 = (bf16[128,768]{1,0:T(8,128)(2,1)S(1)}, bf16[128,768]{1,0:T(8,128)(2,1)S(1)}, u32[]{:S(2)}, u32[]{:S(2)}) collective-permute-start(bf16[128,768]{1,0:T(8,128)(2,1)S(1)} %get-tuple-element.47), channel_id=1, source_target_pairs={{0,96},{16,112},{32,64},{48,80},{64,32},{80,48},{96,0},{112,16},{1... | collective-permute-start | bytes 589832 | tf_op jit(solution)/shard_map/ppermute | solution.py:25
  93.2 8.4 %collective-permute-start.17 = (bf16[128,768]{1,0:T(8,128)(2,1)S(1)}, bf16[128,768]{1,0:T(8,128)(2,1)S(1)}, u32[]{:S(2)}, u32[]{:S(2)}) collective-permute-start(bf16[128,768]{1,0:T(8,128)(2,1)S(1)} %shard_map.113), channel_id=1, source_target_pairs={{0,32},{16,48},{32,0},{48,16},{64,96},{80,112},{96,64},{112,80},{1... | collective-permute-start | bytes 589832 | tf_op jit(solution)/shard_map/ppermute | solution.py:25
  111.8 8.2 %collective-permute-start.26 = (bf16[16,6144]{1,0:T(8,128)(2,1)S(1)}, bf16[16,6144]{1,0:T(8,128)(2,1)S(1)}, u32[]{:S(2)}, u32[]{:S(2)}) collective-permute-start(bf16[16,6144]{1,0:T(8,128)(2,1)S(1)} %get-tuple-element.53), channel_id=1, source_target_pairs={{0,2},{1,3},{2,0},{3,1},{4,6},{5,7},{6,4},{7,5},{8,10},{9,11},{10,... | collective-permute-start | bytes 589832 | tf_op jit(solution)/shard_map/ppermute | solution.py:25
  112.5 8.5 %collective-permute-start.27 = (bf16[16,6144]{1,0:T(8,128)(2,1)S(1)}, bf16[16,6144]{1,0:T(8,128)(2,1)S(1)}, u32[]{:S(2)}, u32[]{:S(2)}) collective-permute-start(bf16[16,6144]{1,0:T(8,128)(2,1)S(1)} %get-tuple-element.54), channel_id=1, source_target_pairs={{0,6},{1,7},{2,4},{3,5},{4,2},{5,3},{6,0},{7,1},{8,14},{9,15},{10,... | collective-permute-start | bytes 589832 | tf_op jit(solution)/shard_map/ppermute | solution.py:25
  125.5 8.8 %collective-permute-start.35 = (bf16[16,6144]{1,0:T(8,128)(2,1)S(1)}, bf16[16,6144]{1,0:T(8,128)(2,1)S(1)}, u32[]{:S(2)}, u32[]{:S(2)}) collective-permute-start(bf16[16,6144]{1,0:T(8,128)(2,1)S(1)} %shard_map.118), channel_id=1, source_target_pairs={{0,6},{1,7},{2,4},{3,5},{4,2},{5,3},{6,0},{7,1},{8,14},{9,15},{10,... | collective-permute-start | bytes 589832 | tf_op jit(solution)/shard_map/ppermute | solution.py:25
  129.6 9.8 %collective-permute-start.39 = (bf16[16,6144]{1,0:T(8,128)(2,1)S(1)}, bf16[16,6144]{1,0:T(8,128)(2,1)S(1)}, u32[]{:S(2)}, u32[]{:S(2)}) collective-permute-start(bf16[16,6144]{1,0:T(8,128)(2,1)S(1)} %collective-permute-done.36), channel_id=1, source_target_pairs={{0,6},{1,7},{2,4},{3,5},{4,2},{5,3},{6,0},{7,1},{8,14},{9,15},{10,... | collective-permute-start | bytes 589832 | tf_op jit(solution)/shard_map/ppermute | solution.py:25
  139.4 16.5 %collective-permute-start.47 = (bf16[8,16,6144]{2,1,0:T(8,128)(2,1)S(1)}, bf16[8,16,6144]{2,1,0:T(8,128)(2,1)S(1)}, u32[]{:S(2)}, u32[]{:S(2)}) collective-permute-start(bf16[8,16,6144]{2,1,0:T(8,128)(2,1)S(1)} %bitcast_dynamic-update-slice_fusion.src), channel_id=1, source_target_pairs={{0,1},{1,0},{2,3},{3,2},{4,5},{5,4},{6,7},{7,6},{8,9},{9,8},{10,11... | collective-permute-start | bytes 4718600 | tf_op jit(solution)/shard_map/ppermute | solution.py:25
  164.2 8.1 %collective-permute-start.42 = (bf16[16,3072]{1,0:T(8,128)(2,1)S(1)}, bf16[16,3072]{1,0:T(8,128)(2,1)S(1)}, u32[]{:S(2)}, u32[]{:S(2)}) collective-permute-start(bf16[16,3072]{1,0:T(8,128)(2,1)S(1)} %get-tuple-element.66), channel_id=1, source_target_pairs={{0,6},{1,7},{2,4},{3,5},{4,2},{5,3},{6,0},{7,1},{8,14},{9,15},{10,... | collective-permute-start | bytes 294920 | tf_op jit(solution)/shard_map/ppermute | solution.py:25
  166.6 9.9 %collective-permute-start.45 = (bf16[16,3072]{1,0:T(8,128)(2,1)S(1)}, bf16[16,3072]{1,0:T(8,128)(2,1)S(1)}, u32[]{:S(2)}, u32[]{:S(2)}) collective-permute-start(bf16[16,3072]{1,0:T(8,128)(2,1)S(1)} %get-tuple-element.69), channel_id=1, source_target_pairs={{0,12},{1,13},{2,14},{3,15},{4,8},{5,9},{6,10},{7,11},{8,4},{9,5},... | collective-permute-start | bytes 294920 | tf_op jit(solution)/shard_map/ppermute | solution.py:25
  169.7 8.0 %collective-permute-start.46 = (bf16[16,3072]{1,0:T(8,128)(2,1)S(1)}, bf16[16,3072]{1,0:T(8,128)(2,1)S(1)}, u32[]{:S(2)}, u32[]{:S(2)}) collective-permute-start(bf16[16,3072]{1,0:T(8,128)(2,1)S(1)} %get-tuple-element.70), channel_id=1, source_target_pairs={{0,14},{1,15},{2,12},{3,13},{4,10},{5,11},{6,8},{7,9},{8,6},{9,7},... | collective-permute-start | bytes 294920 | tf_op jit(solution)/shard_map/ppermute | solution.py:25
  172.3 8.8 %collective-permute-start.55 = (bf16[16,3072]{1,0:T(8,128)(2,1)S(1)}, bf16[16,3072]{1,0:T(8,128)(2,1)S(1)}, u32[]{:S(2)}, u32[]{:S(2)}) collective-permute-start(bf16[16,3072]{1,0:T(8,128)(2,1)S(1)} %get-tuple-element.79), channel_id=1, source_target_pairs={{0,14},{1,15},{2,12},{3,13},{4,10},{5,11},{6,8},{7,9},{8,6},{9,7},... | collective-permute-start | bytes 294920 | tf_op jit(solution)/shard_map/ppermute | solution.py:25
  173.3 7.8 %collective-permute-start.54 = (bf16[16,3072]{1,0:T(8,128)(2,1)S(1)}, bf16[16,3072]{1,0:T(8,128)(2,1)S(1)}, u32[]{:S(2)}, u32[]{:S(2)}) collective-permute-start(bf16[16,3072]{1,0:T(8,128)(2,1)S(1)} %get-tuple-element.80), channel_id=1, source_target_pairs={{0,12},{1,13},{2,14},{3,15},{4,8},{5,9},{6,10},{7,11},{8,4},{9,5},... | collective-permute-start | bytes 294920 | tf_op jit(solution)/shard_map/ppermute | solution.py:25
  173.3 7.8 %collective-permute-start.53 = (bf16[16,3072]{1,0:T(8,128)(2,1)S(1)}, bf16[16,3072]{1,0:T(8,128)(2,1)S(1)}, u32[]{:S(2)}, u32[]{:S(2)}) collective-permute-start(bf16[16,3072]{1,0:T(8,128)(2,1)S(1)} %get-tuple-element.81), channel_id=1, source_target_pairs={{0,10},{1,11},{2,8},{3,9},{4,14},{5,15},{6,12},{7,13},{8,2},{9,3},... | collective-permute-start | bytes 294920 | tf_op jit(solution)/shard_map/ppermute | solution.py:25
  176.5 10.0 %collective-permute-start.52 = (bf16[16,3072]{1,0:T(8,128)(2,1)S(1)}, bf16[16,3072]{1,0:T(8,128)(2,1)S(1)}, u32[]{:S(2)}, u32[]{:S(2)}) collective-permute-start(bf16[16,3072]{1,0:T(8,128)(2,1)S(1)} %get-tuple-element.82), channel_id=1, source_target_pairs={{0,8},{1,9},{2,10},{3,11},{4,12},{5,13},{6,14},{7,15},{8,0},{9,1},... | collective-permute-start | bytes 294920 | tf_op jit(solution)/shard_map/ppermute | solution.py:25
  177.6 8.9 %collective-permute-start.51 = (bf16[16,3072]{1,0:T(8,128)(2,1)S(1)}, bf16[16,3072]{1,0:T(8,128)(2,1)S(1)}, u32[]{:S(2)}, u32[]{:S(2)}) collective-permute-start(bf16[16,3072]{1,0:T(8,128)(2,1)S(1)} %get-tuple-element.83), channel_id=1, source_target_pairs={{0,6},{1,7},{2,4},{3,5},{4,2},{5,3},{6,0},{7,1},{8,14},{9,15},{10,... | collective-permute-start | bytes 294920 | tf_op jit(solution)/shard_map/ppermute | solution.py:25
  189.3 7.8 %collective-permute-start.57 = (bf16[2,16,1024]{2,1,0:T(8,128)(2,1)S(1)}, bf16[2,16,1024]{2,1,0:T(8,128)(2,1)S(1)}, u32[]{:S(2)}, u32[]{:S(2)}) collective-permute-start(bf16[2,16,1024]{2,1,0:T(8,128)(2,1)S(1)} %get-tuple-element.73), channel_id=1, source_target_pairs={{0,4},{1,5},{2,6},{3,7},{4,0},{5,1},{6,2},{7,3},{8,12},{9,13},{10,... | collective-permute-start | bytes 196616 | tf_op jit(solution)/shard_map/ppermute | solution.py:25
  (40 other events, 302.2 us)

commit v3 on v2

--- a/solution.py
+++ b/solution.py
@@ -70,7 +70,7 @@
 
 def attn_kernel(ids, a0, a1, a2, b0, b1, b2, *rest):
     wo = rest[:8]
-    outs = rest[8:10]
+    give, left = rest[8:10]
     packed = rest[10]
     mixed = rest[11]
     length, width = packed.shape
@@ -96,11 +96,19 @@
         mixed[:, h * HEAD:(h + 1) * HEAD] = jnp.dot(
             p, v, preferred_element_type=F32
         ).astype(BF)
+    left[...] = mixed[:half, :]
+    spread(mixed[half:, :], wo, give)
+
+
+def spread(rows, wo, o_ref):
     width = wo[0].shape[1]
     for e in range(8):
-        acc = jnp.dot(mixed[...], wo[e][...], preferred_element_type=F32).astype(BF)
-        outs[0][:, e * width:(e + 1) * width] = acc[:half]
-        outs[1][:, e * width:(e + 1) * width] = acc[half:]
+        acc = jnp.dot(rows, wo[e][...], preferred_element_type=F32)
+        o_ref[:, e * width:(e + 1) * width] = acc.astype(BF)
+
+
+def keep_kernel(left, *rest):
+    spread(left[...], rest[:8], rest[8])
 
 
 def pair_kernel(a_ref, b_ref, *outs):
@@ -182,24 +190,38 @@
     )(pltpu.with_memory_space_constraint(picks, pltpu.VMEM), *big)
 
 
-def depth_kernel(ids, *rest):
-    outs = rest[16:24]
-    z = rest[24]
-    for m in range(16):
-        z[m * 16:(m + 1) * 16, :] = rest[m][...]
+def depth_first(ids, low, high, *rest):
+    o_ref, z = rest[11:13]
+    z[0:16, :] = low[...]
+    z[128:144, :] = high[...]
+    for i in range(3):
+        at = (i + 1) * 16
+        z[at:at + 16, :] = rest[i][0]
+        z[128 + at:144 + at, :] = rest[i][1]
+    for i in range(4):
+        at = (i + 4) * 16
+        z[at:at + 16, :] = rest[3 + i][...]
+        z[128 + at:144 + at, :] = rest[7 + i][...]
+    depth_rows(ids, z, 128, o_ref)
+
+
+def depth_second(ids, z, o_ref):
+    depth_rows(ids, z, 0, o_ref)
+
+
+def depth_rows(ids, z, at, o_ref):
     section = ids[1]
-    rows = lax.broadcasted_iota(jnp.int32, (256, 1), 0)
+    rows = at + lax.broadcasted_iota(jnp.int32, (128, 1), 0)
     cols = lax.broadcasted_iota(jnp.int32, (1, 256), 1)
     rpos = place(rows, section, 16) // 16
     cpos = place(cols, section, 16) // 16
     keep = (cpos <= rpos) & (rows % 16 == cols % 16)
     bias = jnp.where(keep, 0.0, NEG)
-    lane = lax.broadcasted_iota(jnp.int32, (256, 2 * DHEAD), 1)
-    low = lane < DHEAD
+    low = lax.broadcasted_iota(jnp.int32, (128, 2 * DHEAD), 1) < DHEAD
     inner = z.shape[1] // 3
     for pair in range(inner // (2 * DHEAD)):
         base = pair * 2 * DHEAD
-        q = z[:, base:base + 2 * DHEAD]
+        q = z[at:at + 128, base:base + 2 * DHEAD]
         k = z[:, inner + base:inner + base + 2 * DHEAD]
         v = z[:, 2 * inner + base:2 * inner + base + 2 * DHEAD]
         got = []
@@ -216,18 +238,20 @@
             o = jnp.dot(e.astype(BF), v, preferred_element_type=F32)
             got.append(o / total)
         res = jnp.where(low, got[0], got[1]).astype(BF)
-        for e in range(8):
-            outs[e][0, :, base:base + 2 * DHEAD] = res[e * 16:(e + 1) * 16]
-            outs[e][1, :, base:base + 2 * DHEAD] = res[128 + e * 16:128 + (e + 1) * 16]
+        o_ref[:, :, base:base + 2 * DHEAD] = res.reshape(8, 16, 2 * DHEAD)
+
+
+def join_kernel(a_ref, b_ref, *outs):
+    for e, o_ref in enumerate(outs):
+        o_ref[0] = a_ref[e]
+        o_ref[1] = b_ref[e]
 
 
 def final_kernel(ids, *rest):
-    pieces = rest[:8]
-    other = rest[8]
-    o_ref = rest[9]
+    o_ref = rest[8]
     for e in range(8):
-        o_ref[ids[1] ^ (2 * e)] = pieces[e][0]
-        o_ref[ids[1] ^ (2 * e + 1)] = other[e]
+        o_ref[ids[1] ^ (2 * e)] = rest[e][0]
+        o_ref[ids[1] ^ (2 * e + 1)] = rest[e][1]
 
 
 def add_kernel(*refs):
@@ -273,7 +297,7 @@
     local = [rel[0:2]] + [fs(rel[2 * d:2 * d + 2], 2 * d) for d in (1, 2, 3)]
     local = jnp.concatenate(local, axis=0)
     wo_even = [w_out] + [fs(w_out, 2 * d) for d in (1, 2, 3)]
-    wo_odd = [near] + [fs(w, 1) for w in wo_even[1:]]
+    wo_odd = [near] + [fs(near, 2 * d) for d in (1, 2, 3)]
     wo = [w for pair in zip(wo_even, wo_odd) for w in pair]
     even = jnp.stack(gather(local, True))
     odd = cb(even, 1)
@@ -292,14 +316,15 @@
     plain_b = fs(b3, 6)
     sum_a = fs(add(a3, relay_a), 6)
     sum_b = fs(add(b1, relay_b), 2)
-    keep, give = call(
+    give, left = call(
         attn_kernel,
-        [((128, model), BF)] * 2,
+        [((128, model), BF), ((128, w_out.shape[0]), BF)],
         scratch=[pltpu.VMEM((256, cols), BF), pltpu.VMEM((256, w_out.shape[0]), BF)],
         smem=1,
         n_in=15,
     )(ids, a0, plain_a, sum_a, b0, plain_b, sum_b, *wo)
     taken = cb(give, 1)
+    keep = call(keep_kernel, [((128, model), BF)], n_in=9)(left, *wo)[0]
     blocks = call(pair_kernel, [((16, model), F32)] + [((16, model), BF)] * 7, n_in=2)(
         keep, taken
     )
@@ -333,21 +358,23 @@
     low = lift(even, 0, [((16, 3 * inner), BF)] * 8)
     high = lift(odd, 128, [((8, 16, 3 * inner), BF)])[0]
     high = cb(high, 1)
-    got = {e: cb(low[e], 2 * e) for e in (1, 2, 3)}
-    got.update({e: cb(low[e], 2 * e) for e in (4, 5, 6, 7)})
-    deep = [high[0]] + [cb(high[e], 2 * e) for e in range(1, 8)]
-    pieces = [low[0]] + [got[e] for e in range(1, 8)] + deep
-    outs = call(
-        depth_kernel,
-        [((2, 16, inner), BF)] * 8,
-        scratch=[pltpu.VMEM((256, 3 * inner), BF)],
+    got = {e: cb(low[e], 2 * e) for e in (5, 7)}
+    got.update({e: cb(low[e], 2 * e) for e in (6, 4)})
+    both = [cb(jnp.stack([low[e], high[e]]), 2 * e) for e in (2, 1, 3)]
+    deep = [cb(high[e], 2 * e) for e in (4, 5, 6, 7)]
+    both = [both[1], both[0], both[2]]
+    other, z = call(
+        depth_first,
+        [((8, 16, inner), BF), ((256, 3 * inner), BF)],
         smem=1,
-        n_in=17,
-    )(ids, *pieces)
+        n_in=14,
+    )(ids, low[0], high[0], *both, *[got[e] for e in (4, 5, 6, 7)], *deep)
+    other = cb(other, 1)
+    outs = call(depth_second, [((8, 16, inner), BF)], smem=1, n_in=2)(ids, z)[0]
+    outs = call(join_kernel, [((2, 16, inner), BF)] * 8, n_in=2)(outs, other)
     pieces = [outs[0]] + [cb(outs[e], 2 * e) for e in range(1, 8)]
-    other = cb(jnp.stack([p[1] for p in pieces]), 1)
-    out = call(final_kernel, [((16, 16, inner), BF)], smem=1, n_in=10, last=True)(
-        ids, *pieces, other
+    out = call(final_kernel, [((16, 16, inner), BF)], smem=1, n_in=9, last=True)(
+        ids, *pieces
     )[0]
     return out.reshape(1, 1, 256, inner)
 

time: 211 us -> 220 us (1.043)
  waiting for transfers between devices: 93.4 us -> 106 us
  starting transfers between devices: 87.4 us -> 80.7 us
    ppermute x64 -> x61, waiting for transfers between devices: 93.4 us -> 106 us  [swap(): return lax.ppermute(value, axis, [(i, i ^ flip) for i in range(size)])]
    ppermute x64 -> x61, starting transfers between devices: 87.4 us -> 80.7 us  [swap(): return lax.ppermute(value, axis, [(i, i ^ flip) for i in range(size)])]
    pallas_call x14 -> x17, Pallas kernels: 17.3 us -> 18.6 us  [go(): return run(*args[:smem], *near)]
  transfers between devices with their start and end apart: 64 -> 61, of which waited for: 28 -> 30; matrix products, arithmetic and copies ran while one was open for 1% -> 1% of each run, Pallas kernels for 6% -> 7%
where the time goes in v3:
time: 220 us; the launch traced here: 218 us
  waiting for transfers between devices  106 us (48%)
  starting transfers between devices  80.7 us (37%)
  Pallas kernels  26.3 us (12%)
  local copies, waits for them, and re-layouts  2.7 us (1%)
    ppermute x61, waiting for transfers between devices, swap(): return lax.ppermute(value, axis, [(i, i ^ flip) for i in range(size)])  106 us
    ppermute x61, starting transfers between devices, swap(): return lax.ppermute(value, axis, [(i, i ^ flip) for i in range(size)])  80.7 us
    pallas_call x17, Pallas kernels, go(): return run(*args[:smem], *near)  18.6 us
    pallas_call x1, Pallas kernels, fetch(): pl.pallas_call(fetch_kernel, out_shape=[pltpu.VMEM(s, BF) for s in shapes...  7.67 us
  transfers between devices with their start and end apart: 61, of which 30 were waited for; matrix products, arithmetic and copies ran while one was open for 1% of the time, Pallas kernels for 7%

profile of v3, /device:TPU:1, one launch (start us, length us, event | category | flops | bytes accessed | tf_op | source)
XLA Modules:
  0.0 218.0 jit_solution(3793017775612680452)
XLA Ops:
  3.2 4.7 %collective-permute-start.2 = (bf16[2,16,768]{2,1,0:T(8,128)(2,1)S(1)}, bf16[2,16,768]{2,1,0:T(8,128)(2,1)S(1)}, u32[]{:S(2)}, u32[]{:S(2)}) collective-permute-start(bf16[2,16,768]{2,1,0:T(8,128)(2,1)S(1)} %get-tuple-element.92), channel_id=1, source_target_pairs={{0,96},{16,112},{32,64},{48,80},{64,32},{80,48},{96,0},{112,16},{1... | collective-permute-start | bytes 147464 | tf_op jit(solution)/shard_map/ppermute | solution.py:25
  9.3 3.0 %collective-permute-done.1 = bf16[2,16,768]{2,1,0:T(8,128)(2,1)S(1)} collective-permute-done((bf16[2,16,768]{2,1,0:T(8,128)(2,1)S(1)}, bf16[2,16,768]{2,1,0:T(8,128)(2,1)S(1)}, u32[]{:S(2)}, u32[]{:S(2)}) %collective-permute-start.1) | collective-permute-done | bytes 49184 | tf_op jit(solution)/shard_map/ppermute | solution.py:25
  17.4 2.1 collective-permute-start.9
  20.7 3.6 %collective-permute-done.4 = bf16[8,16,768]{2,1,0:T(8,128)(2,1)S(1)} collective-permute-done((bf16[8,16,768]{2,1,0:T(8,128)(2,1)S(1)}, bf16[8,16,768]{2,1,0:T(8,128)(2,1)S(1)}, u32[]{:S(2)}, u32[]{:S(2)}) %collective-permute-start.4) | collective-permute-done | bytes 196640 | tf_op jit(solution)/shard_map/ppermute | solution.py:25
  24.4 7.7 %collective-permute-done.7 = bf16[8,16,768]{2,1,0:T(8,128)(2,1)S(1)} collective-permute-done((bf16[8,16,768]{2,1,0:T(8,128)(2,1)S(1)}, bf16[8,16,768]{2,1,0:T(8,128)(2,1)S(1)}, u32[]{:S(2)}, u32[]{:S(2)}) %collective-permute-start.7) | collective-permute-done | bytes 196640 | tf_op jit(solution)/shard_map/ppermute | solution.py:25
  32.6 3.6 %collective-permute-start.14 = (bf16[8,8,16,768]{3,2,1,0:T(8,128)(2,1)S(1)}, bf16[8,8,16,768]{3,2,1,0:T(8,128)(2,1)S(1)}, u32[]{:S(2)}, u32[]{:S(2)}) collective-permute-start(bf16[8,8,16,768]{3,2,1,0:T(8,128)(2,1)S(1)} %bitcast_dynamic-update-slice_fusion.8.src), channel_id=1, source_target_pairs={{0,1},{1,0},{2,3},{3,2},{4,5},{5,4},{6,7},{7,6},{8,9},{9,8},{10,11... | collective-permute-start | bytes 4718600 | tf_op jit(solution)/shard_map/ppermute | solution.py:25
  36.2 2.6 %collective-permute-start.10 = (bf16[768,768]{1,0:T(8,128)(2,1)S(1)}, bf16[768,768]{1,0:T(8,128)(2,1)S(1)}, u32[]{:S(2)}, u32[]{:S(2)}) collective-permute-start(bf16[768,768]{1,0:T(8,128)(2,1)S(1)} %copy-done), channel_id=1, source_target_pairs={{0,16},{16,0},{32,48},{48,32},{64,80},{80,64},{96,112},{112,96},{1... | collective-permute-start | bytes 3538952 | tf_op jit(solution)/shard_map/ppermute | solution.py:25
  40.4 24.7 %collective-permute-done.10.w1_ref = bf16[768,768]{1,0:T(8,128)(2,1)S(1)} collective-permute-done((bf16[768,768]{1,0:T(8,128)(2,1)S(1)}, bf16[768,768]{1,0:T(8,128)(2,1)S(1)}, u32[]{:S(2)}, u32[]{:S(2)}) %collective-permute-start.10) | collective-permute-done | bytes 1179680 | tf_op jit(solution)/shard_map/ppermute | solution.py:25
  66.6 2.4 %collective-permute-start.21 = (bf16[256,768]{1,0:T(8,128)(2,1)S(1)}, bf16[256,768]{1,0:T(8,128)(2,1)S(1)}, u32[]{:S(2)}, u32[]{:S(2)}) collective-permute-start(bf16[256,768]{1,0:T(8,128)(2,1)S(1)} %copy-done.1), channel_id=1, source_target_pairs={{0,64},{16,80},{32,96},{48,112},{64,0},{80,16},{96,32},{112,48},{1... | collective-permute-start | bytes 1179656 | tf_op jit(solution)/shard_map/ppermute | solution.py:25
  75.5 9.9 %collective-permute-done.16.refs_1_ = bf16[128,768]{1,0:T(8,128)(2,1)S(1)} collective-permute-done((bf16[128,768]{1,0:T(8,128)(2,1)S(1)}, bf16[128,768]{1,0:T(8,128)(2,1)S(1)}, u32[]{:S(2)}, u32[]{:S(2)}) %collective-permute-start.16) | collective-permute-done | bytes 196640 | tf_op jit(solution)/shard_map/ppermute | solution.py:25
  89.6 12.6 %collective-permute-done.24.rest_7_ = bf16[256,768]{1,0:T(8,128)(2,1)S(1)} collective-permute-done((bf16[256,768]{1,0:T(8,128)(2,1)S(1)}, bf16[256,768]{1,0:T(8,128)(2,1)S(1)}, u32[]{:S(2)}, u32[]{:S(2)}) %collective-permute-start.24) | collective-permute-done | bytes 393248 | tf_op jit(solution)/shard_map/ppermute | solution.py:25
  105.3 4.2 %collective-permute-done.11.a1 = bf16[128,768]{1,0:T(8,128)(2,1)S(1)} collective-permute-done((bf16[128,768]{1,0:T(8,128)(2,1)S(1)}, bf16[128,768]{1,0:T(8,128)(2,1)S(1)}, u32[]{:S(2)}, u32[]{:S(2)}) %collective-permute-start.11) | collective-permute-done | bytes 196640 | tf_op jit(solution)/shard_map/ppermute | solution.py:25
  110.1 3.6 %collective-permute-done.17.b2 = bf16[128,768]{1,0:T(8,128)(2,1)S(1)} collective-permute-done((bf16[128,768]{1,0:T(8,128)(2,1)S(1)}, bf16[128,768]{1,0:T(8,128)(2,1)S(1)}, u32[]{:S(2)}, u32[]{:S(2)}) %collective-permute-start.17) | collective-permute-done | bytes 196640 | tf_op jit(solution)/shard_map/ppermute | solution.py:25
  113.7 2.1 shard_map.114
  115.9 2.6 %collective-permute-start.25 = (bf16[128,6144]{1,0:T(8,128)(2,1)S(1)}, bf16[128,6144]{1,0:T(8,128)(2,1)S(1)}, u32[]{:S(2)}, u32[]{:S(2)}) collective-permute-start(bf16[128,6144]{1,0:T(8,128)(2,1)S(1)} %get-tuple-element.53), channel_id=1, source_target_pairs={{0,1},{1,0},{2,3},{3,2},{4,5},{5,4},{6,7},{7,6},{8,9},{9,8},{10,11... | collective-permute-start | bytes 4718600 | tf_op jit(solution)/shard_map/ppermute | solution.py:25
  119.1 2.4 %collective-permute-done.25.b_ref = bf16[128,6144]{1,0:T(8,128)(2,1)S(1)} collective-permute-done((bf16[128,6144]{1,0:T(8,128)(2,1)S(1)}, bf16[128,6144]{1,0:T(8,128)(2,1)S(1)}, u32[]{:S(2)}, u32[]{:S(2)}) %collective-permute-start.25) | collective-permute-done | bytes 1572896 | tf_op jit(solution)/shard_map/ppermute | solution.py:25
  125.9 2.1 collective-permute-done.28.refs_1_
  134.1 2.3 %collective-permute-done.32.rest_4_ = bf16[16,6144]{1,0:T(8,128)(2,1)S(1)} collective-permute-done((bf16[16,6144]{1,0:T(8,128)(2,1)S(1)}, bf16[16,6144]{1,0:T(8,128)(2,1)S(1)}, u32[]{:S(2)}, u32[]{:S(2)}) %collective-permute-start.32) | collective-permute-done | bytes 196640 | tf_op jit(solution)/shard_map/ppermute | solution.py:25
  137.8 2.0 collective-permute-start.35
  143.3 2.7 %collective-permute-done.34 = bf16[16,6144]{1,0:T(8,128)(2,1)S(1)} collective-permute-done((bf16[16,6144]{1,0:T(8,128)(2,1)S(1)}, bf16[16,6144]{1,0:T(8,128)(2,1)S(1)}, u32[]{:S(2)}, u32[]{:S(2)}) %collective-permute-start.34) | collective-permute-done | bytes 196640 | tf_op jit(solution)/shard_map/ppermute | solution.py:25
  146.7 3.4 %collective-permute-done.37 = bf16[16,6144]{1,0:T(8,128)(2,1)S(1)} collective-permute-done((bf16[16,6144]{1,0:T(8,128)(2,1)S(1)}, bf16[16,6144]{1,0:T(8,128)(2,1)S(1)}, u32[]{:S(2)}, u32[]{:S(2)}) %collective-permute-start.37) | collective-permute-done | bytes 196640 | tf_op jit(solution)/shard_map/ppermute | solution.py:25
  151.8 7.1 %collective-permute-start.40 = (bf16[8,16,6144]{2,1,0:T(8,128)(2,1)S(1)}, bf16[8,16,6144]{2,1,0:T(8,128)(2,1)S(1)}, u32[]{:S(2)}, u32[]{:S(2)}) collective-permute-start(bf16[8,16,6144]{2,1,0:T(8,128)(2,1)S(1)} %bitcast_dynamic-update-slice_fusion.src), channel_id=1, source_target_pairs={{0,1},{1,0},{2,3},{3,2},{4,5},{5,4},{6,7},{7,6},{8,9},{9,8},{10,11... | collective-permute-start | bytes 4718600 | tf_op jit(solution)/shard_map/ppermute | solution.py:25
  160.5 7.7 %shard_map.120 = (bf16[6144,1024]{1,0:T(8,128)(2,1)S(1)}, bf16[1024,3072]{1,0:T(8,128)(2,1)S(1)}, bf16[256,1024]{1,0:T(8,128)(2,1)S(1)}) custom-call(s32[256,1]{1,0:T(8,128)S(1)} %reshape.42.picks, bf16[6144,1024]{1,0:T(8,128)(2,1)} %bitcast.61, bf16[1024,3072]{1,0:T(8,128)(2,1)} %bitcast.62, bf16[2048,1024]{1,0:T(8,128)(2,1)} %bitcast.63), custom_call_target="tpu_custom_call" | custom-call | tf_op jit(solution)/shard_map/pallas_call | solution.py:183
  168.2 3.0 %shard_map.122 = bf16[8,16,3072]{2,1,0:T(8,128)(2,1)S(1)} custom-call(bf16[8,16,6144]{2,1,0:T(8,128)(2,1)S(1)} %collective-permute-done.40.src, bf16[6144,1024]{1,0:T(8,128)(2,1)S(1)} %get-tuple-element.62.din, bf16[256,1024]{1,0:T(8,128)(2,1)S(1)} %get-tuple-element.63.emb, f32[1,1024]{1,0:T(1,128)S(1)} %copy-done.6, ...), custom_call_target="tpu_custom_call" | custom-call | tf_op jit(solution)/shard_map/pallas_call | solution.py:41
  171.5 3.0 %shard_map.121 = (bf16[16,3072]{1,0:T(8,128)(2,1)S(1)}, bf16[16,3072]{1,0:T(8,128)(2,1)S(1)}, bf16[16,3072]{1,0:T(8,128)(2,1)S(1)}, bf16[16,3072]{1,0:T(8,128)(2...) custom-call(bf16[8,16,6144]{2,1,0:T(8,128)(2,1)S(1)} %bitcast_dynami, ...), custom_call_target="tpu_custom_call" | custom-call | tf_op jit(solution)/shard_map/pallas_call | solution.py:41
  175.0 2.9 %collective-permute-start.47 = (bf16[16,3072]{1,0:T(8,128)(2,1)S(1)}, bf16[16,3072]{1,0:T(8,128)(2,1)S(1)}, u32[]{:S(2)}, u32[]{:S(2)}) collective-permute-start(bf16[16,3072]{1,0:T(8,128)(2,1)S(1)} %get-tuple-element.71), channel_id=1, source_target_pairs={{0,12},{1,13},{2,14},{3,15},{4,8},{5,9},{6,10},{7,11},{8,4},{9,5},... | collective-permute-start | bytes 294920 | tf_op jit(solution)/shard_map/ppermute | solution.py:25
  177.9 2.6 %collective-permute-start.48 = (bf16[16,3072]{1,0:T(8,128)(2,1)S(1)}, bf16[16,3072]{1,0:T(8,128)(2,1)S(1)}, u32[]{:S(2)}, u32[]{:S(2)}) collective-permute-start(bf16[16,3072]{1,0:T(8,128)(2,1)S(1)} %get-tuple-element.72), channel_id=1, source_target_pairs={{0,14},{1,15},{2,12},{3,13},{4,10},{5,11},{6,8},{7,9},{8,6},{9,7},... | collective-permute-start | bytes 294920 | tf_op jit(solution)/shard_map/ppermute | solution.py:25
  181.8 3.2 %collective-permute-start.42 = (bf16[2,16,3072]{2,1,0:T(8,128)(2,1)S(1)}, bf16[2,16,3072]{2,1,0:T(8,128)(2,1)S(1)}, u32[]{:S(2)}, u32[]{:S(2)}) collective-permute-start(bf16[2,16,3072]{2,1,0:T(8,128)(2,1)S(1)} %pad_maximum_fusion.1), channel_id=1, source_target_pairs={{0,2},{1,3},{2,0},{3,1},{4,6},{5,7},{6,4},{7,5},{8,10},{9,11},{10,... | collective-permute-start | bytes 589832 | tf_op jit(solution)/shard_map/ppermute | solution.py:25
  188.8 7.8 %collective-permute-done.50.rest_8_ = bf16[16,3072]{1,0:T(8,128)(2,1)S(1)} collective-permute-done((bf16[16,3072]{1,0:T(8,128)(2,1)S(1)}, bf16[16,3072]{1,0:T(8,128)(2,1)S(1)}, u32[]{:S(2)}, u32[]{:S(2)}) %collective-permute-start.50) | collective-permute-done | bytes 98336 | tf_op jit(solution)/shard_map/ppermute | solution.py:25
  198.6 3.8 %collective-permute-start.53 = (bf16[8,16,1024]{2,1,0:T(8,128)(2,1)S(1)}, bf16[8,16,1024]{2,1,0:T(8,128)(2,1)S(1)}, u32[]{:S(2)}, u32[]{:S(2)}) collective-permute-start(bf16[8,16,1024]{2,1,0:T(8,128)(2,1)S(1)} %get-tuple-element.74), channel_id=1, source_target_pairs={{0,1},{1,0},{2,3},{3,2},{4,5},{5,4},{6,7},{7,6},{8,9},{9,8},{10,11... | collective-permute-start | bytes 786440 | tf_op jit(solution)/shard_map/ppermute | solution.py:25
  208.7 2.7 %collective-permute-start.59 = (bf16[2,16,1024]{2,1,0:T(8,128)(2,1)S(1)}, bf16[2,16,1024]{2,1,0:T(8,128)(2,1)S(1)}, u32[]{:S(2)}, u32[]{:S(2)}) collective-permute-start(bf16[2,16,1024]{2,1,0:T(8,128)(2,1)S(1)} %get-tuple-element.81), channel_id=1, source_target_pairs={{0,12},{1,13},{2,14},{3,15},{4,8},{5,9},{6,10},{7,11},{8,4},{9,5},... | collective-permute-start | bytes 196616 | tf_op jit(solution)/shard_map/ppermute | solution.py:25
  211.4 2.7 %collective-permute-start.60 = (bf16[2,16,1024]{2,1,0:T(8,128)(2,1)S(1)}, bf16[2,16,1024]{2,1,0:T(8,128)(2,1)S(1)}, u32[]{:S(2)}, u32[]{:S(2)}) collective-permute-start(bf16[2,16,1024]{2,1,0:T(8,128)(2,1)S(1)} %get-tuple-element.82), channel_id=1, source_target_pairs={{0,14},{1,15},{2,12},{3,13},{4,10},{5,11},{6,8},{7,9},{8,6},{9,7},... | collective-permute-start | bytes 196616 | tf_op jit(solution)/shard_map/ppermute | solution.py:25
  (155 shorter events, 66.0 us)
Async XLA Ops:
  14.9 9.5 %collective-permute-start.5 = (bf16[8,16,768]{2,1,0:T(8,128)(2,1)S(1)}, bf16[8,16,768]{2,1,0:T(8,128)(2,1)S(1)}, u32[]{:S(2)}, u32[]{:S(2)}) collective-permute-start(bf16[8,16,768]{2,1,0:T(8,128)(2,1)S(1)} %pad_maximum_fusion), channel_id=1, source_target_pairs={{0,6},{1,7},{2,4},{3,5},{4,2},{5,3},{6,0},{7,1},{8,14},{9,15},{10,... | collective-permute-start | bytes 589832 | tf_op jit(solution)/shard_map/ppermute | solution.py:25
  17.4 15.2 %collective-permute-start.9 = (bf16[8,16,768]{2,1,0:T(8,128)(2,1)S(1)}, bf16[8,16,768]{2,1,0:T(8,128)(2,1)S(1)}, u32[]{:S(2)}, u32[]{:S(2)}) collective-permute-start(bf16[8,16,768]{2,1,0:T(8,128)(2,1)S(1)} %collective-permute-done.6), channel_id=1, source_target_pairs={{0,6},{1,7},{2,4},{3,5},{4,2},{5,3},{6,0},{7,1},{8,14},{9,15},{10,... | collective-permute-start | bytes 589832 | tf_op jit(solution)/shard_map/ppermute | solution.py:25
  19.5 12.6 %collective-permute-start.8 = (bf16[8,16,768]{2,1,0:T(8,128)(2,1)S(1)}, bf16[8,16,768]{2,1,0:T(8,128)(2,1)S(1)}, u32[]{:S(2)}, u32[]{:S(2)}) collective-permute-start(bf16[8,16,768]{2,1,0:T(8,128)(2,1)S(1)} %collective-permute-done.6), channel_id=1, source_target_pairs={{0,4},{1,5},{2,6},{3,7},{4,0},{5,1},{6,2},{7,3},{8,12},{9,13},{10,... | collective-permute-start | bytes 589832 | tf_op jit(solution)/shard_map/ppermute | solution.py:25
  20.1 12.0 %collective-permute-start.7 = (bf16[8,16,768]{2,1,0:T(8,128)(2,1)S(1)}, bf16[8,16,768]{2,1,0:T(8,128)(2,1)S(1)}, u32[]{:S(2)}, u32[]{:S(2)}) collective-permute-start(bf16[8,16,768]{2,1,0:T(8,128)(2,1)S(1)} %collective-permute-done.6), channel_id=1, source_target_pairs={{0,2},{1,3},{2,0},{3,1},{4,6},{5,7},{6,4},{7,5},{8,10},{9,11},{10,... | collective-permute-start | bytes 589832 | tf_op jit(solution)/shard_map/ppermute | solution.py:25
  32.6 36.4 %collective-permute-start.14 = (bf16[8,8,16,768]{3,2,1,0:T(8,128)(2,1)S(1)}, bf16[8,8,16,768]{3,2,1,0:T(8,128)(2,1)S(1)}, u32[]{:S(2)}, u32[]{:S(2)}) collective-permute-start(bf16[8,8,16,768]{3,2,1,0:T(8,128)(2,1)S(1)} %bitcast_dynamic-update-slice_fusion.8.src), channel_id=1, source_target_pairs={{0,1},{1,0},{2,3},{3,2},{4,5},{5,4},{6,7},{7,6},{8,9},{9,8},{10,11... | collective-permute-start | bytes 4718600 | tf_op jit(solution)/shard_map/ppermute | solution.py:25
  36.2 28.9 %collective-permute-start.10 = (bf16[768,768]{1,0:T(8,128)(2,1)S(1)}, bf16[768,768]{1,0:T(8,128)(2,1)S(1)}, u32[]{:S(2)}, u32[]{:S(2)}) collective-permute-start(bf16[768,768]{1,0:T(8,128)(2,1)S(1)} %copy-done), channel_id=1, source_target_pairs={{0,16},{16,0},{32,48},{48,32},{64,80},{80,64},{96,112},{112,96},{1... | collective-permute-start | bytes 3538952 | tf_op jit(solution)/shard_map/ppermute | solution.py:25
  38.8 32.0 %collective-permute-start.23 = (bf16[256,768]{1,0:T(8,128)(2,1)S(1)}, bf16[256,768]{1,0:T(8,128)(2,1)S(1)}, u32[]{:S(2)}, u32[]{:S(2)}) collective-permute-start(bf16[256,768]{1,0:T(8,128)(2,1)S(1)} %copy-done.1), channel_id=1, source_target_pairs={{0,96},{16,112},{32,64},{48,80},{64,32},{80,48},{96,0},{112,16},{1... | collective-permute-start | bytes 1179656 | tf_op jit(solution)/shard_map/ppermute | solution.py:25
  40.0 33.5 %collective-permute-start.18 = (bf16[256,768]{1,0:T(8,128)(2,1)S(1)}, bf16[256,768]{1,0:T(8,128)(2,1)S(1)}, u32[]{:S(2)}, u32[]{:S(2)}) collective-permute-start(bf16[256,768]{1,0:T(8,128)(2,1)S(1)} %copy-done.1), channel_id=1, source_target_pairs={{0,16},{16,0},{32,48},{48,32},{64,80},{80,64},{96,112},{112,96},{1... | collective-permute-start | bytes 1179656 | tf_op jit(solution)/shard_map/ppermute | solution.py:25
  66.5 8.2 %collective-permute-start.12 = (bf16[128,768]{1,0:T(8,128)(2,1)S(1)}, bf16[128,768]{1,0:T(8,128)(2,1)S(1)}, u32[]{:S(2)}, u32[]{:S(2)}) collective-permute-start(bf16[128,768]{1,0:T(8,128)(2,1)S(1)} %get-tuple-element.47), channel_id=1, source_target_pairs={{0,32},{16,48},{32,0},{48,16},{64,96},{80,112},{96,64},{112,80},{1... | collective-permute-start | bytes 589832 | tf_op jit(solution)/shard_map/ppermute | solution.py:25
  66.6 18.9 %collective-permute-start.21 = (bf16[256,768]{1,0:T(8,128)(2,1)S(1)}, bf16[256,768]{1,0:T(8,128)(2,1)S(1)}, u32[]{:S(2)}, u32[]{:S(2)}) collective-permute-start(bf16[256,768]{1,0:T(8,128)(2,1)S(1)} %copy-done.1), channel_id=1, source_target_pairs={{0,64},{16,80},{32,96},{48,112},{64,0},{80,16},{96,32},{112,48},{1... | collective-permute-start | bytes 1179656 | tf_op jit(solution)/shard_map/ppermute | solution.py:25
  69.0 19.4 %collective-permute-start.19 = (bf16[256,768]{1,0:T(8,128)(2,1)S(1)}, bf16[256,768]{1,0:T(8,128)(2,1)S(1)}, u32[]{:S(2)}, u32[]{:S(2)}) collective-permute-start(bf16[256,768]{1,0:T(8,128)(2,1)S(1)} %copy-done.1), channel_id=1, source_target_pairs={{0,32},{16,48},{32,0},{48,16},{64,96},{80,112},{96,64},{112,80},{1... | collective-permute-start | bytes 1179656 | tf_op jit(solution)/shard_map/ppermute | solution.py:25
  70.8 14.6 %collective-permute-start.16 = (bf16[128,768]{1,0:T(8,128)(2,1)S(1)}, bf16[128,768]{1,0:T(8,128)(2,1)S(1)}, u32[]{:S(2)}, u32[]{:S(2)}) collective-permute-start(bf16[128,768]{1,0:T(8,128)(2,1)S(1)} %get-tuple-element.51), channel_id=1, source_target_pairs={{0,96},{16,112},{32,64},{48,80},{64,32},{80,48},{96,0},{112,16},{1... | collective-permute-start | bytes 589832 | tf_op jit(solution)/shard_map/ppermute | solution.py:25
  73.5 28.7 %collective-permute-start.24 = (bf16[256,768]{1,0:T(8,128)(2,1)S(1)}, bf16[256,768]{1,0:T(8,128)(2,1)S(1)}, u32[]{:S(2)}, u32[]{:S(2)}) collective-permute-start(bf16[256,768]{1,0:T(8,128)(2,1)S(1)} %collective-permute-done.18.rest_1_), channel_id=1, source_target_pairs={{0,96},{16,112},{32,64},{48,80},{64,32},{80,48},{96,0},{112,16},{1... | collective-permute-start | bytes 1179656 | tf_op jit(solution)/shard_map/ppermute | solution.py:25
  74.8 28.5 %collective-permute-start.22 = (bf16[256,768]{1,0:T(8,128)(2,1)S(1)}, bf16[256,768]{1,0:T(8,128)(2,1)S(1)}, u32[]{:S(2)}, u32[]{:S(2)}) collective-permute-start(bf16[256,768]{1,0:T(8,128)(2,1)S(1)} %collective-permute-done.18.rest_1_), channel_id=1, source_target_pairs={{0,64},{16,80},{32,96},{48,112},{64,0},{80,16},{96,32},{112,48},{1... | collective-permute-start | bytes 1179656 | tf_op jit(solution)/shard_map/ppermute | solution.py:25
  85.4 19.9 %collective-permute-start.20 = (bf16[256,768]{1,0:T(8,128)(2,1)S(1)}, bf16[256,768]{1,0:T(8,128)(2,1)S(1)}, u32[]{:S(2)}, u32[]{:S(2)}) collective-permute-start(bf16[256,768]{1,0:T(8,128)(2,1)S(1)} %collective-permute-done.18.rest_1_), channel_id=1, source_target_pairs={{0,32},{16,48},{32,0},{48,16},{64,96},{80,112},{96,64},{112,80},{1... | collective-permute-start | bytes 1179656 | tf_op jit(solution)/shard_map/ppermute | solution.py:25
  85.5 24.0 %collective-permute-start.11 = (bf16[128,768]{1,0:T(8,128)(2,1)S(1)}, bf16[128,768]{1,0:T(8,128)(2,1)S(1)}, u32[]{:S(2)}, u32[]{:S(2)}) collective-permute-start(bf16[128,768]{1,0:T(8,128)(2,1)S(1)} %get-tuple-element.45), channel_id=1, source_target_pairs={{0,32},{16,48},{32,0},{48,16},{64,96},{80,112},{96,64},{112,80},{1... | collective-permute-start | bytes 589832 | tf_op jit(solution)/shard_map/ppermute | solution.py:25
  88.4 21.1 %collective-permute-start.13 = (bf16[128,768]{1,0:T(8,128)(2,1)S(1)}, bf16[128,768]{1,0:T(8,128)(2,1)S(1)}, u32[]{:S(2)}, u32[]{:S(2)}) collective-permute-start(bf16[128,768]{1,0:T(8,128)(2,1)S(1)} %shard_map.111), channel_id=1, source_target_pairs={{0,96},{16,112},{32,64},{48,80},{64,32},{80,48},{96,0},{112,16},{1... | collective-permute-start | bytes 589832 | tf_op jit(solution)/shard_map/ppermute | solution.py:25
  102.2 7.9 %collective-permute-start.15 = (bf16[128,768]{1,0:T(8,128)(2,1)S(1)}, bf16[128,768]{1,0:T(8,128)(2,1)S(1)}, u32[]{:S(2)}, u32[]{:S(2)}) collective-permute-start(bf16[128,768]{1,0:T(8,128)(2,1)S(1)} %get-tuple-element.49), channel_id=1, source_target_pairs={{0,96},{16,112},{32,64},{48,80},{64,32},{80,48},{96,0},{112,16},{1... | collective-permute-start | bytes 589832 | tf_op jit(solution)/shard_map/ppermute | solution.py:25
  103.3 10.5 %collective-permute-start.17 = (bf16[128,768]{1,0:T(8,128)(2,1)S(1)}, bf16[128,768]{1,0:T(8,128)(2,1)S(1)}, u32[]{:S(2)}, u32[]{:S(2)}) collective-permute-start(bf16[128,768]{1,0:T(8,128)(2,1)S(1)} %shard_map.113), channel_id=1, source_target_pairs={{0,32},{16,48},{32,0},{48,16},{64,96},{80,112},{96,64},{112,80},{1... | collective-permute-start | bytes 589832 | tf_op jit(solution)/shard_map/ppermute | solution.py:25
  124.1 8.2 %collective-permute-start.26 = (bf16[16,6144]{1,0:T(8,128)(2,1)S(1)}, bf16[16,6144]{1,0:T(8,128)(2,1)S(1)}, u32[]{:S(2)}, u32[]{:S(2)}) collective-permute-start(bf16[16,6144]{1,0:T(8,128)(2,1)S(1)} %get-tuple-element.55), channel_id=1, source_target_pairs={{0,2},{1,3},{2,0},{3,1},{4,6},{5,7},{6,4},{7,5},{8,10},{9,11},{10,... | collective-permute-start | bytes 589832 | tf_op jit(solution)/shard_map/ppermute | solution.py:25
  124.8 8.5 %collective-permute-start.27 = (bf16[16,6144]{1,0:T(8,128)(2,1)S(1)}, bf16[16,6144]{1,0:T(8,128)(2,1)S(1)}, u32[]{:S(2)}, u32[]{:S(2)}) collective-permute-start(bf16[16,6144]{1,0:T(8,128)(2,1)S(1)} %get-tuple-element.56), channel_id=1, source_target_pairs={{0,6},{1,7},{2,4},{3,5},{4,2},{5,3},{6,0},{7,1},{8,14},{9,15},{10,... | collective-permute-start | bytes 589832 | tf_op jit(solution)/shard_map/ppermute | solution.py:25
  137.8 8.8 %collective-permute-start.35 = (bf16[16,6144]{1,0:T(8,128)(2,1)S(1)}, bf16[16,6144]{1,0:T(8,128)(2,1)S(1)}, u32[]{:S(2)}, u32[]{:S(2)}) collective-permute-start(bf16[16,6144]{1,0:T(8,128)(2,1)S(1)} %shard_map.119), channel_id=1, source_target_pairs={{0,6},{1,7},{2,4},{3,5},{4,2},{5,3},{6,0},{7,1},{8,14},{9,15},{10,... | collective-permute-start | bytes 589832 | tf_op jit(solution)/shard_map/ppermute | solution.py:25
  141.9 9.8 %collective-permute-start.39 = (bf16[16,6144]{1,0:T(8,128)(2,1)S(1)}, bf16[16,6144]{1,0:T(8,128)(2,1)S(1)}, u32[]{:S(2)}, u32[]{:S(2)}) collective-permute-start(bf16[16,6144]{1,0:T(8,128)(2,1)S(1)} %collective-permute-done.36), channel_id=1, source_target_pairs={{0,6},{1,7},{2,4},{3,5},{4,2},{5,3},{6,0},{7,1},{8,14},{9,15},{10,... | collective-permute-start | bytes 589832 | tf_op jit(solution)/shard_map/ppermute | solution.py:25
  151.8 16.4 %collective-permute-start.40 = (bf16[8,16,6144]{2,1,0:T(8,128)(2,1)S(1)}, bf16[8,16,6144]{2,1,0:T(8,128)(2,1)S(1)}, u32[]{:S(2)}, u32[]{:S(2)}) collective-permute-start(bf16[8,16,6144]{2,1,0:T(8,128)(2,1)S(1)} %bitcast_dynamic-update-slice_fusion.src), channel_id=1, source_target_pairs={{0,1},{1,0},{2,3},{3,2},{4,5},{5,4},{6,7},{7,6},{8,9},{9,8},{10,11... | collective-permute-start | bytes 4718600 | tf_op jit(solution)/shard_map/ppermute | solution.py:25
  171.2 9.3 %collective-permute-start.41 = (bf16[8,16,3072]{2,1,0:T(8,128)(2,1)S(1)}, bf16[8,16,3072]{2,1,0:T(8,128)(2,1)S(1)}, u32[]{:S(2)}, u32[]{:S(2)}) collective-permute-start(bf16[8,16,3072]{2,1,0:T(8,128)(2,1)S(1)} %shard_map.122), channel_id=1, source_target_pairs={{0,1},{1,0},{2,3},{3,2},{4,5},{5,4},{6,7},{7,6},{8,9},{9,8},{10,11... | collective-permute-start | bytes 2359304 | tf_op jit(solution)/shard_map/ppermute | solution.py:25
  175.0 10.0 %collective-permute-start.47 = (bf16[16,3072]{1,0:T(8,128)(2,1)S(1)}, bf16[16,3072]{1,0:T(8,128)(2,1)S(1)}, u32[]{:S(2)}, u32[]{:S(2)}) collective-permute-start(bf16[16,3072]{1,0:T(8,128)(2,1)S(1)} %get-tuple-element.71), channel_id=1, source_target_pairs={{0,12},{1,13},{2,14},{3,15},{4,8},{5,9},{6,10},{7,11},{8,4},{9,5},... | collective-permute-start | bytes 294920 | tf_op jit(solution)/shard_map/ppermute | solution.py:25
  181.8 14.9 %collective-permute-start.42 = (bf16[2,16,3072]{2,1,0:T(8,128)(2,1)S(1)}, bf16[2,16,3072]{2,1,0:T(8,128)(2,1)S(1)}, u32[]{:S(2)}, u32[]{:S(2)}) collective-permute-start(bf16[2,16,3072]{2,1,0:T(8,128)(2,1)S(1)} %pad_maximum_fusion.1), channel_id=1, source_target_pairs={{0,2},{1,3},{2,0},{3,1},{4,6},{5,7},{6,4},{7,5},{8,10},{9,11},{10,... | collective-permute-start | bytes 589832 | tf_op jit(solution)/shard_map/ppermute | solution.py:25
  185.0 11.7 %collective-permute-start.43 = (bf16[2,16,3072]{2,1,0:T(8,128)(2,1)S(1)}, bf16[2,16,3072]{2,1,0:T(8,128)(2,1)S(1)}, u32[]{:S(2)}, u32[]{:S(2)}) collective-permute-start(bf16[2,16,3072]{2,1,0:T(8,128)(2,1)S(1)} %pad_maximum_fusion.2), channel_id=1, source_target_pairs={{0,4},{1,5},{2,6},{3,7},{4,0},{5,1},{6,2},{7,3},{8,12},{9,13},{10,... | collective-permute-start | bytes 589832 | tf_op jit(solution)/shard_map/ppermute | solution.py:25
  185.5 11.2 %collective-permute-start.44 = (bf16[2,16,3072]{2,1,0:T(8,128)(2,1)S(1)}, bf16[2,16,3072]{2,1,0:T(8,128)(2,1)S(1)}, u32[]{:S(2)}, u32[]{:S(2)}) collective-permute-start(bf16[2,16,3072]{2,1,0:T(8,128)(2,1)S(1)} %pad_maximum_fusion.3), channel_id=1, source_target_pairs={{0,6},{1,7},{2,4},{3,5},{4,2},{5,3},{6,0},{7,1},{8,14},{9,15},{10,... | collective-permute-start | bytes 589832 | tf_op jit(solution)/shard_map/ppermute | solution.py:25
  187.4 9.2 %collective-permute-start.50 = (bf16[16,3072]{1,0:T(8,128)(2,1)S(1)}, bf16[16,3072]{1,0:T(8,128)(2,1)S(1)}, u32[]{:S(2)}, u32[]{:S(2)}) collective-permute-start(bf16[16,3072]{1,0:T(8,128)(2,1)S(1)} %get-tuple-element.85), channel_id=1, source_target_pairs={{0,10},{1,11},{2,8},{3,9},{4,14},{5,15},{6,12},{7,13},{8,2},{9,3},... | collective-permute-start | bytes 294920 | tf_op jit(solution)/shard_map/ppermute | solution.py:25
  187.7 8.9 %collective-permute-start.49 = (bf16[16,3072]{1,0:T(8,128)(2,1)S(1)}, bf16[16,3072]{1,0:T(8,128)(2,1)S(1)}, u32[]{:S(2)}, u32[]{:S(2)}) collective-permute-start(bf16[16,3072]{1,0:T(8,128)(2,1)S(1)} %get-tuple-element.86), channel_id=1, source_target_pairs={{0,8},{1,9},{2,10},{3,11},{4,12},{5,13},{6,14},{7,15},{8,0},{9,1},... | collective-permute-start | bytes 294920 | tf_op jit(solution)/shard_map/ppermute | solution.py:25
  206.1 8.0 %collective-permute-start.56 = (bf16[2,16,1024]{2,1,0:T(8,128)(2,1)S(1)}, bf16[2,16,1024]{2,1,0:T(8,128)(2,1)S(1)}, u32[]{:S(2)}, u32[]{:S(2)}) collective-permute-start(bf16[2,16,1024]{2,1,0:T(8,128)(2,1)S(1)} %get-tuple-element.78), channel_id=1, source_target_pairs={{0,6},{1,7},{2,4},{3,5},{4,2},{5,3},{6,0},{7,1},{8,14},{9,15},{10,... | collective-permute-start | bytes 196616 | tf_op jit(solution)/shard_map/ppermute | solution.py:25
  (37 other events, 290.6 us)

commit v4 on v3

--- a/solution.py
+++ b/solution.py
@@ -25,8 +25,8 @@
     return lax.ppermute(value, axis, [(i, i ^ flip) for i in range(size)])
 
 
-def call(kernel, outs, scratch=(), smem=0, n_in=0, limit=8, last=False):
-    kind = jax.ShapeDtypeStruct if last else pltpu.VMEM
+def call(kernel, outs, scratch=(), smem=0, n_in=0, limit=8):
+    kind = pltpu.VMEM
     run = pl.pallas_call(
         kernel,
         out_shape=[kind(s, d) for s, d in outs],
@@ -37,8 +37,8 @@
     )
 
     def go(*args):
-        near = [pltpu.with_memory_space_constraint(a, pltpu.VMEM) for a in args[smem:]]
-        return run(*args[:smem], *near)
+        held = [pltpu.with_memory_space_constraint(a, pltpu.VMEM) for a in args[smem:]]
+        return run(*args[:smem], *held)
 
     return go
 
@@ -52,14 +52,43 @@
         o_ref[ids[0] ^ b] = y[:, b * width:(b + 1) * width]
 
 
-def qkv_kernel(src, w0_ref, w1_ref, *outs):
-    width = w0_ref.shape[0]
+def qkv_kernel(src, wa, wb, va, vb, *outs):
+    half = wa.shape[0]
     for d, o_ref in enumerate(outs):
-        a = src[:, 2 * d].reshape(-1, width)
-        b = src[:, 2 * d + 1].reshape(-1, width)
-        acc = jnp.dot(a, w0_ref[...], preferred_element_type=F32)
-        acc = acc + jnp.dot(b, w1_ref[...], preferred_element_type=F32)
+        acc = None
+        for h, pair in enumerate(((wa, wb), (va, vb))):
+            rows = src[:, 2 * d + h].reshape(-1, 2 * half)
+            for i, w in enumerate(pair):
+                part = jnp.dot(
+                    rows[:, i * half:(i + 1) * half], w[...], preferred_element_type=F32
+                )
+                acc = part if acc is None else acc + part
         o_ref[...] = acc.astype(o_ref.dtype)
+
+
+def cut_kernel(src, *rest):
+    outs, sems = rest[:-1], rest[-1]
+    rows = outs[0].shape[0]
+    copies = [
+        pltpu.make_async_copy(src.at[pl.ds(i * rows, rows)], o, sems.at[i])
+        for i, o in enumerate(outs)
+    ]
+    for copy in copies:
+        copy.start()
+    for copy in copies:
+        copy.wait()
+
+
+def cut(value):
+    half = (value.shape[0] // 2, value.shape[1])
+    return pl.pallas_call(
+        cut_kernel,
+        out_shape=[pltpu.VMEM(half, value.dtype)] * 2,
+        in_specs=[pl.BlockSpec(memory_space=pltpu.HBM)],
+        out_specs=[VM] * 2,
+        scratch_shapes=[pltpu.SemaphoreType.DMA((2,))],
+        compiler_params=pltpu.CompilerParams(vmem_limit_bytes=1 << 20),
+    )(pltpu.with_memory_space_constraint(value, pltpu.HBM))
 
 
 def place(row, section, step):
@@ -145,7 +174,7 @@
 
 def lift_kernel(row, src, din, emb, gain, wqkv, *outs):
     x = src[...].reshape(-1, src.shape[2])
-    near = emb[row:row + x.shape[0], :].astype(F32)
+    near = emb[row:row + 8].reshape(x.shape[0], -1).astype(F32)
     lifted = jnp.dot(x, din[...], preferred_element_type=F32) + near
     scale = lax.rsqrt(jnp.mean(lifted * lifted, axis=-1, keepdims=True) + EPS)
     dn = (lifted * scale * gain[...]).astype(BF)
@@ -160,37 +189,59 @@
                 outs[0][e, :, cut] = y[e * 16:(e + 1) * 16]
 
 
-def fetch_kernel(picks, din, dqkv, table, din_o, dqkv_o, rows_o, near, sems):
-    moves = ((table, near), (din, din_o), (dqkv, dqkv_o))
+def load_kernel(src, dst, sem):
+    copy = pltpu.make_async_copy(src, dst, sem)
+    copy.start()
+    copy.wait()
+
+
+def load(value):
+    return pl.pallas_call(
+        load_kernel,
+        out_shape=pltpu.VMEM(value.shape, value.dtype),
+        in_specs=[pl.BlockSpec(memory_space=pltpu.HBM)],
+        out_specs=VM,
+        scratch_shapes=[pltpu.SemaphoreType.DMA],
+        compiler_params=pltpu.CompilerParams(vmem_limit_bytes=1 << 20),
+    )(pltpu.with_memory_space_constraint(value, pltpu.HBM))
+
+
+def fetch_kernel(ids, picks, dqkv, table, dqkv_o, rows_o, near, sems):
+    moves = ((table, near), (dqkv, dqkv_o))
     copies = [
         pltpu.make_async_copy(src, dst, sems.at[i]) for i, (src, dst) in enumerate(moves)
     ]
     for copy in copies:
         copy.start()
+    count = near.shape[0]
+    entry = lax.broadcasted_iota(jnp.int32, (count, picks.shape[1]), 0)
+    hot = jnp.where(entry == picks[...], 1.0, 0.0).astype(BF)
     copies[0].wait()
-    count = near.shape[0]
-    lane = lax.broadcasted_iota(jnp.int32, (picks.shape[0], count), 1)
-    hot = jnp.where(lane == picks[...], 1.0, 0.0).astype(BF)
-    rows_o[...] = jnp.dot(hot, near[...], preferred_element_type=F32).astype(BF)
+    rows = lax.dot_general(
+        hot, near[...], (((0,), (0,)), ((), ())), preferred_element_type=F32
+    ).astype(BF)
+    step = rows_o.shape[1]
+    for b in range(rows_o.shape[0]):
+        flip = ids[1] ^ b
+        rows_o[8 * (flip % 2) + flip // 2] = rows[b * step:(b + 1) * step]
     copies[1].wait()
-    copies[2].wait()
-
-
-def fetch(picks, din, dqkv, table):
+
+
+def fetch(ids, picks, dqkv, table):
     far = pl.BlockSpec(memory_space=pltpu.HBM)
-    shapes = [din.shape, dqkv.shape, (picks.shape[0], table.shape[1])]
-    big = [pltpu.with_memory_space_constraint(a, pltpu.HBM) for a in (din, dqkv, table)]
+    shapes = [dqkv.shape, (16, picks.shape[1] // 16, table.shape[1])]
+    big = [pltpu.with_memory_space_constraint(a, pltpu.HBM) for a in (dqkv, table)]
     return pl.pallas_call(
         fetch_kernel,
         out_shape=[pltpu.VMEM(s, BF) for s in shapes],
-        in_specs=[VM, far, far, far],
-        out_specs=[VM] * 3,
-        scratch_shapes=[pltpu.VMEM(table.shape, BF), pltpu.SemaphoreType.DMA((3,))],
+        in_specs=[SM, VM, far, far],
+        out_specs=[VM] * 2,
+        scratch_shapes=[pltpu.VMEM(table.shape, BF), pltpu.SemaphoreType.DMA((2,))],
         compiler_params=pltpu.CompilerParams(vmem_limit_bytes=14 << 20),
-    )(pltpu.with_memory_space_constraint(picks, pltpu.VMEM), *big)
-
-
-def depth_first(ids, low, high, *rest):
+    )(ids, pltpu.with_memory_space_constraint(picks, pltpu.VMEM), *big)
+
+
+def depth_kernel(ids, low, high, *rest):
     o_ref, z = rest[11:13]
     z[0:16, :] = low[...]
     z[128:144, :] = high[...]
@@ -202,31 +253,23 @@
         at = (i + 4) * 16
         z[at:at + 16, :] = rest[3 + i][...]
         z[128 + at:144 + at, :] = rest[7 + i][...]
-    depth_rows(ids, z, 128, o_ref)
-
-
-def depth_second(ids, z, o_ref):
-    depth_rows(ids, z, 0, o_ref)
-
-
-def depth_rows(ids, z, at, o_ref):
     section = ids[1]
-    rows = at + lax.broadcasted_iota(jnp.int32, (128, 1), 0)
+    rows = lax.broadcasted_iota(jnp.int32, (256, 1), 0)
     cols = lax.broadcasted_iota(jnp.int32, (1, 256), 1)
     rpos = place(rows, section, 16) // 16
     cpos = place(cols, section, 16) // 16
     keep = (cpos <= rpos) & (rows % 16 == cols % 16)
     bias = jnp.where(keep, 0.0, NEG)
-    low = lax.broadcasted_iota(jnp.int32, (128, 2 * DHEAD), 1) < DHEAD
+    first = lax.broadcasted_iota(jnp.int32, (256, 2 * DHEAD), 1) < DHEAD
     inner = z.shape[1] // 3
     for pair in range(inner // (2 * DHEAD)):
         base = pair * 2 * DHEAD
-        q = z[at:at + 128, base:base + 2 * DHEAD]
+        q = z[:, base:base + 2 * DHEAD]
         k = z[:, inner + base:inner + base + 2 * DHEAD]
         v = z[:, 2 * inner + base:2 * inner + base + 2 * DHEAD]
         got = []
         for side in range(2):
-            mask = low if side == 0 else jnp.logical_not(low)
+            mask = first if side == 0 else jnp.logical_not(first)
             qs = jnp.where(mask, q, jnp.zeros_like(q))
             s = lax.dot_general(
                 qs, k, (((1,), (1,)), ((), ())), preferred_element_type=F32
@@ -237,21 +280,10 @@
             total = jnp.sum(e, axis=-1, keepdims=True)
             o = jnp.dot(e.astype(BF), v, preferred_element_type=F32)
             got.append(o / total)
-        res = jnp.where(low, got[0], got[1]).astype(BF)
-        o_ref[:, :, base:base + 2 * DHEAD] = res.reshape(8, 16, 2 * DHEAD)
-
-
-def join_kernel(a_ref, b_ref, *outs):
-    for e, o_ref in enumerate(outs):
-        o_ref[0] = a_ref[e]
-        o_ref[1] = b_ref[e]
-
-
-def final_kernel(ids, *rest):
-    o_ref = rest[8]
-    for e in range(8):
-        o_ref[ids[1] ^ (2 * e)] = rest[e][0]
-        o_ref[ids[1] ^ (2 * e + 1)] = rest[e][1]
+        res = jnp.where(first, got[0], got[1]).astype(BF)
+        for m in range(16):
+            to = section ^ (2 * (m % 8) + m // 8)
+            o_ref[to, :, base:base + 2 * DHEAD] = res[m * 16:(m + 1) * 16]
 
 
 def add_kernel(*refs):
@@ -293,19 +325,23 @@
         ids, mine, t_gain[None]
     )[0]
     near = fs(w_out, 1)
-    w_other = fs(w_qkv, 1)
+    wa, wb = cut(w_qkv)
+    va = fs(wa, 1)
+    vb = fs(wb, 1)
     local = [rel[0:2]] + [fs(rel[2 * d:2 * d + 2], 2 * d) for d in (1, 2, 3)]
     local = jnp.concatenate(local, axis=0)
     wo_even = [w_out] + [fs(w_out, 2 * d) for d in (1, 2, 3)]
-    wo_odd = [near] + [fs(near, 2 * d) for d in (1, 2, 3)]
+    odd1, odd3 = fs(near, 2), fs(near, 6)
+    odd2 = fs(wo_even[2], 1)
+    wo_odd = [near, odd1, odd2, odd3]
     wo = [w for pair in zip(wo_even, wo_odd) for w in pair]
     even = jnp.stack(gather(local, True))
     odd = cb(even, 1)
     cols = w_qkv.shape[1]
 
     def project(src, kinds):
-        return call(qkv_kernel, [((128, cols), k) for k in kinds], n_in=3)(
-            src, w_qkv, w_other
+        return call(qkv_kernel, [((128, cols), k) for k in kinds], n_in=5)(
+            src, wa, wb, va, vb
         )
 
     a0, a1, a2, a3 = project(even, (F32, BF, BF, F32))
@@ -344,10 +380,8 @@
     even = jnp.stack(gather(hn))
     odd = cb(even, 1)
 
-    order = jnp.concatenate([2 * jnp.arange(8), 2 * jnp.arange(8) + 1]).astype(jnp.int32)
-    mine_at = (jnp.arange(16, dtype=jnp.int32)[None, :] == (c ^ order)[:, None])[:, :, None]
-    picks = jnp.sum(jnp.where(mine_at, tokens[0, 0].reshape(1, 16, 16), 0), axis=1)
-    din, dqkv, emb = fetch(picks.reshape(256, 1), d_in[0], d_qkv[0], d_embed[0])
+    din = load(d_in[0])
+    dqkv, emb = fetch(ids, tokens[0], d_qkv[0], d_embed[0])
     inner = d_in.shape[2]
 
     def lift(src, row, outs):
@@ -356,26 +390,21 @@
         )
 
     low = lift(even, 0, [((16, 3 * inner), BF)] * 8)
-    high = lift(odd, 128, [((8, 16, 3 * inner), BF)])[0]
+    high = lift(odd, 8, [((8, 16, 3 * inner), BF)])[0]
     high = cb(high, 1)
     got = {e: cb(low[e], 2 * e) for e in (5, 7)}
     got.update({e: cb(low[e], 2 * e) for e in (6, 4)})
     both = [cb(jnp.stack([low[e], high[e]]), 2 * e) for e in (2, 1, 3)]
     deep = [cb(high[e], 2 * e) for e in (4, 5, 6, 7)]
     both = [both[1], both[0], both[2]]
-    other, z = call(
-        depth_first,
-        [((8, 16, inner), BF), ((256, 3 * inner), BF)],
+    outs = call(
+        depth_kernel,
+        [((16, 16, inner), BF)],
+        scratch=[pltpu.VMEM((256, 3 * inner), BF)],
         smem=1,
         n_in=14,
-    )(ids, low[0], high[0], *both, *[got[e] for e in (4, 5, 6, 7)], *deep)
-    other = cb(other, 1)
-    outs = call(depth_second, [((8, 16, inner), BF)], smem=1, n_in=2)(ids, z)[0]
-    outs = call(join_kernel, [((2, 16, inner), BF)] * 8, n_in=2)(outs, other)
-    pieces = [outs[0]] + [cb(outs[e], 2 * e) for e in range(1, 8)]
-    out = call(final_kernel, [((16, 16, inner), BF)], smem=1, n_in=9, last=True)(
-        ids, *pieces
-    )[0]
+    )(ids, low[0], high[0], *both, *[got[e] for e in (4, 5, 6, 7)], *deep)[0]
+    out = lax.all_to_all(outs, "cb", 0, 0, tiled=True)
     return out.reshape(1, 1, 256, inner)
 
 

time: 220 us -> 203 us (0.923)
  waiting for transfers between devices: 106 us -> 82.4 us
  blocking collectives: 0 us -> 15.9 us
  starting transfers between devices: 80.7 us -> 73 us
    ppermute x61 -> x54, waiting for transfers between devices: 106 us -> 82.4 us  [swap(): return lax.ppermute(value, axis, [(i, i ^ flip) for i in range(size)])]
    all_to_all x0 -> x1, blocking collectives: none -> 15.9 us  [work(): out = lax.all_to_all(outs, 'cb', 0, 0, tiled=True)]
    ppermute x61 -> x54, starting transfers between devices: 80.7 us -> 73 us  [swap(): return lax.ppermute(value, axis, [(i, i ^ flip) for i in range(size)])]
    pallas_call x17 -> x16, Pallas kernels: 18.6 us -> 22.8 us  [the longest x14 16.9 us: go(): return run(*args[:smem], *held)]
    pallas_call x1, Pallas kernels: 7.67 us -> 4.62 us  [fetch(): pl.pallas_call(fetch_kernel, out_shape=[pltpu.VMEM(s, BF) for s in shapes...]
  transfers between devices with their start and end apart: 61 -> 54, of which waited for: 30 -> 27; matrix products, arithmetic and copies ran while one was open for 1% -> 0% of each run, Pallas kernels for 7% -> 9%
where the time goes in v4:
time: 203 us
  waiting for transfers between devices  82.4 us (41%)
  starting transfers between devices  73 us (36%)
  Pallas kernels  27.4 us (13%)
  blocking collectives  15.9 us (8%)
  local copies, waits for them, and re-layouts  2.77 us (1%)
    ppermute x54, waiting for transfers between devices, swap(): return lax.ppermute(value, axis, [(i, i ^ flip) for i in range(size)])  82.4 us
    ppermute x54, starting transfers between devices, swap(): return lax.ppermute(value, axis, [(i, i ^ flip) for i in range(size)])  73 us
    pallas_call x14, Pallas kernels, go(): return run(*args[:smem], *held)  16.9 us
    all_to_all x1, blocking collectives, work(): out = lax.all_to_all(outs, 'cb', 0, 0, tiled=True)  15.9 us
    pallas_call x1, Pallas kernels, fetch(): pl.pallas_call(fetch_kernel, out_shape=[pltpu.VMEM(s, BF) for s in shapes...  4.62 us
    pallas_call x1, Pallas kernels, load(): pl.pallas_call(load_kernel, out_shape=pltpu.VMEM(value.shape, value.dtype...  4.6 us
  transfers between devices with their start and end apart: 54, of which 27 were waited for; matrix products, arithmetic and copies ran while one was open for 0% of the time, Pallas kernels for 9%

profile of v4, /device:TPU:1, one launch (start us, length us, event | category | flops | bytes accessed | tf_op | source)
XLA Modules:
  0.0 202.7 jit_solution(9079021659237291557)
XLA Ops:
  3.2 4.7 %collective-permute-start.2 = (bf16[2,16,768]{2,1,0:T(8,128)(2,1)S(1)}, bf16[2,16,768]{2,1,0:T(8,128)(2,1)S(1)}, u32[]{:S(2)}, u32[]{:S(2)}) collective-permute-start(bf16[2,16,768]{2,1,0:T(8,128)(2,1)S(1)} %get-tuple-element.74), channel_id=1, source_target_pairs={{0,96},{16,112},{32,64},{48,80},{64,32},{80,48},{96,0},{112,16},{1... | collective-permute-start | bytes 147464 | tf_op jit(solution)/shard_map/ppermute | solution.py:25
  9.3 3.0 %collective-permute-done.1 = bf16[2,16,768]{2,1,0:T(8,128)(2,1)S(1)} collective-permute-done((bf16[2,16,768]{2,1,0:T(8,128)(2,1)S(1)}, bf16[2,16,768]{2,1,0:T(8,128)(2,1)S(1)}, u32[]{:S(2)}, u32[]{:S(2)}) %collective-permute-start.1) | collective-permute-done | bytes 49184 | tf_op jit(solution)/shard_map/ppermute | solution.py:25
  17.4 2.1 %collective-permute-start.9 = (bf16[8,16,768]{2,1,0:T(8,128)(2,1)S(1)}, bf16[8,16,768]{2,1,0:T(8,128)(2,1)S(1)}, u32[]{:S(2)}, u32[]{:S(2)}) collective-permute-start(bf16[8,16,768]{2,1,0:T(8,128)(2,1)S(1)} %collective-permute-done.6), channel_id=1, source_target_pairs={{0,6},{1,7},{2,4},{3,5},{4,2},{5,3},{6,0},{7,1},{8,14},{9,15},{10,... | collective-permute-start | bytes 589832 | tf_op jit(solution)/shard_map/ppermute | solution.py:25
  20.7 3.6 %collective-permute-done.4 = bf16[8,16,768]{2,1,0:T(8,128)(2,1)S(1)} collective-permute-done((bf16[8,16,768]{2,1,0:T(8,128)(2,1)S(1)}, bf16[8,16,768]{2,1,0:T(8,128)(2,1)S(1)}, u32[]{:S(2)}, u32[]{:S(2)}) %collective-permute-start.4) | collective-permute-done | bytes 196640 | tf_op jit(solution)/shard_map/ppermute | solution.py:25
  24.4 7.7 %collective-permute-done.7 = bf16[8,16,768]{2,1,0:T(8,128)(2,1)S(1)} collective-permute-done((bf16[8,16,768]{2,1,0:T(8,128)(2,1)S(1)}, bf16[8,16,768]{2,1,0:T(8,128)(2,1)S(1)}, u32[]{:S(2)}, u32[]{:S(2)}) %collective-permute-start.7) | collective-permute-done | bytes 196640 | tf_op jit(solution)/shard_map/ppermute | solution.py:25
  32.6 3.6 %collective-permute-start.15 = (bf16[8,8,16,768]{3,2,1,0:T(8,128)(2,1)S(1)}, bf16[8,8,16,768]{3,2,1,0:T(8,128)(2,1)S(1)}, u32[]{:S(2)}, u32[]{:S(2)}) collective-permute-start(bf16[8,8,16,768]{3,2,1,0:T(8,128)(2,1)S(1)} %bitcast_dynamic-update-slice_fusion.8.src), channel_id=1, source_target_pairs={{0,1},{1,0},{2,3},{3,2},{4,5},{5,4},{6,7},{7,6},{8,9},{9,8},{10,11... | collective-permute-start | bytes 4718600 | tf_op jit(solution)/shard_map/ppermute | solution.py:25
  37.4 2.7 %collective-permute-start.10 = (bf16[384,768]{1,0:T(8,128)(2,1)S(1)}, bf16[384,768]{1,0:T(8,128)(2,1)S(1)}, u32[]{:S(2)}, u32[]{:S(2)}) collective-permute-start(bf16[384,768]{1,0:T(8,128)(2,1)S(1)} %get-tuple-element.35.wa), channel_id=1, source_target_pairs={{0,16},{16,0},{32,48},{48,32},{64,80},{80,64},{96,112},{112,96},{1... | collective-permute-start | bytes 1769480 | tf_op jit(solution)/shard_map/ppermute | solution.py:25
  42.4 2.6 %collective-permute-start.19 = (bf16[256,768]{1,0:T(8,128)(2,1)S(1)}, bf16[256,768]{1,0:T(8,128)(2,1)S(1)}, u32[]{:S(2)}, u32[]{:S(2)}) collective-permute-start(bf16[256,768]{1,0:T(8,128)(2,1)S(1)} %copy-done), channel_id=1, source_target_pairs={{0,16},{16,0},{32,48},{48,32},{64,80},{80,64},{96,112},{112,96},{1... | collective-permute-start | bytes 1179656 | tf_op jit(solution)/shard_map/ppermute | solution.py:25
  45.1 8.8 %collective-permute-done.10.va = bf16[384,768]{1,0:T(8,128)(2,1)S(1)} collective-permute-done((bf16[384,768]{1,0:T(8,128)(2,1)S(1)}, bf16[384,768]{1,0:T(8,128)(2,1)S(1)}, u32[]{:S(2)}, u32[]{:S(2)}) %collective-permute-start.10) | collective-permute-done | bytes 589856 | tf_op jit(solution)/shard_map/ppermute | solution.py:25
  53.9 12.6 %collective-permute-done.11.vb = bf16[384,768]{1,0:T(8,128)(2,1)S(1)} collective-permute-done((bf16[384,768]{1,0:T(8,128)(2,1)S(1)}, bf16[384,768]{1,0:T(8,128)(2,1)S(1)}, u32[]{:S(2)}, u32[]{:S(2)}) %collective-permute-start.11) | collective-permute-done | bytes 589856 | tf_op jit(solution)/shard_map/ppermute | solution.py:25
  68.4 2.2 %collective-permute-start.24 = (bf16[256,768]{1,0:T(8,128)(2,1)S(1)}, bf16[256,768]{1,0:T(8,128)(2,1)S(1)}, u32[]{:S(2)}, u32[]{:S(2)}) collective-permute-start(bf16[256,768]{1,0:T(8,128)(2,1)S(1)} %copy-done), channel_id=1, source_target_pairs={{0,96},{16,112},{32,64},{48,80},{64,32},{80,48},{96,0},{112,16},{1... | collective-permute-start | bytes 1179656 | tf_op jit(solution)/shard_map/ppermute | solution.py:25
  74.9 2.6 %collective-permute-start.23 = (bf16[256,768]{1,0:T(8,128)(2,1)S(1)}, bf16[256,768]{1,0:T(8,128)(2,1)S(1)}, u32[]{:S(2)}, u32[]{:S(2)}) collective-permute-start(bf16[256,768]{1,0:T(8,128)(2,1)S(1)} %collective-permute-done.22.rest_4_), channel_id=1, source_target_pairs={{0,16},{16,0},{32,48},{48,32},{64,80},{80,64},{96,112},{112,96},{1... | collective-permute-start | bytes 1179656 | tf_op jit(solution)/shard_map/ppermute | solution.py:25
  78.8 4.4 %collective-permute-done.17.refs_1_ = bf16[128,768]{1,0:T(8,128)(2,1)S(1)} collective-permute-done((bf16[128,768]{1,0:T(8,128)(2,1)S(1)}, bf16[128,768]{1,0:T(8,128)(2,1)S(1)}, u32[]{:S(2)}, u32[]{:S(2)}) %collective-permute-start.17) | collective-permute-done | bytes 196640 | tf_op jit(solution)/shard_map/ppermute | solution.py:25
  87.5 4.1 %collective-permute-done.25.rest_7_ = bf16[256,768]{1,0:T(8,128)(2,1)S(1)} collective-permute-done((bf16[256,768]{1,0:T(8,128)(2,1)S(1)}, bf16[256,768]{1,0:T(8,128)(2,1)S(1)}, u32[]{:S(2)}, u32[]{:S(2)}) %collective-permute-start.25) | collective-permute-done | bytes 393248 | tf_op jit(solution)/shard_map/ppermute | solution.py:25
  91.6 2.4 %collective-permute-done.12.a1 = bf16[128,768]{1,0:T(8,128)(2,1)S(1)} collective-permute-done((bf16[128,768]{1,0:T(8,128)(2,1)S(1)}, bf16[128,768]{1,0:T(8,128)(2,1)S(1)}, u32[]{:S(2)}, u32[]{:S(2)}) %collective-permute-start.12) | collective-permute-done | bytes 196640 | tf_op jit(solution)/shard_map/ppermute | solution.py:25
  95.8 4.2 %collective-permute-done.16.b1 = bf16[128,768]{1,0:T(8,128)(2,1)S(1)} collective-permute-done((bf16[128,768]{1,0:T(8,128)(2,1)S(1)}, bf16[128,768]{1,0:T(8,128)(2,1)S(1)}, u32[]{:S(2)}, u32[]{:S(2)}) %collective-permute-start.16) | collective-permute-done | bytes 196640 | tf_op jit(solution)/shard_map/ppermute | solution.py:25
  102.2 3.2 %collective-permute-start.26 = (bf16[128,6144]{1,0:T(8,128)(2,1)S(1)}, bf16[128,6144]{1,0:T(8,128)(2,1)S(1)}, u32[]{:S(2)}, u32[]{:S(2)}) collective-permute-start(bf16[128,6144]{1,0:T(8,128)(2,1)S(1)} %get-tuple-element.46), channel_id=1, source_target_pairs={{0,1},{1,0},{2,3},{3,2},{4,5},{5,4},{6,7},{7,6},{8,9},{9,8},{10,11... | collective-permute-start | bytes 4718600 | tf_op jit(solution)/shard_map/ppermute | solution.py:25
  106.0 2.4 %collective-permute-done.26.b_ref = bf16[128,6144]{1,0:T(8,128)(2,1)S(1)} collective-permute-done((bf16[128,6144]{1,0:T(8,128)(2,1)S(1)}, bf16[128,6144]{1,0:T(8,128)(2,1)S(1)}, u32[]{:S(2)}, u32[]{:S(2)}) %collective-permute-start.26) | collective-permute-done | bytes 1572896 | tf_op jit(solution)/shard_map/ppermute | solution.py:25
  120.9 2.3 %collective-permute-done.33.rest_4_ = bf16[16,6144]{1,0:T(8,128)(2,1)S(1)} collective-permute-done((bf16[16,6144]{1,0:T(8,128)(2,1)S(1)}, bf16[16,6144]{1,0:T(8,128)(2,1)S(1)}, u32[]{:S(2)}, u32[]{:S(2)}) %collective-permute-start.33) | collective-permute-done | bytes 196640 | tf_op jit(solution)/shard_map/ppermute | solution.py:25
  130.1 2.7 %collective-permute-done.35 = bf16[16,6144]{1,0:T(8,128)(2,1)S(1)} collective-permute-done((bf16[16,6144]{1,0:T(8,128)(2,1)S(1)}, bf16[16,6144]{1,0:T(8,128)(2,1)S(1)}, u32[]{:S(2)}, u32[]{:S(2)}) %collective-permute-start.35) | collective-permute-done | bytes 196640 | tf_op jit(solution)/shard_map/ppermute | solution.py:25
  133.5 3.4 %collective-permute-done.38 = bf16[16,6144]{1,0:T(8,128)(2,1)S(1)} collective-permute-done((bf16[16,6144]{1,0:T(8,128)(2,1)S(1)}, bf16[16,6144]{1,0:T(8,128)(2,1)S(1)}, u32[]{:S(2)}, u32[]{:S(2)}) %collective-permute-start.38) | collective-permute-done | bytes 196640 | tf_op jit(solution)/shard_map/ppermute | solution.py:25
  138.6 7.1 %collective-permute-start.41 = (bf16[8,16,6144]{2,1,0:T(8,128)(2,1)S(1)}, bf16[8,16,6144]{2,1,0:T(8,128)(2,1)S(1)}, u32[]{:S(2)}, u32[]{:S(2)}) collective-permute-start(bf16[8,16,6144]{2,1,0:T(8,128)(2,1)S(1)} %bitcast_dynamic-update-slice_fusion.src), channel_id=1, source_target_pairs={{0,1},{1,0},{2,3},{3,2},{4,5},{5,4},{6,7},{7,6},{8,9},{9,8},{10,11... | collective-permute-start | bytes 4718600 | tf_op jit(solution)/shard_map/ppermute | solution.py:25
  145.7 4.6 %shard_map.121.din = bf16[6144,1024]{1,0:T(8,128)(2,1)S(1)} custom-call(bf16[6144,1024]{1,0:T(8,128)(2,1)} %bitcast.63), custom_call_target="tpu_custom_call" | custom-call | tf_op jit(solution)/shard_map/pallas_call | solution.py:199
  150.3 4.6 %shard_map.122 = (bf16[1024,3072]{1,0:T(8,128)(2,1)S(1)}, bf16[16,16,1024]{2,1,0:T(8,128)(2,1)S(1)}) custom-call(s32[3]{0:T(128)S(1)} %pad_add_fusion.ids, s32[1,256]{1,0:T(1,128)S(1)} %bitcast.62, bf16[1024,3072]{1,0:T(8,128)(2,1)} %bitcast.64, bf16[2048,1024]{1,0:T(8,128)(2,1)} %bitcast.65), custom_call_target="tpu_custom_call" | custom-call | tf_op jit(solution)/shard_map/pallas_call | solution.py:234
  154.9 3.0 %shard_map.124 = bf16[8,16,3072]{2,1,0:T(8,128)(2,1)S(1)} custom-call(bf16[8,16,6144]{2,1,0:T(8,128)(2,1)S(1)} %collective-permute-done.41.src, bf16[6144,1024]{1,0:T(8,128)(2,1)S(1)} %shard_map.121.din, bf16[16,16,1024]{2,1,0:T(8,128)(2,1)S(1)} %get-tuple-element.55.emb, f32[1,1024]{1,0:T(1,128)S(1)} %copy-done.5, bf16[1024,3072]{1,0:T(8,128)(2,1)S(1)} %get-tuple-element.56.wqkv), custom_call_target="tpu_custom_call" | custom-call | tf_op jit(solution)/shard_map/pallas_call | solution.py:41
  158.2 3.0 %shard_map.123 = (bf16[16,3072]{1,0:T(8,128)(2,1)S(1)}, bf16[16,3072]{1,0:T(8,128)(2,1)S(1)}, bf16[16,3072]{1,0:T(8,128)(2,1)S(1)}, bf16[16,3072]{1,0:T(8,128)(2...) custom-call(bf16[8,16,6144]{2,1,0:T(8,128)(2,1)S(1)} %bitcast_dynami, ...), custom_call_target="tpu_custom_call" | custom-call | tf_op jit(solution)/shard_map/pallas_call | solution.py:41
  161.7 2.9 %collective-permute-start.48 = (bf16[16,3072]{1,0:T(8,128)(2,1)S(1)}, bf16[16,3072]{1,0:T(8,128)(2,1)S(1)}, u32[]{:S(2)}, u32[]{:S(2)}) collective-permute-start(bf16[16,3072]{1,0:T(8,128)(2,1)S(1)} %get-tuple-element.63), channel_id=1, source_target_pairs={{0,12},{1,13},{2,14},{3,15},{4,8},{5,9},{6,10},{7,11},{8,4},{9,5},... | collective-permute-start | bytes 294920 | tf_op jit(solution)/shard_map/ppermute | solution.py:25
  164.6 2.6 %collective-permute-start.49 = (bf16[16,3072]{1,0:T(8,128)(2,1)S(1)}, bf16[16,3072]{1,0:T(8,128)(2,1)S(1)}, u32[]{:S(2)}, u32[]{:S(2)}) collective-permute-start(bf16[16,3072]{1,0:T(8,128)(2,1)S(1)} %get-tuple-element.64), channel_id=1, source_target_pairs={{0,14},{1,15},{2,12},{3,13},{4,10},{5,11},{6,8},{7,9},{8,6},{9,7},... | collective-permute-start | bytes 294920 | tf_op jit(solution)/shard_map/ppermute | solution.py:25
  168.5 3.2 %collective-permute-start.43 = (bf16[2,16,3072]{2,1,0:T(8,128)(2,1)S(1)}, bf16[2,16,3072]{2,1,0:T(8,128)(2,1)S(1)}, u32[]{:S(2)}, u32[]{:S(2)}) collective-permute-start(bf16[2,16,3072]{2,1,0:T(8,128)(2,1)S(1)} %pad_maximum_fusion.1), channel_id=1, source_target_pairs={{0,2},{1,3},{2,0},{3,1},{4,6},{5,7},{6,4},{7,5},{8,10},{9,11},{10,... | collective-permute-start | bytes 589832 | tf_op jit(solution)/shard_map/ppermute | solution.py:25
  175.5 7.8 %collective-permute-done.51.rest_8_ = bf16[16,3072]{1,0:T(8,128)(2,1)S(1)} collective-permute-done((bf16[16,3072]{1,0:T(8,128)(2,1)S(1)}, bf16[16,3072]{1,0:T(8,128)(2,1)S(1)}, u32[]{:S(2)}, u32[]{:S(2)}) %collective-permute-start.51) | collective-permute-done | bytes 98336 | tf_op jit(solution)/shard_map/ppermute | solution.py:25
  183.4 2.6 %shard_map.125 = bf16[16,16,1024]{2,1,0:T(8,128)(2,1)S(1)} custom-call(s32[3]{0:T(128)S(1)} %pad_add_fusion.ids, bf16[16,3072]{1,0:T(8,128)(2,1)S(1)} %get-tuple-element.57.low, bf16[16,3072]{1,0:T(8,128)(2,1)S(1)} %get-tuple-element.72.high, bf16[2,16,3072]{2,1,0:T(8,128)(2,1)S(1)} %collective-permute-done.43.rest_0_, ...), custom_call_target="tpu_custom_call" | custom-call | tf_op jit(solution)/shard_map/pallas_call | solution.py:41
  186.0 15.9 %all_to_all.5 = bf16[16,16,1024]{2,1,0:T(8,128)(2,1)S(1)} all-to-all(bf16[16,16,1024]{2,1,0:T(8,128)(2,1)S(1)} %shard_map.125), channel_id=1, replica_groups=mesh['fsdp'=8,'cb'=16] {'cb'}, dimensions={0} | all-to-all | bytes 1048576 | tf_op jit(solution)/shard_map/all_to_all | solution.py:407
  (132 shorter events, 58.9 us)
Async XLA Ops:
  14.9 9.5 %collective-permute-start.5 = (bf16[8,16,768]{2,1,0:T(8,128)(2,1)S(1)}, bf16[8,16,768]{2,1,0:T(8,128)(2,1)S(1)}, u32[]{:S(2)}, u32[]{:S(2)}) collective-permute-start(bf16[8,16,768]{2,1,0:T(8,128)(2,1)S(1)} %pad_maximum_fusion), channel_id=1, source_target_pairs={{0,6},{1,7},{2,4},{3,5},{4,2},{5,3},{6,0},{7,1},{8,14},{9,15},{10,... | collective-permute-start | bytes 589832 | tf_op jit(solution)/shard_map/ppermute | solution.py:25
  17.4 15.2 %collective-permute-start.9 = (bf16[8,16,768]{2,1,0:T(8,128)(2,1)S(1)}, bf16[8,16,768]{2,1,0:T(8,128)(2,1)S(1)}, u32[]{:S(2)}, u32[]{:S(2)}) collective-permute-start(bf16[8,16,768]{2,1,0:T(8,128)(2,1)S(1)} %collective-permute-done.6), channel_id=1, source_target_pairs={{0,6},{1,7},{2,4},{3,5},{4,2},{5,3},{6,0},{7,1},{8,14},{9,15},{10,... | collective-permute-start | bytes 589832 | tf_op jit(solution)/shard_map/ppermute | solution.py:25
  19.5 12.6 %collective-permute-start.8 = (bf16[8,16,768]{2,1,0:T(8,128)(2,1)S(1)}, bf16[8,16,768]{2,1,0:T(8,128)(2,1)S(1)}, u32[]{:S(2)}, u32[]{:S(2)}) collective-permute-start(bf16[8,16,768]{2,1,0:T(8,128)(2,1)S(1)} %collective-permute-done.6), channel_id=1, source_target_pairs={{0,4},{1,5},{2,6},{3,7},{4,0},{5,1},{6,2},{7,3},{8,12},{9,13},{10,... | collective-permute-start | bytes 589832 | tf_op jit(solution)/shard_map/ppermute | solution.py:25
  20.0 12.0 %collective-permute-start.7 = (bf16[8,16,768]{2,1,0:T(8,128)(2,1)S(1)}, bf16[8,16,768]{2,1,0:T(8,128)(2,1)S(1)}, u32[]{:S(2)}, u32[]{:S(2)}) collective-permute-start(bf16[8,16,768]{2,1,0:T(8,128)(2,1)S(1)} %collective-permute-done.6), channel_id=1, source_target_pairs={{0,2},{1,3},{2,0},{3,1},{4,6},{5,7},{6,4},{7,5},{8,10},{9,11},{10,... | collective-permute-start | bytes 589832 | tf_op jit(solution)/shard_map/ppermute | solution.py:25
  32.6 38.1 %collective-permute-start.15 = (bf16[8,8,16,768]{3,2,1,0:T(8,128)(2,1)S(1)}, bf16[8,8,16,768]{3,2,1,0:T(8,128)(2,1)S(1)}, u32[]{:S(2)}, u32[]{:S(2)}) collective-permute-start(bf16[8,8,16,768]{3,2,1,0:T(8,128)(2,1)S(1)} %bitcast_dynamic-update-slice_fusion.8.src), channel_id=1, source_target_pairs={{0,1},{1,0},{2,3},{3,2},{4,5},{5,4},{6,7},{7,6},{8,9},{9,8},{10,11... | collective-permute-start | bytes 4718600 | tf_op jit(solution)/shard_map/ppermute | solution.py:25
  37.4 16.4 %collective-permute-start.10 = (bf16[384,768]{1,0:T(8,128)(2,1)S(1)}, bf16[384,768]{1,0:T(8,128)(2,1)S(1)}, u32[]{:S(2)}, u32[]{:S(2)}) collective-permute-start(bf16[384,768]{1,0:T(8,128)(2,1)S(1)} %get-tuple-element.35.wa), channel_id=1, source_target_pairs={{0,16},{16,0},{32,48},{48,32},{64,80},{80,64},{96,112},{112,96},{1... | collective-permute-start | bytes 1769480 | tf_op jit(solution)/shard_map/ppermute | solution.py:25
  40.1 26.4 %collective-permute-start.11 = (bf16[384,768]{1,0:T(8,128)(2,1)S(1)}, bf16[384,768]{1,0:T(8,128)(2,1)S(1)}, u32[]{:S(2)}, u32[]{:S(2)}) collective-permute-start(bf16[384,768]{1,0:T(8,128)(2,1)S(1)} %get-tuple-element.36.wb), channel_id=1, source_target_pairs={{0,16},{16,0},{32,48},{48,32},{64,80},{80,64},{96,112},{112,96},{1... | collective-permute-start | bytes 1769480 | tf_op jit(solution)/shard_map/ppermute | solution.py:25
  40.5 31.9 %collective-permute-start.22 = (bf16[256,768]{1,0:T(8,128)(2,1)S(1)}, bf16[256,768]{1,0:T(8,128)(2,1)S(1)}, u32[]{:S(2)}, u32[]{:S(2)}) collective-permute-start(bf16[256,768]{1,0:T(8,128)(2,1)S(1)} %copy-done), channel_id=1, source_target_pairs={{0,64},{16,80},{32,96},{48,112},{64,0},{80,16},{96,32},{112,48},{1... | collective-permute-start | bytes 1179656 | tf_op jit(solution)/shard_map/ppermute | solution.py:25
  42.4 32.5 %collective-permute-start.19 = (bf16[256,768]{1,0:T(8,128)(2,1)S(1)}, bf16[256,768]{1,0:T(8,128)(2,1)S(1)}, u32[]{:S(2)}, u32[]{:S(2)}) collective-permute-start(bf16[256,768]{1,0:T(8,128)(2,1)S(1)} %copy-done), channel_id=1, source_target_pairs={{0,16},{16,0},{32,48},{48,32},{64,80},{80,64},{96,112},{112,96},{1... | collective-permute-start | bytes 1179656 | tf_op jit(solution)/shard_map/ppermute | solution.py:25
  68.3 9.3 %collective-permute-start.13 = (bf16[128,768]{1,0:T(8,128)(2,1)S(1)}, bf16[128,768]{1,0:T(8,128)(2,1)S(1)}, u32[]{:S(2)}, u32[]{:S(2)}) collective-permute-start(bf16[128,768]{1,0:T(8,128)(2,1)S(1)} %get-tuple-element.40), channel_id=1, source_target_pairs={{0,32},{16,48},{32,0},{48,16},{64,96},{80,112},{96,64},{112,80},{1... | collective-permute-start | bytes 589832 | tf_op jit(solution)/shard_map/ppermute | solution.py:25
  68.4 14.9 %collective-permute-start.24 = (bf16[256,768]{1,0:T(8,128)(2,1)S(1)}, bf16[256,768]{1,0:T(8,128)(2,1)S(1)}, u32[]{:S(2)}, u32[]{:S(2)}) collective-permute-start(bf16[256,768]{1,0:T(8,128)(2,1)S(1)} %copy-done), channel_id=1, source_target_pairs={{0,96},{16,112},{32,64},{48,80},{64,32},{80,48},{96,0},{112,16},{1... | collective-permute-start | bytes 1179656 | tf_op jit(solution)/shard_map/ppermute | solution.py:25
  70.6 14.2 %collective-permute-start.20 = (bf16[256,768]{1,0:T(8,128)(2,1)S(1)}, bf16[256,768]{1,0:T(8,128)(2,1)S(1)}, u32[]{:S(2)}, u32[]{:S(2)}) collective-permute-start(bf16[256,768]{1,0:T(8,128)(2,1)S(1)} %copy-done), channel_id=1, source_target_pairs={{0,32},{16,48},{32,0},{48,16},{64,96},{80,112},{96,64},{112,80},{1... | collective-permute-start | bytes 1179656 | tf_op jit(solution)/shard_map/ppermute | solution.py:25
  72.4 10.8 %collective-permute-start.17 = (bf16[128,768]{1,0:T(8,128)(2,1)S(1)}, bf16[128,768]{1,0:T(8,128)(2,1)S(1)}, u32[]{:S(2)}, u32[]{:S(2)}) collective-permute-start(bf16[128,768]{1,0:T(8,128)(2,1)S(1)} %get-tuple-element.44), channel_id=1, source_target_pairs={{0,96},{16,112},{32,64},{48,80},{64,32},{80,48},{96,0},{112,16},{1... | collective-permute-start | bytes 589832 | tf_op jit(solution)/shard_map/ppermute | solution.py:25
  74.9 11.8 %collective-permute-start.23 = (bf16[256,768]{1,0:T(8,128)(2,1)S(1)}, bf16[256,768]{1,0:T(8,128)(2,1)S(1)}, u32[]{:S(2)}, u32[]{:S(2)}) collective-permute-start(bf16[256,768]{1,0:T(8,128)(2,1)S(1)} %collective-permute-done.22.rest_4_), channel_id=1, source_target_pairs={{0,16},{16,0},{32,48},{48,32},{64,80},{80,64},{96,112},{112,96},{1... | collective-permute-start | bytes 1179656 | tf_op jit(solution)/shard_map/ppermute | solution.py:25
  77.6 14.1 %collective-permute-start.25 = (bf16[256,768]{1,0:T(8,128)(2,1)S(1)}, bf16[256,768]{1,0:T(8,128)(2,1)S(1)}, u32[]{:S(2)}, u32[]{:S(2)}) collective-permute-start(bf16[256,768]{1,0:T(8,128)(2,1)S(1)} %collective-permute-done.19.rest_1_), channel_id=1, source_target_pairs={{0,96},{16,112},{32,64},{48,80},{64,32},{80,48},{96,0},{112,16},{1... | collective-permute-start | bytes 1179656 | tf_op jit(solution)/shard_map/ppermute | solution.py:25
  83.2 8.4 %collective-permute-start.21 = (bf16[256,768]{1,0:T(8,128)(2,1)S(1)}, bf16[256,768]{1,0:T(8,128)(2,1)S(1)}, u32[]{:S(2)}, u32[]{:S(2)}) collective-permute-start(bf16[256,768]{1,0:T(8,128)(2,1)S(1)} %collective-permute-done.19.rest_1_), channel_id=1, source_target_pairs={{0,32},{16,48},{32,0},{48,16},{64,96},{80,112},{96,64},{112,80},{1... | collective-permute-start | bytes 1179656 | tf_op jit(solution)/shard_map/ppermute | solution.py:25
  83.3 10.8 %collective-permute-start.12 = (bf16[128,768]{1,0:T(8,128)(2,1)S(1)}, bf16[128,768]{1,0:T(8,128)(2,1)S(1)}, u32[]{:S(2)}, u32[]{:S(2)}) collective-permute-start(bf16[128,768]{1,0:T(8,128)(2,1)S(1)} %get-tuple-element.38), channel_id=1, source_target_pairs={{0,32},{16,48},{32,0},{48,16},{64,96},{80,112},{96,64},{112,80},{1... | collective-permute-start | bytes 589832 | tf_op jit(solution)/shard_map/ppermute | solution.py:25
  84.9 11.0 %collective-permute-start.14 = (bf16[128,768]{1,0:T(8,128)(2,1)S(1)}, bf16[128,768]{1,0:T(8,128)(2,1)S(1)}, u32[]{:S(2)}, u32[]{:S(2)}) collective-permute-start(bf16[128,768]{1,0:T(8,128)(2,1)S(1)} %shard_map.112), channel_id=1, source_target_pairs={{0,96},{16,112},{32,64},{48,80},{64,32},{80,48},{96,0},{112,16},{1... | collective-permute-start | bytes 589832 | tf_op jit(solution)/shard_map/ppermute | solution.py:25
  86.7 13.3 %collective-permute-start.16 = (bf16[128,768]{1,0:T(8,128)(2,1)S(1)}, bf16[128,768]{1,0:T(8,128)(2,1)S(1)}, u32[]{:S(2)}, u32[]{:S(2)}) collective-permute-start(bf16[128,768]{1,0:T(8,128)(2,1)S(1)} %get-tuple-element.42), channel_id=1, source_target_pairs={{0,96},{16,112},{32,64},{48,80},{64,32},{80,48},{96,0},{112,16},{1... | collective-permute-start | bytes 589832 | tf_op jit(solution)/shard_map/ppermute | solution.py:25
  91.6 8.4 %collective-permute-start.18 = (bf16[128,768]{1,0:T(8,128)(2,1)S(1)}, bf16[128,768]{1,0:T(8,128)(2,1)S(1)}, u32[]{:S(2)}, u32[]{:S(2)}) collective-permute-start(bf16[128,768]{1,0:T(8,128)(2,1)S(1)} %shard_map.114), channel_id=1, source_target_pairs={{0,32},{16,48},{32,0},{48,16},{64,96},{80,112},{96,64},{112,80},{1... | collective-permute-start | bytes 589832 | tf_op jit(solution)/shard_map/ppermute | solution.py:25
  110.9 8.2 %collective-permute-start.27 = (bf16[16,6144]{1,0:T(8,128)(2,1)S(1)}, bf16[16,6144]{1,0:T(8,128)(2,1)S(1)}, u32[]{:S(2)}, u32[]{:S(2)}) collective-permute-start(bf16[16,6144]{1,0:T(8,128)(2,1)S(1)} %get-tuple-element.48), channel_id=1, source_target_pairs={{0,2},{1,3},{2,0},{3,1},{4,6},{5,7},{6,4},{7,5},{8,10},{9,11},{10,... | collective-permute-start | bytes 589832 | tf_op jit(solution)/shard_map/ppermute | solution.py:25
  111.7 8.5 %collective-permute-start.28 = (bf16[16,6144]{1,0:T(8,128)(2,1)S(1)}, bf16[16,6144]{1,0:T(8,128)(2,1)S(1)}, u32[]{:S(2)}, u32[]{:S(2)}) collective-permute-start(bf16[16,6144]{1,0:T(8,128)(2,1)S(1)} %get-tuple-element.49), channel_id=1, source_target_pairs={{0,6},{1,7},{2,4},{3,5},{4,2},{5,3},{6,0},{7,1},{8,14},{9,15},{10,... | collective-permute-start | bytes 589832 | tf_op jit(solution)/shard_map/ppermute | solution.py:25
  124.7 8.8 %collective-permute-start.36 = (bf16[16,6144]{1,0:T(8,128)(2,1)S(1)}, bf16[16,6144]{1,0:T(8,128)(2,1)S(1)}, u32[]{:S(2)}, u32[]{:S(2)}) collective-permute-start(bf16[16,6144]{1,0:T(8,128)(2,1)S(1)} %shard_map.120), channel_id=1, source_target_pairs={{0,6},{1,7},{2,4},{3,5},{4,2},{5,3},{6,0},{7,1},{8,14},{9,15},{10,... | collective-permute-start | bytes 589832 | tf_op jit(solution)/shard_map/ppermute | solution.py:25
  128.7 9.8 %collective-permute-start.40 = (bf16[16,6144]{1,0:T(8,128)(2,1)S(1)}, bf16[16,6144]{1,0:T(8,128)(2,1)S(1)}, u32[]{:S(2)}, u32[]{:S(2)}) collective-permute-start(bf16[16,6144]{1,0:T(8,128)(2,1)S(1)} %collective-permute-done.37), channel_id=1, source_target_pairs={{0,6},{1,7},{2,4},{3,5},{4,2},{5,3},{6,0},{7,1},{8,14},{9,15},{10,... | collective-permute-start | bytes 589832 | tf_op jit(solution)/shard_map/ppermute | solution.py:25
  138.6 16.3 %collective-permute-start.41 = (bf16[8,16,6144]{2,1,0:T(8,128)(2,1)S(1)}, bf16[8,16,6144]{2,1,0:T(8,128)(2,1)S(1)}, u32[]{:S(2)}, u32[]{:S(2)}) collective-permute-start(bf16[8,16,6144]{2,1,0:T(8,128)(2,1)S(1)} %bitcast_dynamic-update-slice_fusion.src), channel_id=1, source_target_pairs={{0,1},{1,0},{2,3},{3,2},{4,5},{5,4},{6,7},{7,6},{8,9},{9,8},{10,11... | collective-permute-start | bytes 4718600 | tf_op jit(solution)/shard_map/ppermute | solution.py:25
  157.9 9.3 %collective-permute-start.42 = (bf16[8,16,3072]{2,1,0:T(8,128)(2,1)S(1)}, bf16[8,16,3072]{2,1,0:T(8,128)(2,1)S(1)}, u32[]{:S(2)}, u32[]{:S(2)}) collective-permute-start(bf16[8,16,3072]{2,1,0:T(8,128)(2,1)S(1)} %shard_map.124), channel_id=1, source_target_pairs={{0,1},{1,0},{2,3},{3,2},{4,5},{5,4},{6,7},{7,6},{8,9},{9,8},{10,11... | collective-permute-start | bytes 2359304 | tf_op jit(solution)/shard_map/ppermute | solution.py:25
  161.7 10.0 %collective-permute-start.48 = (bf16[16,3072]{1,0:T(8,128)(2,1)S(1)}, bf16[16,3072]{1,0:T(8,128)(2,1)S(1)}, u32[]{:S(2)}, u32[]{:S(2)}) collective-permute-start(bf16[16,3072]{1,0:T(8,128)(2,1)S(1)} %get-tuple-element.63), channel_id=1, source_target_pairs={{0,12},{1,13},{2,14},{3,15},{4,8},{5,9},{6,10},{7,11},{8,4},{9,5},... | collective-permute-start | bytes 294920 | tf_op jit(solution)/shard_map/ppermute | solution.py:25
  168.5 14.9 %collective-permute-start.43 = (bf16[2,16,3072]{2,1,0:T(8,128)(2,1)S(1)}, bf16[2,16,3072]{2,1,0:T(8,128)(2,1)S(1)}, u32[]{:S(2)}, u32[]{:S(2)}) collective-permute-start(bf16[2,16,3072]{2,1,0:T(8,128)(2,1)S(1)} %pad_maximum_fusion.1), channel_id=1, source_target_pairs={{0,2},{1,3},{2,0},{3,1},{4,6},{5,7},{6,4},{7,5},{8,10},{9,11},{10,... | collective-permute-start | bytes 589832 | tf_op jit(solution)/shard_map/ppermute | solution.py:25
  171.7 11.7 %collective-permute-start.44 = (bf16[2,16,3072]{2,1,0:T(8,128)(2,1)S(1)}, bf16[2,16,3072]{2,1,0:T(8,128)(2,1)S(1)}, u32[]{:S(2)}, u32[]{:S(2)}) collective-permute-start(bf16[2,16,3072]{2,1,0:T(8,128)(2,1)S(1)} %pad_maximum_fusion.2), channel_id=1, source_target_pairs={{0,4},{1,5},{2,6},{3,7},{4,0},{5,1},{6,2},{7,3},{8,12},{9,13},{10,... | collective-permute-start | bytes 589832 | tf_op jit(solution)/shard_map/ppermute | solution.py:25
  172.2 11.2 %collective-permute-start.45 = (bf16[2,16,3072]{2,1,0:T(8,128)(2,1)S(1)}, bf16[2,16,3072]{2,1,0:T(8,128)(2,1)S(1)}, u32[]{:S(2)}, u32[]{:S(2)}) collective-permute-start(bf16[2,16,3072]{2,1,0:T(8,128)(2,1)S(1)} %pad_maximum_fusion.3), channel_id=1, source_target_pairs={{0,6},{1,7},{2,4},{3,5},{4,2},{5,3},{6,0},{7,1},{8,14},{9,15},{10,... | collective-permute-start | bytes 589832 | tf_op jit(solution)/shard_map/ppermute | solution.py:25
  174.2 9.2 %collective-permute-start.51 = (bf16[16,3072]{1,0:T(8,128)(2,1)S(1)}, bf16[16,3072]{1,0:T(8,128)(2,1)S(1)}, u32[]{:S(2)}, u32[]{:S(2)}) collective-permute-start(bf16[16,3072]{1,0:T(8,128)(2,1)S(1)} %get-tuple-element.67), channel_id=1, source_target_pairs={{0,10},{1,11},{2,8},{3,9},{4,14},{5,15},{6,12},{7,13},{8,2},{9,3},... | collective-permute-start | bytes 294920 | tf_op jit(solution)/shard_map/ppermute | solution.py:25
  174.4 9.0 %collective-permute-start.50 = (bf16[16,3072]{1,0:T(8,128)(2,1)S(1)}, bf16[16,3072]{1,0:T(8,128)(2,1)S(1)}, u32[]{:S(2)}, u32[]{:S(2)}) collective-permute-start(bf16[16,3072]{1,0:T(8,128)(2,1)S(1)} %get-tuple-element.68), channel_id=1, source_target_pairs={{0,8},{1,9},{2,10},{3,11},{4,12},{5,13},{6,14},{7,15},{8,0},{9,1},... | collective-permute-start | bytes 294920 | tf_op jit(solution)/shard_map/ppermute | solution.py:25
  (29 other events, 196.3 us)

commit v5 on v4

--- a/solution.py
+++ b/solution.py
@@ -16,6 +16,11 @@
 BF = jnp.bfloat16
 F32 = jnp.float32
 
+
+SENDS = (
+    ("l", 6), ("l", 7), ("l", 5), ("b", 2), ("h", 6), ("b", 3), ("h", 7), ("b", 1),
+    ("h", 5), ("l", 4), ("h", 4),
+)
 
 VM = pl.BlockSpec(memory_space=pltpu.VMEM)
 SM = pl.BlockSpec(memory_space=pltpu.SMEM)
@@ -43,13 +48,48 @@
     return go
 
 
-def norm_kernel(ids, x_ref, g_ref, o_ref):
+def first_kernel(ids, x_hbm, g_hbm, w_hbm, o_ref, wa, wb, x_ref, g_ref, sems):
+    half = wa.shape[0]
+    moves = (
+        (x_hbm, x_ref),
+        (g_hbm, g_ref),
+        (w_hbm.at[pl.ds(0, half)], wa),
+        (w_hbm.at[pl.ds(half, half)], wb),
+    )
+    copies = [
+        pltpu.make_async_copy(src, dst, sems.at[i]) for i, (src, dst) in enumerate(moves)
+    ]
+    for copy in copies:
+        copy.start()
+    copies[0].wait()
+    copies[1].wait()
     x = x_ref[...].astype(F32)
     scale = lax.rsqrt(jnp.mean(x * x, axis=-1, keepdims=True) + EPS)
     y = (x * scale * g_ref[...]).astype(BF)
     width = o_ref.shape[2]
     for b in range(o_ref.shape[0]):
         o_ref[ids[0] ^ b] = y[:, b * width:(b + 1) * width]
+    copies[2].wait()
+    copies[3].wait()
+
+
+def first(ids, mine, gain, weight):
+    far = pl.BlockSpec(memory_space=pltpu.HBM)
+    half = (weight.shape[0] // 2, weight.shape[1])
+    rel = (8, mine.shape[0], mine.shape[1] // 8)
+    big = [pltpu.with_memory_space_constraint(a, pltpu.HBM) for a in (mine, gain, weight)]
+    return pl.pallas_call(
+        first_kernel,
+        out_shape=[pltpu.VMEM(s, BF) for s in (rel, half, half)],
+        in_specs=[SM, far, far, far],
+        out_specs=[VM] * 3,
+        scratch_shapes=[
+            pltpu.VMEM(mine.shape, BF),
+            pltpu.VMEM(gain.shape, F32),
+            pltpu.SemaphoreType.DMA((4,)),
+        ],
+        compiler_params=pltpu.CompilerParams(vmem_limit_bytes=8 << 20),
+    )(ids, *big)
 
 
 def qkv_kernel(src, wa, wb, va, vb, *outs):
@@ -64,31 +104,6 @@
                 )
                 acc = part if acc is None else acc + part
         o_ref[...] = acc.astype(o_ref.dtype)
-
-
-def cut_kernel(src, *rest):
-    outs, sems = rest[:-1], rest[-1]
-    rows = outs[0].shape[0]
-    copies = [
-        pltpu.make_async_copy(src.at[pl.ds(i * rows, rows)], o, sems.at[i])
-        for i, o in enumerate(outs)
-    ]
-    for copy in copies:
-        copy.start()
-    for copy in copies:
-        copy.wait()
-
-
-def cut(value):
-    half = (value.shape[0] // 2, value.shape[1])
-    return pl.pallas_call(
-        cut_kernel,
-        out_shape=[pltpu.VMEM(half, value.dtype)] * 2,
-        in_specs=[pl.BlockSpec(memory_space=pltpu.HBM)],
-        out_specs=[VM] * 2,
-        scratch_shapes=[pltpu.SemaphoreType.DMA((2,))],
-        compiler_params=pltpu.CompilerParams(vmem_limit_bytes=1 << 20),
-    )(pltpu.with_memory_space_constraint(value, pltpu.HBM))
 
 
 def place(row, section, step):
@@ -321,11 +336,8 @@
     cb = lambda v, flip: swap(v, "cb", 16, flip)
     block = model // 8
 
-    rel = call(norm_kernel, [((8, 16, block), BF)], smem=1, n_in=3)(
-        ids, mine, t_gain[None]
-    )[0]
+    rel, wa, wb = first(ids, mine, t_gain[None], w_qkv)
     near = fs(w_out, 1)
-    wa, wb = cut(w_qkv)
     va = fs(wa, 1)
     vb = fs(wb, 1)
     local = [rel[0:2]] + [fs(rel[2 * d:2 * d + 2], 2 * d) for d in (1, 2, 3)]
@@ -369,7 +381,9 @@
     near1, near3 = cb(blocks[1], 2), cb(blocks[3], 6)
     side = add(blocks[4], far1, far3)
     deep = add(blocks[2], far2)
-    pieces = [blocks[0], near1, near3, cb(side, 8), cb(deep, 4)]
+    last2 = cb(deep, 4)
+    last1 = cb(side, 8)
+    pieces = [blocks[0], near1, near3, last1, last2]
     hn = call(
         hidden_kernel,
         [((16, model), BF)],
@@ -392,18 +406,22 @@
     low = lift(even, 0, [((16, 3 * inner), BF)] * 8)
     high = lift(odd, 8, [((8, 16, 3 * inner), BF)])[0]
     high = cb(high, 1)
-    got = {e: cb(low[e], 2 * e) for e in (5, 7)}
-    got.update({e: cb(low[e], 2 * e) for e in (6, 4)})
-    both = [cb(jnp.stack([low[e], high[e]]), 2 * e) for e in (2, 1, 3)]
-    deep = [cb(high[e], 2 * e) for e in (4, 5, 6, 7)]
-    both = [both[1], both[0], both[2]]
+    sent = {}
+    for kind, e in SENDS:
+        piece = {"l": low[e], "h": high[e]}.get(kind)
+        if piece is None:
+            piece = jnp.stack([low[e], high[e]])
+        sent[kind, e] = cb(piece, 2 * e)
+    both = [sent["b", e] for e in (1, 2, 3)]
+    got = [sent["l", e] for e in (4, 5, 6, 7)]
+    deep = [sent["h", e] for e in (4, 5, 6, 7)]
     outs = call(
         depth_kernel,
         [((16, 16, inner), BF)],
         scratch=[pltpu.VMEM((256, 3 * inner), BF)],
         smem=1,
         n_in=14,
-    )(ids, low[0], high[0], *both, *[got[e] for e in (4, 5, 6, 7)], *deep)[0]
+    )(ids, low[0], high[0], *both, *got, *deep)[0]
     out = lax.all_to_all(outs, "cb", 0, 0, tiled=True)
     return out.reshape(1, 1, 256, inner)
 

time: 203 us -> 201 us (level)
    pallas_call x14 -> x13, Pallas kernels: 16.9 us -> 16.2 us  [go(): return run(*args[:smem], *held)]
  transfers between devices with their start and end apart: 54 -> 54, of which waited for: 27 -> 27; matrix products, arithmetic and copies ran while one was open for 0% -> 0% of each run, Pallas kernels for 9% -> 8%
where the time goes in v5:
time: 201 us
  waiting for transfers between devices  82.2 us (41%)
  starting transfers between devices  72.9 us (36%)
  Pallas kernels  27.4 us (14%)
  blocking collectives  15.7 us (8%)
    ppermute x54, waiting for transfers between devices, swap(): return lax.ppermute(value, axis, [(i, i ^ flip) for i in range(size)])  82.2 us
    ppermute x54, starting transfers between devices, swap(): return lax.ppermute(value, axis, [(i, i ^ flip) for i in range(size)])  72.9 us
    pallas_call x13, Pallas kernels, go(): return run(*args[:smem], *held)  16.2 us
    all_to_all x1, blocking collectives, work(): out = lax.all_to_all(outs, 'cb', 0, 0, tiled=True)  15.7 us
    pallas_call x1, Pallas kernels, fetch(): pl.pallas_call(fetch_kernel, out_shape=[pltpu.VMEM(s, BF) for s in shapes...  4.62 us
    pallas_call x1, Pallas kernels, load(): pl.pallas_call(load_kernel, out_shape=pltpu.VMEM(value.shape, value.dtype...  4.6 us
  transfers between devices with their start and end apart: 54, of which 27 were waited for; matrix products, arithmetic and copies ran while one was open for 0% of the time, Pallas kernels for 8%

profile of v5, /device:TPU:1, one launch (start us, length us, event | category | flops | bytes accessed | tf_op | source)
XLA Modules:
  0.0 200.5 jit_solution(12517708665525209959)
XLA Ops:
  2.7 4.7 %collective-permute-start.2 = (bf16[2,16,768]{2,1,0:T(8,128)(2,1)S(1)}, bf16[2,16,768]{2,1,0:T(8,128)(2,1)S(1)}, u32[]{:S(2)}, u32[]{:S(2)}) collective-permute-start(bf16[2,16,768]{2,1,0:T(8,128)(2,1)S(1)} %get-tuple-element.76), channel_id=1, source_target_pairs={{0,96},{16,112},{32,64},{48,80},{64,32},{80,48},{96,0},{112,16},{1... | collective-permute-start | bytes 147464 | tf_op jit(solution)/shard_map/ppermute | solution.py:30
  8.8 3.0 %collective-permute-done.1 = bf16[2,16,768]{2,1,0:T(8,128)(2,1)S(1)} collective-permute-done((bf16[2,16,768]{2,1,0:T(8,128)(2,1)S(1)}, bf16[2,16,768]{2,1,0:T(8,128)(2,1)S(1)}, u32[]{:S(2)}, u32[]{:S(2)}) %collective-permute-start.1) | collective-permute-done | bytes 49184 | tf_op jit(solution)/shard_map/ppermute | solution.py:30
  16.9 2.1 %collective-permute-start.9 = (bf16[8,16,768]{2,1,0:T(8,128)(2,1)S(1)}, bf16[8,16,768]{2,1,0:T(8,128)(2,1)S(1)}, u32[]{:S(2)}, u32[]{:S(2)}) collective-permute-start(bf16[8,16,768]{2,1,0:T(8,128)(2,1)S(1)} %collective-permute-done.6), channel_id=1, source_target_pairs={{0,6},{1,7},{2,4},{3,5},{4,2},{5,3},{6,0},{7,1},{8,14},{9,15},{10,... | collective-permute-start | bytes 589832 | tf_op jit(solution)/shard_map/ppermute | solution.py:30
  20.3 3.6 %collective-permute-done.4 = bf16[8,16,768]{2,1,0:T(8,128)(2,1)S(1)} collective-permute-done((bf16[8,16,768]{2,1,0:T(8,128)(2,1)S(1)}, bf16[8,16,768]{2,1,0:T(8,128)(2,1)S(1)}, u32[]{:S(2)}, u32[]{:S(2)}) %collective-permute-start.4) | collective-permute-done | bytes 196640 | tf_op jit(solution)/shard_map/ppermute | solution.py:30
  24.0 7.7 %collective-permute-done.7 = bf16[8,16,768]{2,1,0:T(8,128)(2,1)S(1)} collective-permute-done((bf16[8,16,768]{2,1,0:T(8,128)(2,1)S(1)}, bf16[8,16,768]{2,1,0:T(8,128)(2,1)S(1)}, u32[]{:S(2)}, u32[]{:S(2)}) %collective-permute-start.7) | collective-permute-done | bytes 196640 | tf_op jit(solution)/shard_map/ppermute | solution.py:30
  32.1 3.6 %collective-permute-start.15 = (bf16[8,8,16,768]{3,2,1,0:T(8,128)(2,1)S(1)}, bf16[8,8,16,768]{3,2,1,0:T(8,128)(2,1)S(1)}, u32[]{:S(2)}, u32[]{:S(2)}) collective-permute-start(bf16[8,8,16,768]{3,2,1,0:T(8,128)(2,1)S(1)} %bitcast_dynamic-update-slice_fusion.8.src), channel_id=1, source_target_pairs={{0,1},{1,0},{2,3},{3,2},{4,5},{5,4},{6,7},{7,6},{8,9},{9,8},{10,11... | collective-permute-start | bytes 4718600 | tf_op jit(solution)/shard_map/ppermute | solution.py:30
  35.7 2.6 %collective-permute-start.10 = (bf16[384,768]{1,0:T(8,128)(2,1)S(1)}, bf16[384,768]{1,0:T(8,128)(2,1)S(1)}, u32[]{:S(2)}, u32[]{:S(2)}) collective-permute-start(bf16[384,768]{1,0:T(8,128)(2,1)S(1)} %get-tuple-element.37.wa), channel_id=1, source_target_pairs={{0,16},{16,0},{32,48},{48,32},{64,80},{80,64},{96,112},{112,96},{1... | collective-permute-start | bytes 1769480 | tf_op jit(solution)/shard_map/ppermute | solution.py:30
  40.7 2.6 %collective-permute-start.19 = (bf16[256,768]{1,0:T(8,128)(2,1)S(1)}, bf16[256,768]{1,0:T(8,128)(2,1)S(1)}, u32[]{:S(2)}, u32[]{:S(2)}) collective-permute-start(bf16[256,768]{1,0:T(8,128)(2,1)S(1)} %copy-done), channel_id=1, source_target_pairs={{0,16},{16,0},{32,48},{48,32},{64,80},{80,64},{96,112},{112,96},{1... | collective-permute-start | bytes 1179656 | tf_op jit(solution)/shard_map/ppermute | solution.py:30
  43.3 8.7 %collective-permute-done.10.va = bf16[384,768]{1,0:T(8,128)(2,1)S(1)} collective-permute-done((bf16[384,768]{1,0:T(8,128)(2,1)S(1)}, bf16[384,768]{1,0:T(8,128)(2,1)S(1)}, u32[]{:S(2)}, u32[]{:S(2)}) %collective-permute-start.10) | collective-permute-done | bytes 589856 | tf_op jit(solution)/shard_map/ppermute | solution.py:30
  52.0 12.6 %collective-permute-done.11.vb = bf16[384,768]{1,0:T(8,128)(2,1)S(1)} collective-permute-done((bf16[384,768]{1,0:T(8,128)(2,1)S(1)}, bf16[384,768]{1,0:T(8,128)(2,1)S(1)}, u32[]{:S(2)}, u32[]{:S(2)}) %collective-permute-start.11) | collective-permute-done | bytes 589856 | tf_op jit(solution)/shard_map/ppermute | solution.py:30
  66.5 2.2 %collective-permute-start.24 = (bf16[256,768]{1,0:T(8,128)(2,1)S(1)}, bf16[256,768]{1,0:T(8,128)(2,1)S(1)}, u32[]{:S(2)}, u32[]{:S(2)}) collective-permute-start(bf16[256,768]{1,0:T(8,128)(2,1)S(1)} %copy-done), channel_id=1, source_target_pairs={{0,96},{16,112},{32,64},{48,80},{64,32},{80,48},{96,0},{112,16},{1... | collective-permute-start | bytes 1179656 | tf_op jit(solution)/shard_map/ppermute | solution.py:30
  73.1 2.6 %collective-permute-start.23 = (bf16[256,768]{1,0:T(8,128)(2,1)S(1)}, bf16[256,768]{1,0:T(8,128)(2,1)S(1)}, u32[]{:S(2)}, u32[]{:S(2)}) collective-permute-start(bf16[256,768]{1,0:T(8,128)(2,1)S(1)} %collective-permute-done.22.rest_4_), channel_id=1, source_target_pairs={{0,16},{16,0},{32,48},{48,32},{64,80},{80,64},{96,112},{112,96},{1... | collective-permute-start | bytes 1179656 | tf_op jit(solution)/shard_map/ppermute | solution.py:30
  76.9 4.3 %collective-permute-done.17.refs_1_ = bf16[128,768]{1,0:T(8,128)(2,1)S(1)} collective-permute-done((bf16[128,768]{1,0:T(8,128)(2,1)S(1)}, bf16[128,768]{1,0:T(8,128)(2,1)S(1)}, u32[]{:S(2)}, u32[]{:S(2)}) %collective-permute-start.17) | collective-permute-done | bytes 196640 | tf_op jit(solution)/shard_map/ppermute | solution.py:30
  85.5 4.1 %collective-permute-done.25.rest_7_ = bf16[256,768]{1,0:T(8,128)(2,1)S(1)} collective-permute-done((bf16[256,768]{1,0:T(8,128)(2,1)S(1)}, bf16[256,768]{1,0:T(8,128)(2,1)S(1)}, u32[]{:S(2)}, u32[]{:S(2)}) %collective-permute-start.25) | collective-permute-done | bytes 393248 | tf_op jit(solution)/shard_map/ppermute | solution.py:30
  89.6 2.1 %collective-permute-done.12.a1 = bf16[128,768]{1,0:T(8,128)(2,1)S(1)} collective-permute-done((bf16[128,768]{1,0:T(8,128)(2,1)S(1)}, bf16[128,768]{1,0:T(8,128)(2,1)S(1)}, u32[]{:S(2)}, u32[]{:S(2)}) %collective-permute-start.12) | collective-permute-done | bytes 196640 | tf_op jit(solution)/shard_map/ppermute | solution.py:30
  93.8 4.2 %collective-permute-done.16.b1 = bf16[128,768]{1,0:T(8,128)(2,1)S(1)} collective-permute-done((bf16[128,768]{1,0:T(8,128)(2,1)S(1)}, bf16[128,768]{1,0:T(8,128)(2,1)S(1)}, u32[]{:S(2)}, u32[]{:S(2)}) %collective-permute-start.16) | collective-permute-done | bytes 196640 | tf_op jit(solution)/shard_map/ppermute | solution.py:30
  100.2 3.2 %collective-permute-start.26 = (bf16[128,6144]{1,0:T(8,128)(2,1)S(1)}, bf16[128,6144]{1,0:T(8,128)(2,1)S(1)}, u32[]{:S(2)}, u32[]{:S(2)}) collective-permute-start(bf16[128,6144]{1,0:T(8,128)(2,1)S(1)} %get-tuple-element.48), channel_id=1, source_target_pairs={{0,1},{1,0},{2,3},{3,2},{4,5},{5,4},{6,7},{7,6},{8,9},{9,8},{10,11... | collective-permute-start | bytes 4718600 | tf_op jit(solution)/shard_map/ppermute | solution.py:30
  104.0 2.4 %collective-permute-done.26.b_ref = bf16[128,6144]{1,0:T(8,128)(2,1)S(1)} collective-permute-done((bf16[128,6144]{1,0:T(8,128)(2,1)S(1)}, bf16[128,6144]{1,0:T(8,128)(2,1)S(1)}, u32[]{:S(2)}, u32[]{:S(2)}) %collective-permute-start.26) | collective-permute-done | bytes 1572896 | tf_op jit(solution)/shard_map/ppermute | solution.py:30
  118.9 2.4 %collective-permute-done.33.rest_4_ = bf16[16,6144]{1,0:T(8,128)(2,1)S(1)} collective-permute-done((bf16[16,6144]{1,0:T(8,128)(2,1)S(1)}, bf16[16,6144]{1,0:T(8,128)(2,1)S(1)}, u32[]{:S(2)}, u32[]{:S(2)}) %collective-permute-start.33) | collective-permute-done | bytes 196640 | tf_op jit(solution)/shard_map/ppermute | solution.py:30
  128.1 2.7 %collective-permute-done.35 = bf16[16,6144]{1,0:T(8,128)(2,1)S(1)} collective-permute-done((bf16[16,6144]{1,0:T(8,128)(2,1)S(1)}, bf16[16,6144]{1,0:T(8,128)(2,1)S(1)}, u32[]{:S(2)}, u32[]{:S(2)}) %collective-permute-start.35) | collective-permute-done | bytes 196640 | tf_op jit(solution)/shard_map/ppermute | solution.py:30
  131.5 3.4 %collective-permute-done.38 = bf16[16,6144]{1,0:T(8,128)(2,1)S(1)} collective-permute-done((bf16[16,6144]{1,0:T(8,128)(2,1)S(1)}, bf16[16,6144]{1,0:T(8,128)(2,1)S(1)}, u32[]{:S(2)}, u32[]{:S(2)}) %collective-permute-start.38) | collective-permute-done | bytes 196640 | tf_op jit(solution)/shard_map/ppermute | solution.py:30
  136.6 7.1 %collective-permute-start.41 = (bf16[8,16,6144]{2,1,0:T(8,128)(2,1)S(1)}, bf16[8,16,6144]{2,1,0:T(8,128)(2,1)S(1)}, u32[]{:S(2)}, u32[]{:S(2)}) collective-permute-start(bf16[8,16,6144]{2,1,0:T(8,128)(2,1)S(1)} %bitcast_dynamic-update-slice_fusion.src), channel_id=1, source_target_pairs={{0,1},{1,0},{2,3},{3,2},{4,5},{5,4},{6,7},{7,6},{8,9},{9,8},{10,11... | collective-permute-start | bytes 4718600 | tf_op jit(solution)/shard_map/ppermute | solution.py:30
  143.7 4.6 %shard_map.120.din = bf16[6144,1024]{1,0:T(8,128)(2,1)S(1)} custom-call(bf16[6144,1024]{1,0:T(8,128)(2,1)} %bitcast.62), custom_call_target="tpu_custom_call" | custom-call | tf_op jit(solution)/shard_map/pallas_call | solution.py:214
  148.3 4.6 %shard_map.121 = (bf16[1024,3072]{1,0:T(8,128)(2,1)S(1)}, bf16[16,16,1024]{2,1,0:T(8,128)(2,1)S(1)}) custom-call(s32[3]{0:T(128)S(1)} %pad_add_fusion.ids, s32[1,256]{1,0:T(1,128)S(1)} %bitcast.61, bf16[1024,3072]{1,0:T(8,128)(2,1)} %bitcast.63, bf16[2048,1024]{1,0:T(8,128)(2,1)} %bitcast.64), custom_call_target="tpu_custom_call" | custom-call | tf_op jit(solution)/shard_map/pallas_call | solution.py:249
  152.9 3.0 %shard_map.123 = bf16[8,16,3072]{2,1,0:T(8,128)(2,1)S(1)} custom-call(bf16[8,16,6144]{2,1,0:T(8,128)(2,1)S(1)} %collective-permute-done.41.src, bf16[6144,1024]{1,0:T(8,128)(2,1)S(1)} %shard_map.120.din, bf16[16,16,1024]{2,1,0:T(8,128)(2,1)S(1)} %get-tuple-element.57.emb, f32[1,1024]{1,0:T(1,128)S(1)} %copy-done.3, bf16[1024,3072]{1,0:T(8,128)(2,1)S(1)} %get-tuple-element.58.wqkv), custom_call_target="tpu_custom_call" | custom-call | tf_op jit(solution)/shard_map/pallas_call | solution.py:46
  156.2 3.0 %shard_map.122 = (bf16[16,3072]{1,0:T(8,128)(2,1)S(1)}, bf16[16,3072]{1,0:T(8,128)(2,1)S(1)}, bf16[16,3072]{1,0:T(8,128)(2,1)S(1)}, bf16[16,3072]{1,0:T(8,128)(2...) custom-call(bf16[8,16,6144]{2,1,0:T(8,128)(2,1)S(1)} %bitcast_dynami, ...), custom_call_target="tpu_custom_call" | custom-call | tf_op jit(solution)/shard_map/pallas_call | solution.py:46
  159.7 2.8 %collective-permute-start.48 = (bf16[16,3072]{1,0:T(8,128)(2,1)S(1)}, bf16[16,3072]{1,0:T(8,128)(2,1)S(1)}, u32[]{:S(2)}, u32[]{:S(2)}) collective-permute-start(bf16[16,3072]{1,0:T(8,128)(2,1)S(1)} %get-tuple-element.65), channel_id=1, source_target_pairs={{0,12},{1,13},{2,14},{3,15},{4,8},{5,9},{6,10},{7,11},{8,4},{9,5},... | collective-permute-start | bytes 294920 | tf_op jit(solution)/shard_map/ppermute | solution.py:30
  162.6 2.7 %collective-permute-start.49 = (bf16[16,3072]{1,0:T(8,128)(2,1)S(1)}, bf16[16,3072]{1,0:T(8,128)(2,1)S(1)}, u32[]{:S(2)}, u32[]{:S(2)}) collective-permute-start(bf16[16,3072]{1,0:T(8,128)(2,1)S(1)} %get-tuple-element.66), channel_id=1, source_target_pairs={{0,14},{1,15},{2,12},{3,13},{4,10},{5,11},{6,8},{7,9},{8,6},{9,7},... | collective-permute-start | bytes 294920 | tf_op jit(solution)/shard_map/ppermute | solution.py:30
  166.5 3.2 %collective-permute-start.43 = (bf16[2,16,3072]{2,1,0:T(8,128)(2,1)S(1)}, bf16[2,16,3072]{2,1,0:T(8,128)(2,1)S(1)}, u32[]{:S(2)}, u32[]{:S(2)}) collective-permute-start(bf16[2,16,3072]{2,1,0:T(8,128)(2,1)S(1)} %pad_maximum_fusion.1), channel_id=1, source_target_pairs={{0,2},{1,3},{2,0},{3,1},{4,6},{5,7},{6,4},{7,5},{8,10},{9,11},{10,... | collective-permute-start | bytes 589832 | tf_op jit(solution)/shard_map/ppermute | solution.py:30
  173.5 7.8 %collective-permute-done.51.rest_8_ = bf16[16,3072]{1,0:T(8,128)(2,1)S(1)} collective-permute-done((bf16[16,3072]{1,0:T(8,128)(2,1)S(1)}, bf16[16,3072]{1,0:T(8,128)(2,1)S(1)}, u32[]{:S(2)}, u32[]{:S(2)}) %collective-permute-start.51) | collective-permute-done | bytes 98336 | tf_op jit(solution)/shard_map/ppermute | solution.py:30
  181.4 2.6 %shard_map.124 = bf16[16,16,1024]{2,1,0:T(8,128)(2,1)S(1)} custom-call(s32[3]{0:T(128)S(1)} %pad_add_fusion.ids, bf16[16,3072]{1,0:T(8,128)(2,1)S(1)} %get-tuple-element.59.low, bf16[16,3072]{1,0:T(8,128)(2,1)S(1)} %get-tuple-element.74.high, bf16[2,16,3072]{2,1,0:T(8,128)(2,1)S(1)} %collective-permute-done.43.rest_0_, ...), custom_call_target="tpu_custom_call" | custom-call | tf_op jit(solution)/shard_map/pallas_call | solution.py:46
  184.0 15.7 %all_to_all.5 = bf16[16,16,1024]{2,1,0:T(8,128)(2,1)S(1)} all-to-all(bf16[16,16,1024]{2,1,0:T(8,128)(2,1)S(1)} %shard_map.124), channel_id=1, replica_groups=mesh['fsdp'=8,'cb'=16] {'cb'}, dimensions={0} | all-to-all | bytes 1048576 | tf_op jit(solution)/shard_map/all_to_all | solution.py:425
  (127 shorter events, 57.5 us)
Async XLA Ops:
  14.4 9.5 %collective-permute-start.5 = (bf16[8,16,768]{2,1,0:T(8,128)(2,1)S(1)}, bf16[8,16,768]{2,1,0:T(8,128)(2,1)S(1)}, u32[]{:S(2)}, u32[]{:S(2)}) collective-permute-start(bf16[8,16,768]{2,1,0:T(8,128)(2,1)S(1)} %pad_maximum_fusion), channel_id=1, source_target_pairs={{0,6},{1,7},{2,4},{3,5},{4,2},{5,3},{6,0},{7,1},{8,14},{9,15},{10,... | collective-permute-start | bytes 589832 | tf_op jit(solution)/shard_map/ppermute | solution.py:30
  16.9 15.2 %collective-permute-start.9 = (bf16[8,16,768]{2,1,0:T(8,128)(2,1)S(1)}, bf16[8,16,768]{2,1,0:T(8,128)(2,1)S(1)}, u32[]{:S(2)}, u32[]{:S(2)}) collective-permute-start(bf16[8,16,768]{2,1,0:T(8,128)(2,1)S(1)} %collective-permute-done.6), channel_id=1, source_target_pairs={{0,6},{1,7},{2,4},{3,5},{4,2},{5,3},{6,0},{7,1},{8,14},{9,15},{10,... | collective-permute-start | bytes 589832 | tf_op jit(solution)/shard_map/ppermute | solution.py:30
  19.1 12.6 %collective-permute-start.8 = (bf16[8,16,768]{2,1,0:T(8,128)(2,1)S(1)}, bf16[8,16,768]{2,1,0:T(8,128)(2,1)S(1)}, u32[]{:S(2)}, u32[]{:S(2)}) collective-permute-start(bf16[8,16,768]{2,1,0:T(8,128)(2,1)S(1)} %collective-permute-done.6), channel_id=1, source_target_pairs={{0,4},{1,5},{2,6},{3,7},{4,0},{5,1},{6,2},{7,3},{8,12},{9,13},{10,... | collective-permute-start | bytes 589832 | tf_op jit(solution)/shard_map/ppermute | solution.py:30
  19.6 12.0 %collective-permute-start.7 = (bf16[8,16,768]{2,1,0:T(8,128)(2,1)S(1)}, bf16[8,16,768]{2,1,0:T(8,128)(2,1)S(1)}, u32[]{:S(2)}, u32[]{:S(2)}) collective-permute-start(bf16[8,16,768]{2,1,0:T(8,128)(2,1)S(1)} %collective-permute-done.6), channel_id=1, source_target_pairs={{0,2},{1,3},{2,0},{3,1},{4,6},{5,7},{6,4},{7,5},{8,10},{9,11},{10,... | collective-permute-start | bytes 589832 | tf_op jit(solution)/shard_map/ppermute | solution.py:30
  32.1 36.7 %collective-permute-start.15 = (bf16[8,8,16,768]{3,2,1,0:T(8,128)(2,1)S(1)}, bf16[8,8,16,768]{3,2,1,0:T(8,128)(2,1)S(1)}, u32[]{:S(2)}, u32[]{:S(2)}) collective-permute-start(bf16[8,8,16,768]{3,2,1,0:T(8,128)(2,1)S(1)} %bitcast_dynamic-update-slice_fusion.8.src), channel_id=1, source_target_pairs={{0,1},{1,0},{2,3},{3,2},{4,5},{5,4},{6,7},{7,6},{8,9},{9,8},{10,11... | collective-permute-start | bytes 4718600 | tf_op jit(solution)/shard_map/ppermute | solution.py:30
  35.7 16.3 %collective-permute-start.10 = (bf16[384,768]{1,0:T(8,128)(2,1)S(1)}, bf16[384,768]{1,0:T(8,128)(2,1)S(1)}, u32[]{:S(2)}, u32[]{:S(2)}) collective-permute-start(bf16[384,768]{1,0:T(8,128)(2,1)S(1)} %get-tuple-element.37.wa), channel_id=1, source_target_pairs={{0,16},{16,0},{32,48},{48,32},{64,80},{80,64},{96,112},{112,96},{1... | collective-permute-start | bytes 1769480 | tf_op jit(solution)/shard_map/ppermute | solution.py:30
  38.3 26.3 %collective-permute-start.11 = (bf16[384,768]{1,0:T(8,128)(2,1)S(1)}, bf16[384,768]{1,0:T(8,128)(2,1)S(1)}, u32[]{:S(2)}, u32[]{:S(2)}) collective-permute-start(bf16[384,768]{1,0:T(8,128)(2,1)S(1)} %get-tuple-element.38.wb), channel_id=1, source_target_pairs={{0,16},{16,0},{32,48},{48,32},{64,80},{80,64},{96,112},{112,96},{1... | collective-permute-start | bytes 1769480 | tf_op jit(solution)/shard_map/ppermute | solution.py:30
  38.7 31.9 %collective-permute-start.22 = (bf16[256,768]{1,0:T(8,128)(2,1)S(1)}, bf16[256,768]{1,0:T(8,128)(2,1)S(1)}, u32[]{:S(2)}, u32[]{:S(2)}) collective-permute-start(bf16[256,768]{1,0:T(8,128)(2,1)S(1)} %copy-done), channel_id=1, source_target_pairs={{0,64},{16,80},{32,96},{48,112},{64,0},{80,16},{96,32},{112,48},{1... | collective-permute-start | bytes 1179656 | tf_op jit(solution)/shard_map/ppermute | solution.py:30
  40.7 32.4 %collective-permute-start.19 = (bf16[256,768]{1,0:T(8,128)(2,1)S(1)}, bf16[256,768]{1,0:T(8,128)(2,1)S(1)}, u32[]{:S(2)}, u32[]{:S(2)}) collective-permute-start(bf16[256,768]{1,0:T(8,128)(2,1)S(1)} %copy-done), channel_id=1, source_target_pairs={{0,16},{16,0},{32,48},{48,32},{64,80},{80,64},{96,112},{112,96},{1... | collective-permute-start | bytes 1179656 | tf_op jit(solution)/shard_map/ppermute | solution.py:30
  66.4 9.3 %collective-permute-start.13 = (bf16[128,768]{1,0:T(8,128)(2,1)S(1)}, bf16[128,768]{1,0:T(8,128)(2,1)S(1)}, u32[]{:S(2)}, u32[]{:S(2)}) collective-permute-start(bf16[128,768]{1,0:T(8,128)(2,1)S(1)} %get-tuple-element.42), channel_id=1, source_target_pairs={{0,32},{16,48},{32,0},{48,16},{64,96},{80,112},{96,64},{112,80},{1... | collective-permute-start | bytes 589832 | tf_op jit(solution)/shard_map/ppermute | solution.py:30
  66.5 14.8 %collective-permute-start.24 = (bf16[256,768]{1,0:T(8,128)(2,1)S(1)}, bf16[256,768]{1,0:T(8,128)(2,1)S(1)}, u32[]{:S(2)}, u32[]{:S(2)}) collective-permute-start(bf16[256,768]{1,0:T(8,128)(2,1)S(1)} %copy-done), channel_id=1, source_target_pairs={{0,96},{16,112},{32,64},{48,80},{64,32},{80,48},{96,0},{112,16},{1... | collective-permute-start | bytes 1179656 | tf_op jit(solution)/shard_map/ppermute | solution.py:30
  68.8 14.1 %collective-permute-start.20 = (bf16[256,768]{1,0:T(8,128)(2,1)S(1)}, bf16[256,768]{1,0:T(8,128)(2,1)S(1)}, u32[]{:S(2)}, u32[]{:S(2)}) collective-permute-start(bf16[256,768]{1,0:T(8,128)(2,1)S(1)} %copy-done), channel_id=1, source_target_pairs={{0,32},{16,48},{32,0},{48,16},{64,96},{80,112},{96,64},{112,80},{1... | collective-permute-start | bytes 1179656 | tf_op jit(solution)/shard_map/ppermute | solution.py:30
  70.6 10.6 %collective-permute-start.17 = (bf16[128,768]{1,0:T(8,128)(2,1)S(1)}, bf16[128,768]{1,0:T(8,128)(2,1)S(1)}, u32[]{:S(2)}, u32[]{:S(2)}) collective-permute-start(bf16[128,768]{1,0:T(8,128)(2,1)S(1)} %get-tuple-element.46), channel_id=1, source_target_pairs={{0,96},{16,112},{32,64},{48,80},{64,32},{80,48},{96,0},{112,16},{1... | collective-permute-start | bytes 589832 | tf_op jit(solution)/shard_map/ppermute | solution.py:30
  73.1 11.7 %collective-permute-start.23 = (bf16[256,768]{1,0:T(8,128)(2,1)S(1)}, bf16[256,768]{1,0:T(8,128)(2,1)S(1)}, u32[]{:S(2)}, u32[]{:S(2)}) collective-permute-start(bf16[256,768]{1,0:T(8,128)(2,1)S(1)} %collective-permute-done.22.rest_4_), channel_id=1, source_target_pairs={{0,16},{16,0},{32,48},{48,32},{64,80},{80,64},{96,112},{112,96},{1... | collective-permute-start | bytes 1179656 | tf_op jit(solution)/shard_map/ppermute | solution.py:30
  75.7 13.9 %collective-permute-start.25 = (bf16[256,768]{1,0:T(8,128)(2,1)S(1)}, bf16[256,768]{1,0:T(8,128)(2,1)S(1)}, u32[]{:S(2)}, u32[]{:S(2)}) collective-permute-start(bf16[256,768]{1,0:T(8,128)(2,1)S(1)} %collective-permute-done.19.rest_1_), channel_id=1, source_target_pairs={{0,96},{16,112},{32,64},{48,80},{64,32},{80,48},{96,0},{112,16},{1... | collective-permute-start | bytes 1179656 | tf_op jit(solution)/shard_map/ppermute | solution.py:30
  81.2 8.4 %collective-permute-start.21 = (bf16[256,768]{1,0:T(8,128)(2,1)S(1)}, bf16[256,768]{1,0:T(8,128)(2,1)S(1)}, u32[]{:S(2)}, u32[]{:S(2)}) collective-permute-start(bf16[256,768]{1,0:T(8,128)(2,1)S(1)} %collective-permute-done.19.rest_1_), channel_id=1, source_target_pairs={{0,32},{16,48},{32,0},{48,16},{64,96},{80,112},{96,64},{112,80},{1... | collective-permute-start | bytes 1179656 | tf_op jit(solution)/shard_map/ppermute | solution.py:30
  81.3 10.5 %collective-permute-start.12 = (bf16[128,768]{1,0:T(8,128)(2,1)S(1)}, bf16[128,768]{1,0:T(8,128)(2,1)S(1)}, u32[]{:S(2)}, u32[]{:S(2)}) collective-permute-start(bf16[128,768]{1,0:T(8,128)(2,1)S(1)} %get-tuple-element.40), channel_id=1, source_target_pairs={{0,32},{16,48},{32,0},{48,16},{64,96},{80,112},{96,64},{112,80},{1... | collective-permute-start | bytes 589832 | tf_op jit(solution)/shard_map/ppermute | solution.py:30
  82.9 11.0 %collective-permute-start.14 = (bf16[128,768]{1,0:T(8,128)(2,1)S(1)}, bf16[128,768]{1,0:T(8,128)(2,1)S(1)}, u32[]{:S(2)}, u32[]{:S(2)}) collective-permute-start(bf16[128,768]{1,0:T(8,128)(2,1)S(1)} %shard_map.111), channel_id=1, source_target_pairs={{0,96},{16,112},{32,64},{48,80},{64,32},{80,48},{96,0},{112,16},{1... | collective-permute-start | bytes 589832 | tf_op jit(solution)/shard_map/ppermute | solution.py:30
  84.7 13.3 %collective-permute-start.16 = (bf16[128,768]{1,0:T(8,128)(2,1)S(1)}, bf16[128,768]{1,0:T(8,128)(2,1)S(1)}, u32[]{:S(2)}, u32[]{:S(2)}) collective-permute-start(bf16[128,768]{1,0:T(8,128)(2,1)S(1)} %get-tuple-element.44), channel_id=1, source_target_pairs={{0,96},{16,112},{32,64},{48,80},{64,32},{80,48},{96,0},{112,16},{1... | collective-permute-start | bytes 589832 | tf_op jit(solution)/shard_map/ppermute | solution.py:30
  89.6 8.4 %collective-permute-start.18 = (bf16[128,768]{1,0:T(8,128)(2,1)S(1)}, bf16[128,768]{1,0:T(8,128)(2,1)S(1)}, u32[]{:S(2)}, u32[]{:S(2)}) collective-permute-start(bf16[128,768]{1,0:T(8,128)(2,1)S(1)} %shard_map.113), channel_id=1, source_target_pairs={{0,32},{16,48},{32,0},{48,16},{64,96},{80,112},{96,64},{112,80},{1... | collective-permute-start | bytes 589832 | tf_op jit(solution)/shard_map/ppermute | solution.py:30
  108.9 8.2 %collective-permute-start.27 = (bf16[16,6144]{1,0:T(8,128)(2,1)S(1)}, bf16[16,6144]{1,0:T(8,128)(2,1)S(1)}, u32[]{:S(2)}, u32[]{:S(2)}) collective-permute-start(bf16[16,6144]{1,0:T(8,128)(2,1)S(1)} %get-tuple-element.50), channel_id=1, source_target_pairs={{0,2},{1,3},{2,0},{3,1},{4,6},{5,7},{6,4},{7,5},{8,10},{9,11},{10,... | collective-permute-start | bytes 589832 | tf_op jit(solution)/shard_map/ppermute | solution.py:30
  109.7 8.5 %collective-permute-start.28 = (bf16[16,6144]{1,0:T(8,128)(2,1)S(1)}, bf16[16,6144]{1,0:T(8,128)(2,1)S(1)}, u32[]{:S(2)}, u32[]{:S(2)}) collective-permute-start(bf16[16,6144]{1,0:T(8,128)(2,1)S(1)} %get-tuple-element.51), channel_id=1, source_target_pairs={{0,6},{1,7},{2,4},{3,5},{4,2},{5,3},{6,0},{7,1},{8,14},{9,15},{10,... | collective-permute-start | bytes 589832 | tf_op jit(solution)/shard_map/ppermute | solution.py:30
  122.7 8.8 %collective-permute-start.36 = (bf16[16,6144]{1,0:T(8,128)(2,1)S(1)}, bf16[16,6144]{1,0:T(8,128)(2,1)S(1)}, u32[]{:S(2)}, u32[]{:S(2)}) collective-permute-start(bf16[16,6144]{1,0:T(8,128)(2,1)S(1)} %shard_map.119), channel_id=1, source_target_pairs={{0,6},{1,7},{2,4},{3,5},{4,2},{5,3},{6,0},{7,1},{8,14},{9,15},{10,... | collective-permute-start | bytes 589832 | tf_op jit(solution)/shard_map/ppermute | solution.py:30
  126.7 9.8 %collective-permute-start.40 = (bf16[16,6144]{1,0:T(8,128)(2,1)S(1)}, bf16[16,6144]{1,0:T(8,128)(2,1)S(1)}, u32[]{:S(2)}, u32[]{:S(2)}) collective-permute-start(bf16[16,6144]{1,0:T(8,128)(2,1)S(1)} %collective-permute-done.37), channel_id=1, source_target_pairs={{0,6},{1,7},{2,4},{3,5},{4,2},{5,3},{6,0},{7,1},{8,14},{9,15},{10,... | collective-permute-start | bytes 589832 | tf_op jit(solution)/shard_map/ppermute | solution.py:30
  136.6 16.3 %collective-permute-start.41 = (bf16[8,16,6144]{2,1,0:T(8,128)(2,1)S(1)}, bf16[8,16,6144]{2,1,0:T(8,128)(2,1)S(1)}, u32[]{:S(2)}, u32[]{:S(2)}) collective-permute-start(bf16[8,16,6144]{2,1,0:T(8,128)(2,1)S(1)} %bitcast_dynamic-update-slice_fusion.src), channel_id=1, source_target_pairs={{0,1},{1,0},{2,3},{3,2},{4,5},{5,4},{6,7},{7,6},{8,9},{9,8},{10,11... | collective-permute-start | bytes 4718600 | tf_op jit(solution)/shard_map/ppermute | solution.py:30
  155.9 9.3 %collective-permute-start.42 = (bf16[8,16,3072]{2,1,0:T(8,128)(2,1)S(1)}, bf16[8,16,3072]{2,1,0:T(8,128)(2,1)S(1)}, u32[]{:S(2)}, u32[]{:S(2)}) collective-permute-start(bf16[8,16,3072]{2,1,0:T(8,128)(2,1)S(1)} %shard_map.123), channel_id=1, source_target_pairs={{0,1},{1,0},{2,3},{3,2},{4,5},{5,4},{6,7},{7,6},{8,9},{9,8},{10,11... | collective-permute-start | bytes 2359304 | tf_op jit(solution)/shard_map/ppermute | solution.py:30
  159.7 10.0 %collective-permute-start.48 = (bf16[16,3072]{1,0:T(8,128)(2,1)S(1)}, bf16[16,3072]{1,0:T(8,128)(2,1)S(1)}, u32[]{:S(2)}, u32[]{:S(2)}) collective-permute-start(bf16[16,3072]{1,0:T(8,128)(2,1)S(1)} %get-tuple-element.65), channel_id=1, source_target_pairs={{0,12},{1,13},{2,14},{3,15},{4,8},{5,9},{6,10},{7,11},{8,4},{9,5},... | collective-permute-start | bytes 294920 | tf_op jit(solution)/shard_map/ppermute | solution.py:30
  166.5 14.9 %collective-permute-start.43 = (bf16[2,16,3072]{2,1,0:T(8,128)(2,1)S(1)}, bf16[2,16,3072]{2,1,0:T(8,128)(2,1)S(1)}, u32[]{:S(2)}, u32[]{:S(2)}) collective-permute-start(bf16[2,16,3072]{2,1,0:T(8,128)(2,1)S(1)} %pad_maximum_fusion.1), channel_id=1, source_target_pairs={{0,2},{1,3},{2,0},{3,1},{4,6},{5,7},{6,4},{7,5},{8,10},{9,11},{10,... | collective-permute-start | bytes 589832 | tf_op jit(solution)/shard_map/ppermute | solution.py:30
  169.7 11.7 %collective-permute-start.44 = (bf16[2,16,3072]{2,1,0:T(8,128)(2,1)S(1)}, bf16[2,16,3072]{2,1,0:T(8,128)(2,1)S(1)}, u32[]{:S(2)}, u32[]{:S(2)}) collective-permute-start(bf16[2,16,3072]{2,1,0:T(8,128)(2,1)S(1)} %pad_maximum_fusion.2), channel_id=1, source_target_pairs={{0,4},{1,5},{2,6},{3,7},{4,0},{5,1},{6,2},{7,3},{8,12},{9,13},{10,... | collective-permute-start | bytes 589832 | tf_op jit(solution)/shard_map/ppermute | solution.py:30
  170.2 11.2 %collective-permute-start.45 = (bf16[2,16,3072]{2,1,0:T(8,128)(2,1)S(1)}, bf16[2,16,3072]{2,1,0:T(8,128)(2,1)S(1)}, u32[]{:S(2)}, u32[]{:S(2)}) collective-permute-start(bf16[2,16,3072]{2,1,0:T(8,128)(2,1)S(1)} %pad_maximum_fusion.3), channel_id=1, source_target_pairs={{0,6},{1,7},{2,4},{3,5},{4,2},{5,3},{6,0},{7,1},{8,14},{9,15},{10,... | collective-permute-start | bytes 589832 | tf_op jit(solution)/shard_map/ppermute | solution.py:30
  172.2 9.2 %collective-permute-start.51 = (bf16[16,3072]{1,0:T(8,128)(2,1)S(1)}, bf16[16,3072]{1,0:T(8,128)(2,1)S(1)}, u32[]{:S(2)}, u32[]{:S(2)}) collective-permute-start(bf16[16,3072]{1,0:T(8,128)(2,1)S(1)} %get-tuple-element.69), channel_id=1, source_target_pairs={{0,10},{1,11},{2,8},{3,9},{4,14},{5,15},{6,12},{7,13},{8,2},{9,3},... | collective-permute-start | bytes 294920 | tf_op jit(solution)/shard_map/ppermute | solution.py:30
  172.4 9.0 %collective-permute-start.50 = (bf16[16,3072]{1,0:T(8,128)(2,1)S(1)}, bf16[16,3072]{1,0:T(8,128)(2,1)S(1)}, u32[]{:S(2)}, u32[]{:S(2)}) collective-permute-start(bf16[16,3072]{1,0:T(8,128)(2,1)S(1)} %get-tuple-element.70), channel_id=1, source_target_pairs={{0,8},{1,9},{2,10},{3,11},{4,12},{5,13},{6,14},{7,15},{8,0},{9,1},... | collective-permute-start | bytes 294920 | tf_op jit(solution)/shard_map/ppermute | solution.py:30
  (27 other events, 205.3 us)

commit v6 on v5

--- a/solution.py
+++ b/solution.py
@@ -18,7 +18,7 @@
 
 
 SENDS = (
-    ("l", 6), ("l", 7), ("l", 5), ("b", 2), ("h", 6), ("b", 3), ("h", 7), ("b", 1),
+    ("l", 7), ("l", 6), ("l", 5), ("b", 3), ("h", 7), ("b", 2), ("h", 6), ("b", 1),
     ("h", 5), ("l", 4), ("h", 4),
 )
 
@@ -155,8 +155,8 @@
     spread(left[...], rest[:8], rest[8])
 
 
-def pair_kernel(a_ref, b_ref, *outs):
-    for j, o_ref in enumerate(outs):
+def pair_kernel(picks, a_ref, b_ref, *outs):
+    for j, o_ref in zip(picks, outs):
         rows = o_ref.shape[0]
         part = a_ref[j * rows:(j + 1) * rows, :].astype(F32) + b_ref[
             j * rows:(j + 1) * rows, :
@@ -317,11 +317,11 @@
         return swap(v, "cb", 16, flip)
 
     y = cb(value, 8)
+    x3 = cb(value, 6)
     x1 = cb(value, 2)
-    x3 = cb(value, 6)
     x2 = cb(value, 4)
+    y3 = cb(y, 6)
     y1 = cb(y, 2)
-    y3 = cb(y, 6)
     y2 = cb(y, 4) if across else cb(x2, 8)
     return [value, x1, x2, x3, y, y1, y2, y3]
 
@@ -373,12 +373,16 @@
     )(ids, a0, plain_a, sum_a, b0, plain_b, sum_b, *wo)
     taken = cb(give, 1)
     keep = call(keep_kernel, [((128, model), BF)], n_in=9)(left, *wo)[0]
-    blocks = call(pair_kernel, [((16, model), F32)] + [((16, model), BF)] * 7, n_in=2)(
-        keep, taken
-    )
-    far1, far3 = cb(blocks[5], 2), cb(blocks[7], 6)
+    blocks = {}
+    for picks in ((6, 5, 7), (1, 3, 2, 4, 0)):
+        kinds = [((16, model), BF if e else F32) for e in picks]
+        run = call(functools.partial(pair_kernel, picks), kinds, n_in=2)
+        blocks.update(zip(picks, run(keep, taken)))
+    far3 = cb(blocks[7], 6)
+    far1 = cb(blocks[5], 2)
     far2 = cb(blocks[6], 8)
-    near1, near3 = cb(blocks[1], 2), cb(blocks[3], 6)
+    near3 = cb(blocks[3], 6)
+    near1 = cb(blocks[1], 2)
     side = add(blocks[4], far1, far3)
     deep = add(blocks[2], far2)
     last2 = cb(deep, 4)

time: 201 us -> 200 us (level)
    pallas_call x13 -> x14, Pallas kernels: 16.2 us -> 16.2 us  [go(): return run(*args[:smem], *held)]
where the time goes in v6:
time: 200 us
  waiting for transfers between devices  82.7 us (41%)
  starting transfers between devices  72.3 us (36%)
  Pallas kernels  27.3 us (14%)
  blocking collectives  15.6 us (8%)
    ppermute x54, waiting for transfers between devices, swap(): return lax.ppermute(value, axis, [(i, i ^ flip) for i in range(size)])  82.7 us
    ppermute x54, starting transfers between devices, swap(): return lax.ppermute(value, axis, [(i, i ^ flip) for i in range(size)])  72.3 us
    pallas_call x14, Pallas kernels, go(): return run(*args[:smem], *held)  16.2 us
    all_to_all x1, blocking collectives, work(): out = lax.all_to_all(outs, 'cb', 0, 0, tiled=True)  15.6 us
    pallas_call x1, Pallas kernels, fetch(): pl.pallas_call(fetch_kernel, out_shape=[pltpu.VMEM(s, BF) for s in shapes...  4.62 us
    pallas_call x1, Pallas kernels, load(): pl.pallas_call(load_kernel, out_shape=pltpu.VMEM(value.shape, value.dtype...  4.6 us
  transfers between devices with their start and end apart: 54, of which 27 were waited for; matrix products, arithmetic and copies ran while one was open for 0% of the time, Pallas kernels for 8%

profile of v6, /device:TPU:1, one launch (start us, length us, event | category | flops | bytes accessed | tf_op | source)
XLA Modules:
  0.0 200.2 jit_solution(7813490806682665017)
XLA Ops:
  2.7 4.7 %collective-permute-start.2 = (bf16[2,16,768]{2,1,0:T(8,128)(2,1)S(1)}, bf16[2,16,768]{2,1,0:T(8,128)(2,1)S(1)}, u32[]{:S(2)}, u32[]{:S(2)}) collective-permute-start(bf16[2,16,768]{2,1,0:T(8,128)(2,1)S(1)} %get-tuple-element.76), channel_id=1, source_target_pairs={{0,96},{16,112},{32,64},{48,80},{64,32},{80,48},{96,0},{112,16},{1... | collective-permute-start | bytes 147464 | tf_op jit(solution)/shard_map/ppermute | solution.py:30
  8.8 3.0 %collective-permute-done.1 = bf16[2,16,768]{2,1,0:T(8,128)(2,1)S(1)} collective-permute-done((bf16[2,16,768]{2,1,0:T(8,128)(2,1)S(1)}, bf16[2,16,768]{2,1,0:T(8,128)(2,1)S(1)}, u32[]{:S(2)}, u32[]{:S(2)}) %collective-permute-start.1) | collective-permute-done | bytes 49184 | tf_op jit(solution)/shard_map/ppermute | solution.py:30
  16.9 2.1 %collective-permute-start.9 = (bf16[8,16,768]{2,1,0:T(8,128)(2,1)S(1)}, bf16[8,16,768]{2,1,0:T(8,128)(2,1)S(1)}, u32[]{:S(2)}, u32[]{:S(2)}) collective-permute-start(bf16[8,16,768]{2,1,0:T(8,128)(2,1)S(1)} %collective-permute-done.6), channel_id=1, source_target_pairs={{0,6},{1,7},{2,4},{3,5},{4,2},{5,3},{6,0},{7,1},{8,14},{9,15},{10,... | collective-permute-start | bytes 589832 | tf_op jit(solution)/shard_map/ppermute | solution.py:30
  20.3 3.6 %collective-permute-done.4 = bf16[8,16,768]{2,1,0:T(8,128)(2,1)S(1)} collective-permute-done((bf16[8,16,768]{2,1,0:T(8,128)(2,1)S(1)}, bf16[8,16,768]{2,1,0:T(8,128)(2,1)S(1)}, u32[]{:S(2)}, u32[]{:S(2)}) %collective-permute-start.4) | collective-permute-done | bytes 196640 | tf_op jit(solution)/shard_map/ppermute | solution.py:30
  24.0 7.7 %collective-permute-done.7 = bf16[8,16,768]{2,1,0:T(8,128)(2,1)S(1)} collective-permute-done((bf16[8,16,768]{2,1,0:T(8,128)(2,1)S(1)}, bf16[8,16,768]{2,1,0:T(8,128)(2,1)S(1)}, u32[]{:S(2)}, u32[]{:S(2)}) %collective-permute-start.7) | collective-permute-done | bytes 196640 | tf_op jit(solution)/shard_map/ppermute | solution.py:30
  32.1 3.6 %collective-permute-start.15 = (bf16[8,8,16,768]{3,2,1,0:T(8,128)(2,1)S(1)}, bf16[8,8,16,768]{3,2,1,0:T(8,128)(2,1)S(1)}, u32[]{:S(2)}, u32[]{:S(2)}) collective-permute-start(bf16[8,8,16,768]{3,2,1,0:T(8,128)(2,1)S(1)} %bitcast_dynamic-update-slice_fusion.8.src), channel_id=1, source_target_pairs={{0,1},{1,0},{2,3},{3,2},{4,5},{5,4},{6,7},{7,6},{8,9},{9,8},{10,11... | collective-permute-start | bytes 4718600 | tf_op jit(solution)/shard_map/ppermute | solution.py:30
  35.7 2.6 %collective-permute-start.10 = (bf16[384,768]{1,0:T(8,128)(2,1)S(1)}, bf16[384,768]{1,0:T(8,128)(2,1)S(1)}, u32[]{:S(2)}, u32[]{:S(2)}) collective-permute-start(bf16[384,768]{1,0:T(8,128)(2,1)S(1)} %get-tuple-element.37.wa), channel_id=1, source_target_pairs={{0,16},{16,0},{32,48},{48,32},{64,80},{80,64},{96,112},{112,96},{1... | collective-permute-start | bytes 1769480 | tf_op jit(solution)/shard_map/ppermute | solution.py:30
  40.7 2.6 %collective-permute-start.19 = (bf16[256,768]{1,0:T(8,128)(2,1)S(1)}, bf16[256,768]{1,0:T(8,128)(2,1)S(1)}, u32[]{:S(2)}, u32[]{:S(2)}) collective-permute-start(bf16[256,768]{1,0:T(8,128)(2,1)S(1)} %copy-done), channel_id=1, source_target_pairs={{0,16},{16,0},{32,48},{48,32},{64,80},{80,64},{96,112},{112,96},{1... | collective-permute-start | bytes 1179656 | tf_op jit(solution)/shard_map/ppermute | solution.py:30
  43.3 8.7 %collective-permute-done.10.va = bf16[384,768]{1,0:T(8,128)(2,1)S(1)} collective-permute-done((bf16[384,768]{1,0:T(8,128)(2,1)S(1)}, bf16[384,768]{1,0:T(8,128)(2,1)S(1)}, u32[]{:S(2)}, u32[]{:S(2)}) %collective-permute-start.10) | collective-permute-done | bytes 589856 | tf_op jit(solution)/shard_map/ppermute | solution.py:30
  52.0 12.6 %collective-permute-done.11.vb = bf16[384,768]{1,0:T(8,128)(2,1)S(1)} collective-permute-done((bf16[384,768]{1,0:T(8,128)(2,1)S(1)}, bf16[384,768]{1,0:T(8,128)(2,1)S(1)}, u32[]{:S(2)}, u32[]{:S(2)}) %collective-permute-start.11) | collective-permute-done | bytes 589856 | tf_op jit(solution)/shard_map/ppermute | solution.py:30
  66.5 2.2 %collective-permute-start.24 = (bf16[256,768]{1,0:T(8,128)(2,1)S(1)}, bf16[256,768]{1,0:T(8,128)(2,1)S(1)}, u32[]{:S(2)}, u32[]{:S(2)}) collective-permute-start(bf16[256,768]{1,0:T(8,128)(2,1)S(1)} %copy-done), channel_id=1, source_target_pairs={{0,96},{16,112},{32,64},{48,80},{64,32},{80,48},{96,0},{112,16},{1... | collective-permute-start | bytes 1179656 | tf_op jit(solution)/shard_map/ppermute | solution.py:30
  73.1 2.6 %collective-permute-start.23 = (bf16[256,768]{1,0:T(8,128)(2,1)S(1)}, bf16[256,768]{1,0:T(8,128)(2,1)S(1)}, u32[]{:S(2)}, u32[]{:S(2)}) collective-permute-start(bf16[256,768]{1,0:T(8,128)(2,1)S(1)} %collective-permute-done.22.rest_4_), channel_id=1, source_target_pairs={{0,16},{16,0},{32,48},{48,32},{64,80},{80,64},{96,112},{112,96},{1... | collective-permute-start | bytes 1179656 | tf_op jit(solution)/shard_map/ppermute | solution.py:30
  76.9 4.3 %collective-permute-done.17.refs_1_ = bf16[128,768]{1,0:T(8,128)(2,1)S(1)} collective-permute-done((bf16[128,768]{1,0:T(8,128)(2,1)S(1)}, bf16[128,768]{1,0:T(8,128)(2,1)S(1)}, u32[]{:S(2)}, u32[]{:S(2)}) %collective-permute-start.17) | collective-permute-done | bytes 196640 | tf_op jit(solution)/shard_map/ppermute | solution.py:30
  85.5 4.1 %collective-permute-done.25.rest_7_ = bf16[256,768]{1,0:T(8,128)(2,1)S(1)} collective-permute-done((bf16[256,768]{1,0:T(8,128)(2,1)S(1)}, bf16[256,768]{1,0:T(8,128)(2,1)S(1)}, u32[]{:S(2)}, u32[]{:S(2)}) %collective-permute-start.25) | collective-permute-done | bytes 393248 | tf_op jit(solution)/shard_map/ppermute | solution.py:30
  89.6 2.1 %collective-permute-done.12.a1 = bf16[128,768]{1,0:T(8,128)(2,1)S(1)} collective-permute-done((bf16[128,768]{1,0:T(8,128)(2,1)S(1)}, bf16[128,768]{1,0:T(8,128)(2,1)S(1)}, u32[]{:S(2)}, u32[]{:S(2)}) %collective-permute-start.12) | collective-permute-done | bytes 196640 | tf_op jit(solution)/shard_map/ppermute | solution.py:30
  93.8 4.2 %collective-permute-done.16.b1 = bf16[128,768]{1,0:T(8,128)(2,1)S(1)} collective-permute-done((bf16[128,768]{1,0:T(8,128)(2,1)S(1)}, bf16[128,768]{1,0:T(8,128)(2,1)S(1)}, u32[]{:S(2)}, u32[]{:S(2)}) %collective-permute-start.16) | collective-permute-done | bytes 196640 | tf_op jit(solution)/shard_map/ppermute | solution.py:30
  100.2 3.2 %collective-permute-start.26 = (bf16[128,6144]{1,0:T(8,128)(2,1)S(1)}, bf16[128,6144]{1,0:T(8,128)(2,1)S(1)}, u32[]{:S(2)}, u32[]{:S(2)}) collective-permute-start(bf16[128,6144]{1,0:T(8,128)(2,1)S(1)} %get-tuple-element.48), channel_id=1, source_target_pairs={{0,1},{1,0},{2,3},{3,2},{4,5},{5,4},{6,7},{7,6},{8,9},{9,8},{10,11... | collective-permute-start | bytes 4718600 | tf_op jit(solution)/shard_map/ppermute | solution.py:30
  103.9 2.4 %collective-permute-done.26.b_ref = bf16[128,6144]{1,0:T(8,128)(2,1)S(1)} collective-permute-done((bf16[128,6144]{1,0:T(8,128)(2,1)S(1)}, bf16[128,6144]{1,0:T(8,128)(2,1)S(1)}, u32[]{:S(2)}, u32[]{:S(2)}) %collective-permute-start.26) | collective-permute-done | bytes 1572896 | tf_op jit(solution)/shard_map/ppermute | solution.py:30
  118.7 2.7 %collective-permute-done.33.rest_4_ = bf16[16,6144]{1,0:T(8,128)(2,1)S(1)} collective-permute-done((bf16[16,6144]{1,0:T(8,128)(2,1)S(1)}, bf16[16,6144]{1,0:T(8,128)(2,1)S(1)}, u32[]{:S(2)}, u32[]{:S(2)}) %collective-permute-start.33) | collective-permute-done | bytes 196640 | tf_op jit(solution)/shard_map/ppermute | solution.py:30
  127.9 2.7 %collective-permute-done.35 = bf16[16,6144]{1,0:T(8,128)(2,1)S(1)} collective-permute-done((bf16[16,6144]{1,0:T(8,128)(2,1)S(1)}, bf16[16,6144]{1,0:T(8,128)(2,1)S(1)}, u32[]{:S(2)}, u32[]{:S(2)}) %collective-permute-start.35) | collective-permute-done | bytes 196640 | tf_op jit(solution)/shard_map/ppermute | solution.py:30
  131.3 3.4 %collective-permute-done.38 = bf16[16,6144]{1,0:T(8,128)(2,1)S(1)} collective-permute-done((bf16[16,6144]{1,0:T(8,128)(2,1)S(1)}, bf16[16,6144]{1,0:T(8,128)(2,1)S(1)}, u32[]{:S(2)}, u32[]{:S(2)}) %collective-permute-start.38) | collective-permute-done | bytes 196640 | tf_op jit(solution)/shard_map/ppermute | solution.py:30
  136.4 7.1 %collective-permute-start.41 = (bf16[8,16,6144]{2,1,0:T(8,128)(2,1)S(1)}, bf16[8,16,6144]{2,1,0:T(8,128)(2,1)S(1)}, u32[]{:S(2)}, u32[]{:S(2)}) collective-permute-start(bf16[8,16,6144]{2,1,0:T(8,128)(2,1)S(1)} %bitcast_dynamic-update-slice_fusion.src), channel_id=1, source_target_pairs={{0,1},{1,0},{2,3},{3,2},{4,5},{5,4},{6,7},{7,6},{8,9},{9,8},{10,11... | collective-permute-start | bytes 4718600 | tf_op jit(solution)/shard_map/ppermute | solution.py:30
  143.4 4.6 %shard_map.121.din = bf16[6144,1024]{1,0:T(8,128)(2,1)S(1)} custom-call(bf16[6144,1024]{1,0:T(8,128)(2,1)} %bitcast.62), custom_call_target="tpu_custom_call" | custom-call | tf_op jit(solution)/shard_map/pallas_call | solution.py:214
  148.1 4.6 %shard_map.122 = (bf16[1024,3072]{1,0:T(8,128)(2,1)S(1)}, bf16[16,16,1024]{2,1,0:T(8,128)(2,1)S(1)}) custom-call(s32[3]{0:T(128)S(1)} %pad_add_fusion.ids, s32[1,256]{1,0:T(1,128)S(1)} %bitcast.61, bf16[1024,3072]{1,0:T(8,128)(2,1)} %bitcast.63, bf16[2048,1024]{1,0:T(8,128)(2,1)} %bitcast.64), custom_call_target="tpu_custom_call" | custom-call | tf_op jit(solution)/shard_map/pallas_call | solution.py:249
  152.7 3.0 %shard_map.124 = bf16[8,16,3072]{2,1,0:T(8,128)(2,1)S(1)} custom-call(bf16[8,16,6144]{2,1,0:T(8,128)(2,1)S(1)} %collective-permute-done.41.src, bf16[6144,1024]{1,0:T(8,128)(2,1)S(1)} %shard_map.121.din, bf16[16,16,1024]{2,1,0:T(8,128)(2,1)S(1)} %get-tuple-element.57.emb, f32[1,1024]{1,0:T(1,128)S(1)} %copy-done.3, bf16[1024,3072]{1,0:T(8,128)(2,1)S(1)} %get-tuple-element.58.wqkv), custom_call_target="tpu_custom_call" | custom-call | tf_op jit(solution)/shard_map/pallas_call | solution.py:46
  156.0 3.0 %shard_map.123 = (bf16[16,3072]{1,0:T(8,128)(2,1)S(1)}, bf16[16,3072]{1,0:T(8,128)(2,1)S(1)}, bf16[16,3072]{1,0:T(8,128)(2,1)S(1)}, bf16[16,3072]{1,0:T(8,128)(2...) custom-call(bf16[8,16,6144]{2,1,0:T(8,128)(2,1)S(1)} %bitcast_dynami, ...), custom_call_target="tpu_custom_call" | custom-call | tf_op jit(solution)/shard_map/pallas_call | solution.py:46
  159.5 2.8 %collective-permute-start.48 = (bf16[16,3072]{1,0:T(8,128)(2,1)S(1)}, bf16[16,3072]{1,0:T(8,128)(2,1)S(1)}, u32[]{:S(2)}, u32[]{:S(2)}) collective-permute-start(bf16[16,3072]{1,0:T(8,128)(2,1)S(1)} %get-tuple-element.65), channel_id=1, source_target_pairs={{0,12},{1,13},{2,14},{3,15},{4,8},{5,9},{6,10},{7,11},{8,4},{9,5},... | collective-permute-start | bytes 294920 | tf_op jit(solution)/shard_map/ppermute | solution.py:30
  162.2 2.7 %collective-permute-start.49 = (bf16[16,3072]{1,0:T(8,128)(2,1)S(1)}, bf16[16,3072]{1,0:T(8,128)(2,1)S(1)}, u32[]{:S(2)}, u32[]{:S(2)}) collective-permute-start(bf16[16,3072]{1,0:T(8,128)(2,1)S(1)} %get-tuple-element.66), channel_id=1, source_target_pairs={{0,14},{1,15},{2,12},{3,13},{4,10},{5,11},{6,8},{7,9},{8,6},{9,7},... | collective-permute-start | bytes 294920 | tf_op jit(solution)/shard_map/ppermute | solution.py:30
  166.2 3.3 %collective-permute-start.43 = (bf16[2,16,3072]{2,1,0:T(8,128)(2,1)S(1)}, bf16[2,16,3072]{2,1,0:T(8,128)(2,1)S(1)}, u32[]{:S(2)}, u32[]{:S(2)}) collective-permute-start(bf16[2,16,3072]{2,1,0:T(8,128)(2,1)S(1)} %pad_maximum_fusion.1), channel_id=1, source_target_pairs={{0,2},{1,3},{2,0},{3,1},{4,6},{5,7},{6,4},{7,5},{8,10},{9,11},{10,... | collective-permute-start | bytes 589832 | tf_op jit(solution)/shard_map/ppermute | solution.py:30
  173.3 7.9 %collective-permute-done.51.rest_8_ = bf16[16,3072]{1,0:T(8,128)(2,1)S(1)} collective-permute-done((bf16[16,3072]{1,0:T(8,128)(2,1)S(1)}, bf16[16,3072]{1,0:T(8,128)(2,1)S(1)}, u32[]{:S(2)}, u32[]{:S(2)}) %collective-permute-start.51) | collective-permute-done | bytes 98336 | tf_op jit(solution)/shard_map/ppermute | solution.py:30
  181.2 2.6 %shard_map.125 = bf16[16,16,1024]{2,1,0:T(8,128)(2,1)S(1)} custom-call(s32[3]{0:T(128)S(1)} %pad_add_fusion.ids, bf16[16,3072]{1,0:T(8,128)(2,1)S(1)} %get-tuple-element.59.low, bf16[16,3072]{1,0:T(8,128)(2,1)S(1)} %get-tuple-element.74.high, bf16[2,16,3072]{2,1,0:T(8,128)(2,1)S(1)} %collective-permute-done.43.rest_0_, ...), custom_call_target="tpu_custom_call" | custom-call | tf_op jit(solution)/shard_map/pallas_call | solution.py:46
  183.8 15.6 %all_to_all.5 = bf16[16,16,1024]{2,1,0:T(8,128)(2,1)S(1)} all-to-all(bf16[16,16,1024]{2,1,0:T(8,128)(2,1)S(1)} %shard_map.125), channel_id=1, replica_groups=mesh['fsdp'=8,'cb'=16] {'cb'}, dimensions={0} | all-to-all | bytes 1048576 | tf_op jit(solution)/shard_map/all_to_all | solution.py:429
  (128 shorter events, 56.8 us)
Async XLA Ops:
  14.4 9.5 %collective-permute-start.5 = (bf16[8,16,768]{2,1,0:T(8,128)(2,1)S(1)}, bf16[8,16,768]{2,1,0:T(8,128)(2,1)S(1)}, u32[]{:S(2)}, u32[]{:S(2)}) collective-permute-start(bf16[8,16,768]{2,1,0:T(8,128)(2,1)S(1)} %pad_maximum_fusion), channel_id=1, source_target_pairs={{0,6},{1,7},{2,4},{3,5},{4,2},{5,3},{6,0},{7,1},{8,14},{9,15},{10,... | collective-permute-start | bytes 589832 | tf_op jit(solution)/shard_map/ppermute | solution.py:30
  16.9 15.2 %collective-permute-start.9 = (bf16[8,16,768]{2,1,0:T(8,128)(2,1)S(1)}, bf16[8,16,768]{2,1,0:T(8,128)(2,1)S(1)}, u32[]{:S(2)}, u32[]{:S(2)}) collective-permute-start(bf16[8,16,768]{2,1,0:T(8,128)(2,1)S(1)} %collective-permute-done.6), channel_id=1, source_target_pairs={{0,6},{1,7},{2,4},{3,5},{4,2},{5,3},{6,0},{7,1},{8,14},{9,15},{10,... | collective-permute-start | bytes 589832 | tf_op jit(solution)/shard_map/ppermute | solution.py:30
  19.1 12.6 %collective-permute-start.8 = (bf16[8,16,768]{2,1,0:T(8,128)(2,1)S(1)}, bf16[8,16,768]{2,1,0:T(8,128)(2,1)S(1)}, u32[]{:S(2)}, u32[]{:S(2)}) collective-permute-start(bf16[8,16,768]{2,1,0:T(8,128)(2,1)S(1)} %collective-permute-done.6), channel_id=1, source_target_pairs={{0,4},{1,5},{2,6},{3,7},{4,0},{5,1},{6,2},{7,3},{8,12},{9,13},{10,... | collective-permute-start | bytes 589832 | tf_op jit(solution)/shard_map/ppermute | solution.py:30
  19.6 12.0 %collective-permute-start.7 = (bf16[8,16,768]{2,1,0:T(8,128)(2,1)S(1)}, bf16[8,16,768]{2,1,0:T(8,128)(2,1)S(1)}, u32[]{:S(2)}, u32[]{:S(2)}) collective-permute-start(bf16[8,16,768]{2,1,0:T(8,128)(2,1)S(1)} %collective-permute-done.6), channel_id=1, source_target_pairs={{0,2},{1,3},{2,0},{3,1},{4,6},{5,7},{6,4},{7,5},{8,10},{9,11},{10,... | collective-permute-start | bytes 589832 | tf_op jit(solution)/shard_map/ppermute | solution.py:30
  32.1 36.7 %collective-permute-start.15 = (bf16[8,8,16,768]{3,2,1,0:T(8,128)(2,1)S(1)}, bf16[8,8,16,768]{3,2,1,0:T(8,128)(2,1)S(1)}, u32[]{:S(2)}, u32[]{:S(2)}) collective-permute-start(bf16[8,8,16,768]{3,2,1,0:T(8,128)(2,1)S(1)} %bitcast_dynamic-update-slice_fusion.8.src), channel_id=1, source_target_pairs={{0,1},{1,0},{2,3},{3,2},{4,5},{5,4},{6,7},{7,6},{8,9},{9,8},{10,11... | collective-permute-start | bytes 4718600 | tf_op jit(solution)/shard_map/ppermute | solution.py:30
  35.7 16.3 %collective-permute-start.10 = (bf16[384,768]{1,0:T(8,128)(2,1)S(1)}, bf16[384,768]{1,0:T(8,128)(2,1)S(1)}, u32[]{:S(2)}, u32[]{:S(2)}) collective-permute-start(bf16[384,768]{1,0:T(8,128)(2,1)S(1)} %get-tuple-element.37.wa), channel_id=1, source_target_pairs={{0,16},{16,0},{32,48},{48,32},{64,80},{80,64},{96,112},{112,96},{1... | collective-permute-start | bytes 1769480 | tf_op jit(solution)/shard_map/ppermute | solution.py:30
  38.3 26.3 %collective-permute-start.11 = (bf16[384,768]{1,0:T(8,128)(2,1)S(1)}, bf16[384,768]{1,0:T(8,128)(2,1)S(1)}, u32[]{:S(2)}, u32[]{:S(2)}) collective-permute-start(bf16[384,768]{1,0:T(8,128)(2,1)S(1)} %get-tuple-element.38.wb), channel_id=1, source_target_pairs={{0,16},{16,0},{32,48},{48,32},{64,80},{80,64},{96,112},{112,96},{1... | collective-permute-start | bytes 1769480 | tf_op jit(solution)/shard_map/ppermute | solution.py:30
  38.7 31.9 %collective-permute-start.22 = (bf16[256,768]{1,0:T(8,128)(2,1)S(1)}, bf16[256,768]{1,0:T(8,128)(2,1)S(1)}, u32[]{:S(2)}, u32[]{:S(2)}) collective-permute-start(bf16[256,768]{1,0:T(8,128)(2,1)S(1)} %copy-done), channel_id=1, source_target_pairs={{0,64},{16,80},{32,96},{48,112},{64,0},{80,16},{96,32},{112,48},{1... | collective-permute-start | bytes 1179656 | tf_op jit(solution)/shard_map/ppermute | solution.py:30
  40.7 32.4 %collective-permute-start.19 = (bf16[256,768]{1,0:T(8,128)(2,1)S(1)}, bf16[256,768]{1,0:T(8,128)(2,1)S(1)}, u32[]{:S(2)}, u32[]{:S(2)}) collective-permute-start(bf16[256,768]{1,0:T(8,128)(2,1)S(1)} %copy-done), channel_id=1, source_target_pairs={{0,16},{16,0},{32,48},{48,32},{64,80},{80,64},{96,112},{112,96},{1... | collective-permute-start | bytes 1179656 | tf_op jit(solution)/shard_map/ppermute | solution.py:30
  66.4 9.3 %collective-permute-start.13 = (bf16[128,768]{1,0:T(8,128)(2,1)S(1)}, bf16[128,768]{1,0:T(8,128)(2,1)S(1)}, u32[]{:S(2)}, u32[]{:S(2)}) collective-permute-start(bf16[128,768]{1,0:T(8,128)(2,1)S(1)} %get-tuple-element.42), channel_id=1, source_target_pairs={{0,32},{16,48},{32,0},{48,16},{64,96},{80,112},{96,64},{112,80},{1... | collective-permute-start | bytes 589832 | tf_op jit(solution)/shard_map/ppermute | solution.py:30
  66.5 14.8 %collective-permute-start.24 = (bf16[256,768]{1,0:T(8,128)(2,1)S(1)}, bf16[256,768]{1,0:T(8,128)(2,1)S(1)}, u32[]{:S(2)}, u32[]{:S(2)}) collective-permute-start(bf16[256,768]{1,0:T(8,128)(2,1)S(1)} %copy-done), channel_id=1, source_target_pairs={{0,96},{16,112},{32,64},{48,80},{64,32},{80,48},{96,0},{112,16},{1... | collective-permute-start | bytes 1179656 | tf_op jit(solution)/shard_map/ppermute | solution.py:30
  68.8 14.1 %collective-permute-start.20 = (bf16[256,768]{1,0:T(8,128)(2,1)S(1)}, bf16[256,768]{1,0:T(8,128)(2,1)S(1)}, u32[]{:S(2)}, u32[]{:S(2)}) collective-permute-start(bf16[256,768]{1,0:T(8,128)(2,1)S(1)} %copy-done), channel_id=1, source_target_pairs={{0,32},{16,48},{32,0},{48,16},{64,96},{80,112},{96,64},{112,80},{1... | collective-permute-start | bytes 1179656 | tf_op jit(solution)/shard_map/ppermute | solution.py:30
  70.6 10.6 %collective-permute-start.17 = (bf16[128,768]{1,0:T(8,128)(2,1)S(1)}, bf16[128,768]{1,0:T(8,128)(2,1)S(1)}, u32[]{:S(2)}, u32[]{:S(2)}) collective-permute-start(bf16[128,768]{1,0:T(8,128)(2,1)S(1)} %get-tuple-element.46), channel_id=1, source_target_pairs={{0,96},{16,112},{32,64},{48,80},{64,32},{80,48},{96,0},{112,16},{1... | collective-permute-start | bytes 589832 | tf_op jit(solution)/shard_map/ppermute | solution.py:30
  73.1 11.7 %collective-permute-start.23 = (bf16[256,768]{1,0:T(8,128)(2,1)S(1)}, bf16[256,768]{1,0:T(8,128)(2,1)S(1)}, u32[]{:S(2)}, u32[]{:S(2)}) collective-permute-start(bf16[256,768]{1,0:T(8,128)(2,1)S(1)} %collective-permute-done.22.rest_4_), channel_id=1, source_target_pairs={{0,16},{16,0},{32,48},{48,32},{64,80},{80,64},{96,112},{112,96},{1... | collective-permute-start | bytes 1179656 | tf_op jit(solution)/shard_map/ppermute | solution.py:30
  75.7 13.9 %collective-permute-start.25 = (bf16[256,768]{1,0:T(8,128)(2,1)S(1)}, bf16[256,768]{1,0:T(8,128)(2,1)S(1)}, u32[]{:S(2)}, u32[]{:S(2)}) collective-permute-start(bf16[256,768]{1,0:T(8,128)(2,1)S(1)} %collective-permute-done.19.rest_1_), channel_id=1, source_target_pairs={{0,96},{16,112},{32,64},{48,80},{64,32},{80,48},{96,0},{112,16},{1... | collective-permute-start | bytes 1179656 | tf_op jit(solution)/shard_map/ppermute | solution.py:30
  81.2 8.4 %collective-permute-start.21 = (bf16[256,768]{1,0:T(8,128)(2,1)S(1)}, bf16[256,768]{1,0:T(8,128)(2,1)S(1)}, u32[]{:S(2)}, u32[]{:S(2)}) collective-permute-start(bf16[256,768]{1,0:T(8,128)(2,1)S(1)} %collective-permute-done.19.rest_1_), channel_id=1, source_target_pairs={{0,32},{16,48},{32,0},{48,16},{64,96},{80,112},{96,64},{112,80},{1... | collective-permute-start | bytes 1179656 | tf_op jit(solution)/shard_map/ppermute | solution.py:30
  81.3 10.5 %collective-permute-start.12 = (bf16[128,768]{1,0:T(8,128)(2,1)S(1)}, bf16[128,768]{1,0:T(8,128)(2,1)S(1)}, u32[]{:S(2)}, u32[]{:S(2)}) collective-permute-start(bf16[128,768]{1,0:T(8,128)(2,1)S(1)} %get-tuple-element.40), channel_id=1, source_target_pairs={{0,32},{16,48},{32,0},{48,16},{64,96},{80,112},{96,64},{112,80},{1... | collective-permute-start | bytes 589832 | tf_op jit(solution)/shard_map/ppermute | solution.py:30
  82.8 11.0 %collective-permute-start.14 = (bf16[128,768]{1,0:T(8,128)(2,1)S(1)}, bf16[128,768]{1,0:T(8,128)(2,1)S(1)}, u32[]{:S(2)}, u32[]{:S(2)}) collective-permute-start(bf16[128,768]{1,0:T(8,128)(2,1)S(1)} %shard_map.111), channel_id=1, source_target_pairs={{0,96},{16,112},{32,64},{48,80},{64,32},{80,48},{96,0},{112,16},{1... | collective-permute-start | bytes 589832 | tf_op jit(solution)/shard_map/ppermute | solution.py:30
  84.7 13.3 %collective-permute-start.16 = (bf16[128,768]{1,0:T(8,128)(2,1)S(1)}, bf16[128,768]{1,0:T(8,128)(2,1)S(1)}, u32[]{:S(2)}, u32[]{:S(2)}) collective-permute-start(bf16[128,768]{1,0:T(8,128)(2,1)S(1)} %get-tuple-element.44), channel_id=1, source_target_pairs={{0,96},{16,112},{32,64},{48,80},{64,32},{80,48},{96,0},{112,16},{1... | collective-permute-start | bytes 589832 | tf_op jit(solution)/shard_map/ppermute | solution.py:30
  89.6 8.4 %collective-permute-start.18 = (bf16[128,768]{1,0:T(8,128)(2,1)S(1)}, bf16[128,768]{1,0:T(8,128)(2,1)S(1)}, u32[]{:S(2)}, u32[]{:S(2)}) collective-permute-start(bf16[128,768]{1,0:T(8,128)(2,1)S(1)} %shard_map.113), channel_id=1, source_target_pairs={{0,32},{16,48},{32,0},{48,16},{64,96},{80,112},{96,64},{112,80},{1... | collective-permute-start | bytes 589832 | tf_op jit(solution)/shard_map/ppermute | solution.py:30
  108.9 8.0 %collective-permute-start.27 = (bf16[16,6144]{1,0:T(8,128)(2,1)S(1)}, bf16[16,6144]{1,0:T(8,128)(2,1)S(1)}, u32[]{:S(2)}, u32[]{:S(2)}) collective-permute-start(bf16[16,6144]{1,0:T(8,128)(2,1)S(1)} %get-tuple-element.50), channel_id=1, source_target_pairs={{0,2},{1,3},{2,0},{3,1},{4,6},{5,7},{6,4},{7,5},{8,10},{9,11},{10,... | collective-permute-start | bytes 589832 | tf_op jit(solution)/shard_map/ppermute | solution.py:30
  109.8 8.2 %collective-permute-start.28 = (bf16[16,6144]{1,0:T(8,128)(2,1)S(1)}, bf16[16,6144]{1,0:T(8,128)(2,1)S(1)}, u32[]{:S(2)}, u32[]{:S(2)}) collective-permute-start(bf16[16,6144]{1,0:T(8,128)(2,1)S(1)} %get-tuple-element.51), channel_id=1, source_target_pairs={{0,6},{1,7},{2,4},{3,5},{4,2},{5,3},{6,0},{7,1},{8,14},{9,15},{10,... | collective-permute-start | bytes 589832 | tf_op jit(solution)/shard_map/ppermute | solution.py:30
  122.4 8.8 %collective-permute-start.36 = (bf16[16,6144]{1,0:T(8,128)(2,1)S(1)}, bf16[16,6144]{1,0:T(8,128)(2,1)S(1)}, u32[]{:S(2)}, u32[]{:S(2)}) collective-permute-start(bf16[16,6144]{1,0:T(8,128)(2,1)S(1)} %shard_map.120), channel_id=1, source_target_pairs={{0,6},{1,7},{2,4},{3,5},{4,2},{5,3},{6,0},{7,1},{8,14},{9,15},{10,... | collective-permute-start | bytes 589832 | tf_op jit(solution)/shard_map/ppermute | solution.py:30
  126.9 9.5 %collective-permute-start.40 = (bf16[16,6144]{1,0:T(8,128)(2,1)S(1)}, bf16[16,6144]{1,0:T(8,128)(2,1)S(1)}, u32[]{:S(2)}, u32[]{:S(2)}) collective-permute-start(bf16[16,6144]{1,0:T(8,128)(2,1)S(1)} %collective-permute-done.37), channel_id=1, source_target_pairs={{0,6},{1,7},{2,4},{3,5},{4,2},{5,3},{6,0},{7,1},{8,14},{9,15},{10,... | collective-permute-start | bytes 589832 | tf_op jit(solution)/shard_map/ppermute | solution.py:30
  136.4 16.3 %collective-permute-start.41 = (bf16[8,16,6144]{2,1,0:T(8,128)(2,1)S(1)}, bf16[8,16,6144]{2,1,0:T(8,128)(2,1)S(1)}, u32[]{:S(2)}, u32[]{:S(2)}) collective-permute-start(bf16[8,16,6144]{2,1,0:T(8,128)(2,1)S(1)} %bitcast_dynamic-update-slice_fusion.src), channel_id=1, source_target_pairs={{0,1},{1,0},{2,3},{3,2},{4,5},{5,4},{6,7},{7,6},{8,9},{9,8},{10,11... | collective-permute-start | bytes 4718600 | tf_op jit(solution)/shard_map/ppermute | solution.py:30
  155.7 9.3 %collective-permute-start.42 = (bf16[8,16,3072]{2,1,0:T(8,128)(2,1)S(1)}, bf16[8,16,3072]{2,1,0:T(8,128)(2,1)S(1)}, u32[]{:S(2)}, u32[]{:S(2)}) collective-permute-start(bf16[8,16,3072]{2,1,0:T(8,128)(2,1)S(1)} %shard_map.124), channel_id=1, source_target_pairs={{0,1},{1,0},{2,3},{3,2},{4,5},{5,4},{6,7},{7,6},{8,9},{9,8},{10,11... | collective-permute-start | bytes 2359304 | tf_op jit(solution)/shard_map/ppermute | solution.py:30
  159.5 10.0 %collective-permute-start.48 = (bf16[16,3072]{1,0:T(8,128)(2,1)S(1)}, bf16[16,3072]{1,0:T(8,128)(2,1)S(1)}, u32[]{:S(2)}, u32[]{:S(2)}) collective-permute-start(bf16[16,3072]{1,0:T(8,128)(2,1)S(1)} %get-tuple-element.65), channel_id=1, source_target_pairs={{0,12},{1,13},{2,14},{3,15},{4,8},{5,9},{6,10},{7,11},{8,4},{9,5},... | collective-permute-start | bytes 294920 | tf_op jit(solution)/shard_map/ppermute | solution.py:30
  166.2 15.0 %collective-permute-start.43 = (bf16[2,16,3072]{2,1,0:T(8,128)(2,1)S(1)}, bf16[2,16,3072]{2,1,0:T(8,128)(2,1)S(1)}, u32[]{:S(2)}, u32[]{:S(2)}) collective-permute-start(bf16[2,16,3072]{2,1,0:T(8,128)(2,1)S(1)} %pad_maximum_fusion.1), channel_id=1, source_target_pairs={{0,2},{1,3},{2,0},{3,1},{4,6},{5,7},{6,4},{7,5},{8,10},{9,11},{10,... | collective-permute-start | bytes 589832 | tf_op jit(solution)/shard_map/ppermute | solution.py:30
  169.5 11.7 %collective-permute-start.44 = (bf16[2,16,3072]{2,1,0:T(8,128)(2,1)S(1)}, bf16[2,16,3072]{2,1,0:T(8,128)(2,1)S(1)}, u32[]{:S(2)}, u32[]{:S(2)}) collective-permute-start(bf16[2,16,3072]{2,1,0:T(8,128)(2,1)S(1)} %pad_maximum_fusion.2), channel_id=1, source_target_pairs={{0,4},{1,5},{2,6},{3,7},{4,0},{5,1},{6,2},{7,3},{8,12},{9,13},{10,... | collective-permute-start | bytes 589832 | tf_op jit(solution)/shard_map/ppermute | solution.py:30
  170.0 11.2 %collective-permute-start.45 = (bf16[2,16,3072]{2,1,0:T(8,128)(2,1)S(1)}, bf16[2,16,3072]{2,1,0:T(8,128)(2,1)S(1)}, u32[]{:S(2)}, u32[]{:S(2)}) collective-permute-start(bf16[2,16,3072]{2,1,0:T(8,128)(2,1)S(1)} %pad_maximum_fusion.3), channel_id=1, source_target_pairs={{0,6},{1,7},{2,4},{3,5},{4,2},{5,3},{6,0},{7,1},{8,14},{9,15},{10,... | collective-permute-start | bytes 589832 | tf_op jit(solution)/shard_map/ppermute | solution.py:30
  171.9 9.2 %collective-permute-start.51 = (bf16[16,3072]{1,0:T(8,128)(2,1)S(1)}, bf16[16,3072]{1,0:T(8,128)(2,1)S(1)}, u32[]{:S(2)}, u32[]{:S(2)}) collective-permute-start(bf16[16,3072]{1,0:T(8,128)(2,1)S(1)} %get-tuple-element.69), channel_id=1, source_target_pairs={{0,10},{1,11},{2,8},{3,9},{4,14},{5,15},{6,12},{7,13},{8,2},{9,3},... | collective-permute-start | bytes 294920 | tf_op jit(solution)/shard_map/ppermute | solution.py:30
  172.2 9.0 %collective-permute-start.50 = (bf16[16,3072]{1,0:T(8,128)(2,1)S(1)}, bf16[16,3072]{1,0:T(8,128)(2,1)S(1)}, u32[]{:S(2)}, u32[]{:S(2)}) collective-permute-start(bf16[16,3072]{1,0:T(8,128)(2,1)S(1)} %get-tuple-element.70), channel_id=1, source_target_pairs={{0,8},{1,9},{2,10},{3,11},{4,12},{5,13},{6,14},{7,15},{8,0},{9,1},... | collective-permute-start | bytes 294920 | tf_op jit(solution)/shard_map/ppermute | solution.py:30
  (27 other events, 197.0 us)
